TPU v7x, 512 devices: a whole 4x4x16 slice. The times are simulated.
512 devices in a mesh: pair: 128 (over x, z, y_lo), col: 4 (over y_hi, core).
Axes of the slice: x: 4, y: 4 (y_hi: 2, y_lo: 2; y = y_hi * 2 + y_lo), z: 16, core: 2. Of those that a mesh axis runs over, the one named last changes fastest.
Arguments:
- amplitudes: bfloat16 [640, 512, 512], P('pair', None, 'col'), may hold values from -6 to 6
- fock_left: bfloat16 [512, 512], replicated, may hold values from -0.25 to 0.25
- dress_left: bfloat16 [512, 512], replicated, may hold values from -0.25 to 0.25
- fock_right: bfloat16 [512, 512], P(None, 'col'), may hold values from -0.25 to 0.25
- dress_right: bfloat16 [512, 512], P(None, 'col'), may hold values from -0.25 to 0.25
- hole_ladder: bfloat16 [576, 576], replicated, may hold values from -0.25 to 0.25
- slot_pair: int32 [640], replicated, may hold values from 0 to 639, as said below
- partner: int32 [640], replicated, may hold values from 0 to 639, as said below
- occ_energy: float32 [24], replicated, may hold values from -2 to -0.5
- virt_energy: float32 [512], replicated, may hold values from 0.3 to 3
- virt_order: int32 [512], replicated, may hold values from 0 to 511, each once
Outputs:
- update: float32 [640, 512, 512], P('pair', None, 'col')
Inputs may be any that keep to these rules, and one draw needn't show every extreme that they name: slot_pair is a permutation of 0 to 639; values of 576 or more mark empty slots. partner[s] is the slot whose pair is (j, i) when slot s holds pair (i, j) = i * 24 + j; an empty slot is its own partner.
All inputs are finite; a program needn't handle non-finite values.
Results may differ from a plain program's by a relative error of at most 0.0033.
Values may be sent and summed in bfloat16 or wider, within the bound.
No kernel may reach another device: no remote copies, remote signals or barrier semaphores. Data moves between devices by JAX's collectives and lax.ppermute only.
A program may use at most 64 MiB of HBM per device.

v0:
```python
import jax
import jax.numpy as jnp
from jax import lax
from jax.sharding import PartitionSpec as P


def right_times(block, matrix):
    count, height, width = block.shape
    result = jnp.dot(
        block.reshape(count * height, width), matrix, preferred_element_type=jnp.float32
    )
    return result.reshape(count, height, matrix.shape[1])


def left_times(matrix, block):
    count, height, width = block.shape
    columns = jnp.transpose(block, (1, 0, 2)).reshape(height, count * width)
    result = jnp.dot(matrix, columns, preferred_element_type=jnp.float32)
    return jnp.transpose(result.reshape(matrix.shape[0], count, width), (1, 0, 2))


def pair_times(weights, block):
    count, height, width = block.shape
    result = jnp.dot(
        weights, block.reshape(count, height * width), preferred_element_type=jnp.float32
    )
    return result.reshape(weights.shape[0], height, width)


def body(
    amplitudes,
    fock_left,
    dress_left,
    fock_right,
    dress_right,
    hole_ladder,
    slot_pair,
    partner,
    occ_energy,
    virt_energy,
    virt_order,
):
    slot_dev, nvirt, ncols = amplitudes.shape
    slots = slot_pair.shape[0]
    npairs = hole_ladder.shape[0]
    nocc = occ_energy.shape[0]
    col_index = lax.axis_index("col")
    pair_index = lax.axis_index("pair")
    piece = lax.all_gather(amplitudes, "col", axis=2, tiled=True)
    right_fock = right_times(piece, fock_right)
    right_dress = right_times(piece, dress_right)
    own_rows = lax.dynamic_slice_in_dim(piece, col_index * ncols, ncols, 1)
    flipped = jnp.transpose(own_rows, (0, 2, 1))
    dressed = right_dress.astype(jnp.bfloat16)
    particle = left_times(fock_left, amplitudes)
    particle = particle + left_times(dress_left, dressed)
    particle_b = (particle + right_fock).astype(jnp.bfloat16)
    padded = jnp.pad(hole_ladder, ((0, slots - npairs), (0, slots - npairs)))
    ladder_w = padded[slot_pair][:, slot_pair]
    mirrored_w = ladder_w[partner]
    y_part = lax.all_to_all(particle_b, "col", split_axis=1, concat_axis=2, tiled=True)
    y_flip = jnp.transpose(y_part, (0, 2, 1))
    ladder_terms = pair_times(
        ladder_w, lax.all_to_all(amplitudes, "pair", split_axis=1, concat_axis=0, tiled=True)
    )
    mirror_terms = pair_times(
        mirrored_w, lax.all_to_all(flipped, "pair", split_axis=1, concat_axis=0, tiled=True)
    )
    result = ladder_terms.astype(jnp.bfloat16).astype(jnp.float32)
    result = result + mirror_terms.astype(jnp.bfloat16).astype(jnp.float32)
    summed = result + lax.all_to_all(y_flip, "pair", split_axis=1, concat_axis=0, tiled=True)[
        partner
    ].astype(jnp.float32)
    returned = lax.all_to_all(summed, "pair", split_axis=0, concat_axis=1, tiled=True)
    total = particle_b.astype(jnp.float32) + returned
    own_pairs = lax.dynamic_slice_in_dim(slot_pair, pair_index * slot_dev, slot_dev)
    occ_iota = jnp.arange(nocc, dtype=jnp.int32)
    first_hot = (own_pairs[:, None] // nocc == occ_iota[None, :]).astype(jnp.float32)
    second_hot = (own_pairs[:, None] % nocc == occ_iota[None, :]).astype(jnp.float32)
    live = (own_pairs < npairs).astype(jnp.float32)
    occ_sum = live * (
        jnp.sum(first_hot * occ_energy[None, :], axis=1)
        + jnp.sum(second_hot * occ_energy[None, :], axis=1)
    )
    virt_iota = jnp.arange(nvirt, dtype=jnp.int32)
    row_hot = (virt_order[:, None] == virt_iota[None, :]).astype(jnp.float32)
    row_energy = jnp.sum(row_hot * virt_energy[None, :], axis=1)
    col_energy = lax.dynamic_slice_in_dim(row_energy, col_index * ncols, ncols)
    denom = row_energy[None, :, None] + col_energy[None, None, :] - occ_sum[:, None, None]
    return total / denom


def solution(mesh):
    placed = (
        P("pair", None, "col"),
        P(),
        P(),
        P(None, "col"),
        P(None, "col"),
        P(),
        P(),
        P(),
        P(),
        P(),
        P(),
    )
    return jax.shard_map(
        body, mesh=mesh, in_specs=placed, out_specs=P("pair", None, "col"), check_vma=False
    )
```

profile of v0, /device:TPU:2, one launch (start us, length us, event | category | flops | bytes accessed | tf_op | source)
XLA Modules:
  0.0 323.7 jit_solution(2363075832311798946)
XLA Ops:
  7.3 2.6 copy.80
  9.8 21.1 %all-to-all-start = ((bf16[5,512,128]{2,0,1:T(8,128)(2,1)}), bf16[5,512,128]{2,0,1:T(8,128)(2,1)}, u32[]{:S(2)}, u32[]{:S(2)}) async-start(bf16[5,512,128]{2,0,1:T(8,128)(2,1)} %copy.80), calls=%async_computation | async-start | bytes 2097152 | tf_op jit(solution)/shard_map/all_to_all | solution.py:64
  32.1 24.2 %all-gather.2.cloned.1.call-done = bf16[5,512,512]{2,1,0:T(8,128)(2,1)} async-done(((bf16[5,512,128]{2,1,0:T(8,128)(2,1)}), bf16[5,512,512]{2,1,0:T(8,128)(2,1)}) %all-gather.2.cloned.1.call-update) | async-done | bytes 2621456 | tf_op jit(solution)/shard_map/all_gather | solution.py:49
  56.3 2.7 convolution_convert_fusion.2
  59.5 1.5 copy.78
  61.0 2.4 fusion
  66.7 19.5 %all-to-all-done = bf16[5,512,128]{2,0,1:T(8,128)(2,1)} async-done(((bf16[5,512,128]{2,0,1:T(8,128)(2,1)}), bf16[5,512,128]{2,0,1:T(8,128)(2,1)}, u32[]{:S(2)}, u32[]{:S(2)}) %all-to-all-start) | async-done | bytes 655392 | tf_op jit(solution)/shard_map/all_to_all | solution.py:64
  86.2 4.2 %all-to-all-start.2 = ((bf16[5,512,128]{2,0,1:T(8,128)(2,1)}), bf16[5,512,128]{2,0,1:T(8,128)(2,1)}, u32[]{:S(2)}, u32[]{:S(2)}) async-start(bf16[5,512,128]{2,0,1:T(8,128)(2,1)} %copy.89), calls=%async_computation.2 | async-start | bytes 2097152 | tf_op jit(solution)/shard_map/all_to_all | solution.py:61
  91.3 2.4 copy.85
  93.7 12.8 %all-to-all-done.2 = bf16[5,512,128]{2,0,1:T(8,128)(2,1)} async-done(((bf16[5,512,128]{2,0,1:T(8,128)(2,1)}), bf16[5,512,128]{2,0,1:T(8,128)(2,1)}, u32[]{:S(2)}, u32[]{:S(2)}) %all-to-all-start.2) | async-done | bytes 655392 | tf_op jit(solution)/shard_map/all_to_all | solution.py:61
  106.5 7.2 %all-to-all-start.1 = ((bf16[5,512,128]{2,0,1:T(8,128)(2,1)}), bf16[5,512,128]{2,0,1:T(8,128)(2,1)S(1)}, u32[]{:S(2)}, u32[]{:S(2)}) async-start(bf16[5,512,128]{2,0,1:T(8,128)(2,1)} %copy.85), calls=%async_computation.1 | async-start | bytes 2097152 | tf_op jit(solution)/shard_map/all_to_all | solution.py:67
  113.7 2.7 copy.103
  116.4 52.6 %all-to-all-done.1 = bf16[5,512,128]{2,0,1:T(8,128)(2,1)S(1)} async-done(((bf16[5,512,128]{2,0,1:T(8,128)(2,1)}), bf16[5,512,128]{2,0,1:T(8,128)(2,1)S(1)}, u32[]{:S(2)}, u32[]{:S(2)}) %all-to-all-start.1) | async-done | bytes 655392 | tf_op jit(solution)/shard_map/all_to_all | solution.py:67
  170.0 7.7 %all-to-all-start.3 = ((bf16[5,512,128]{2,0,1:T(8,128)(2,1)}), bf16[5,512,128]{2,0,1:T(8,128)(2,1)}, u32[]{:S(2)}, u32[]{:S(2)}) async-start(bf16[5,512,128]{2,0,1:T(8,128)(2,1)} %bitcast.29), calls=%async_computation.3 | async-start | bytes 2097152 | tf_op jit(solution)/shard_map/all_to_all | solution.py:71
  177.9 3.0 gather_fusion
  181.8 3.0 gather_fusion.1
  185.8 3.4 %gather_fusion.2 = bf16[640,640]{1,0:T(8,128)(2,1)} fusion(bf16[640,640]{1,0:T(8,128)(2,1)S(1)} %copy.84, s32[1024]{0:T(1024)S(1)} %pad_clamp_fusion), kind=kCustom, calls=%fused_computation.2 | custom fusion | bytes 1640960 | tf_op jit(solution)/shard_map/gather | solution.py:60
  189.1 1.5 copy.81
  193.0 39.5 %all-to-all-done.3 = bf16[5,512,128]{2,0,1:T(8,128)(2,1)} async-done(((bf16[5,512,128]{2,0,1:T(8,128)(2,1)}), bf16[5,512,128]{2,0,1:T(8,128)(2,1)}, u32[]{:S(2)}, u32[]{:S(2)}) %all-to-all-start.3) | async-done | bytes 655392 | tf_op jit(solution)/shard_map/all_to_all | solution.py:71
  234.8 2.8 gather_fusion.3
  237.6 1.9 fusion.4
  239.5 1.9 copy.96
  241.4 7.4 %all-to-all-start.4 = ((f32[640,4,128]{2,1,0:T(4,128)}), f32[640,4,128]{2,1,0:T(4,128)S(1)}, u32[]{:S(2)}, u32[]{:S(2)}) async-start(f32[640,4,128]{2,1,0:T(4,128)} %copy.96), calls=%async_computation.4 | async-start | bytes 2621440 | tf_op jit(solution)/shard_map/all_to_all | solution.py:74
  249.7 64.8 %all-to-all-done.4 = f32[640,4,128]{2,1,0:T(4,128)S(1)} async-done(((f32[640,4,128]{2,1,0:T(4,128)}), f32[640,4,128]{2,1,0:T(4,128)S(1)}, u32[]{:S(2)}, u32[]{:S(2)}) %all-to-all-start.4) | async-done | bytes 1310752 | tf_op jit(solution)/shard_map/all_to_all | solution.py:74
  (61 shorter events, 17.4 us)
Async XLA Ops:
  6.5 52.5 %copy-start = (bf16[512,512]{1,0:T(8,128)(2,1)S(1)}, bf16[512,512]{1,0:T(8,128)(2,1)}, u32[]{:S(2)}) copy-start(bf16[512,512]{1,0:T(8,128)(2,1)} %param.13) | copy-start | bytes 1572868
  6.5 49.7 %all-gather.2.cloned.1.call-start = ((), (), s32[]{:S(2)}) async-start(), calls=%async_computation.5 | async-start | bytes 3276800 | tf_op jit(solution)/shard_map/all_gather | solution.py:49
  9.8 21.1 %copy-start.2 = (bf16[5,512,128]{2,1,0:T(8,128)(2,1)S(1)}, bf16[5,512,128]{2,1,0:T(8,128)(2,1)}, u32[]{:S(2)}) copy-start(bf16[5,512,128]{2,1,0:T(8,128)(2,1)} %param.11) | copy-start | bytes 1966084
  9.8 46.4 %copy-start.9 = (bf16[512,128]{1,0:T(8,128)(2,1)S(1)}, bf16[512,128]{1,0:T(8,128)(2,1)}, u32[]{:S(2)}) copy-start(bf16[512,128]{1,0:T(8,128)(2,1)} %param.15) | copy-start | bytes 393220
  9.8 76.4 %all-to-all-start = ((bf16[5,512,128]{2,0,1:T(8,128)(2,1)}), bf16[5,512,128]{2,0,1:T(8,128)(2,1)}, u32[]{:S(2)}, u32[]{:S(2)}) async-start(bf16[5,512,128]{2,0,1:T(8,128)(2,1)} %copy.80), calls=%async_computation | async-start | bytes 2097152 | tf_op jit(solution)/shard_map/all_to_all | solution.py:64
  61.0 2.5 copy-start.1
  61.0 2.5 copy-start.8
  64.4 0.8 copy-start.3
  86.2 20.2 %all-to-all-start.2 = ((bf16[5,512,128]{2,0,1:T(8,128)(2,1)}), bf16[5,512,128]{2,0,1:T(8,128)(2,1)}, u32[]{:S(2)}, u32[]{:S(2)}) async-start(bf16[5,512,128]{2,0,1:T(8,128)(2,1)} %copy.89), calls=%async_computation.2 | async-start | bytes 2097152 | tf_op jit(solution)/shard_map/all_to_all | solution.py:61
  106.5 62.6 %all-to-all-start.1 = ((bf16[5,512,128]{2,0,1:T(8,128)(2,1)}), bf16[5,512,128]{2,0,1:T(8,128)(2,1)S(1)}, u32[]{:S(2)}, u32[]{:S(2)}) async-start(bf16[5,512,128]{2,0,1:T(8,128)(2,1)} %copy.85), calls=%async_computation.1 | async-start | bytes 2097152 | tf_op jit(solution)/shard_map/all_to_all | solution.py:67
  116.4 61.3 %copy-start.7 = (bf16[576,576]{1,0:T(8,128)(2,1)S(1)}, bf16[576,576]{1,0:T(8,128)(2,1)}, u32[]{:S(2)}) copy-start(bf16[576,576]{1,0:T(8,128)(2,1)} %param.16) | copy-start | bytes 1990660
  169.0 1.0 copy-start.5
  169.0 8.8 %copy-start.10 = (s32[640]{0:T(1024)S(1)}, s32[640]{0:T(1024)}, u32[]{:S(2)}) copy-start(s32[640]{0:T(1024)} %param.17) | copy-start | bytes 7684
  170.0 62.4 %all-to-all-start.3 = ((bf16[5,512,128]{2,0,1:T(8,128)(2,1)}), bf16[5,512,128]{2,0,1:T(8,128)(2,1)}, u32[]{:S(2)}, u32[]{:S(2)}) async-start(bf16[5,512,128]{2,0,1:T(8,128)(2,1)} %bitcast.29), calls=%async_computation.3 | async-start | bytes 2097152 | tf_op jit(solution)/shard_map/all_to_all | solution.py:71
  184.8 1.0 copy-start.11
  191.0 1.2 copy-start.6
  241.4 7.4 %copy-start.12 = (f32[512]{0:T(512)S(1)}, f32[512]{0:T(512)}, u32[]{:S(2)}) copy-start(f32[512]{0:T(512)} %param.20) | copy-start | bytes 6148
  241.4 7.4 %copy-start.13 = (s32[512]{0:T(512)S(1)}, s32[512]{0:T(512)}, u32[]{:S(2)}) copy-start(s32[512]{0:T(512)} %param.21) | copy-start | bytes 6148
  241.4 7.8 %copy-start.14 = (f32[24]{0:T(128)S(1)}, f32[24]{0:T(128)}, u32[]{:S(2)}) copy-start(f32[24]{0:T(128)} %param.19) | copy-start | bytes 292
  241.4 73.0 %all-to-all-start.4 = ((f32[640,4,128]{2,1,0:T(4,128)}), f32[640,4,128]{2,1,0:T(4,128)S(1)}, u32[]{:S(2)}, u32[]{:S(2)}) async-start(f32[640,4,128]{2,1,0:T(4,128)} %copy.96), calls=%async_computation.4 | async-start | bytes 2621440 | tf_op jit(solution)/shard_map/all_to_all | solution.py:74
  314.5 1.1 copy-start.4
Sparse Core Ops, SparseCore 0:
  9.4 46.7 all-gather.1
where the time goes:
time: 325 us; the launch traced here: 324 us
  waiting for transfers between devices  214 us (66%)
  starting transfers between devices  47.7 us (15%)
  local copies, waits for them, and re-layouts  37 us (11%)
  between operations  13.7 us (4%)
  matrix products  9.17 us (3%)
    all_to_all x1, waiting for transfers between devices, body(): lax.all_to_all(summed, 'pair', split_axis=0, concat_axis=1, tiled=True)  64.8 us
    all_to_all x1, waiting for transfers between devices, body(): lax.all_to_all(flipped, 'pair', split_axis=1, concat_axis=0, tiled=True)  52.6 us
    all_to_all x1, waiting for transfers between devices, body(): lax.all_to_all(y_flip, 'pair', split_axis=1, concat_axis=0, tiled=True)  39.5 us
    all_gather x1, waiting for transfers between devices, body(): piece = lax.all_gather(amplitudes, 'col', axis=2, tiled=True)  24.2 us
    all_to_all x1, starting transfers between devices, body(): lax.all_to_all(amplitudes, 'pair', split_axis=1, concat_axis=0, tiled=True)  21.1 us
    all_to_all x1, waiting for transfers between devices, body(): lax.all_to_all(amplitudes, 'pair', split_axis=1, concat_axis=0, tiled=True)  19.5 us
    all_to_all x1, waiting for transfers between devices, body(): lax.all_to_all(particle_b, 'col', split_axis=1, concat_axis=2, tiled=True)  12.8 us
    gather x4, local copies, waits for them, and re-layouts, body(): ladder_w = padded[slot_pair][:, slot_pair]  7.83 us
  transfers between devices with their start and end apart: 6, of which 6 were waited for; matrix products, arithmetic and copies ran while one was open for 11% of the time, Pallas kernels for 0%

commit v1 on v0

v1 whole, which is shorter than its diff:
```python
import functools

import jax
import jax.numpy as jnp
from jax import lax
from jax.experimental import pallas as pl
from jax.experimental.pallas import tpu as pltpu
from jax.sharding import PartitionSpec as P

F32 = jnp.float32
BF16 = jnp.bfloat16


def dot(left, right):
    return jnp.dot(left, right, preferred_element_type=F32)


def chunks_of(total):
    return [(start, min(8, total - start)) for start in range(0, total, 8)]


def swap_rows(values, bits, first_bit, lanes):
    for step in range(bits):
        take = ((lax.broadcasted_iota(jnp.int32, values[0].shape, 1) >> (first_bit + step)) & 1) == 1
        bit = 1 << step
        values = [jnp.where(take, values[i ^ bit], values[i]) for i in range(len(values))]
    return values


def split_bits(nb):
    total = nb.bit_length() - 1
    low = (total + 1) // 2
    return low, total - low


def skew(source, middle, target, nb, count):
    low, high = split_bits(nb)
    for start, size in chunks_of(count):
        for base in range(1 << high):
            rows = [(base << low) + i for i in range(1 << low)]
            values = [source[pl.ds(start * nb + r, size, stride=nb), :] for r in rows]
            for r, value in zip(rows, swap_rows(values, low, 0, nb)):
                middle[r, start : start + size, :] = value
        for base in range(1 << low):
            rows = [base + (i << low) for i in range(1 << high)]
            values = [middle[r, start : start + size, :] for r in rows]
            for r, value in zip(rows, swap_rows(values, high, low, nb)):
                target[r * count + start : r * count + start + size, :] = value


def unskew(source, middle, target, nb, count):
    low, high = split_bits(nb)
    for start, size in chunks_of(count):
        for base in range(1 << low):
            rows = [base + (i << low) for i in range(1 << high)]
            values = [source[r * count + start : r * count + start + size, :] for r in rows]
            for r, value in zip(rows, swap_rows(values, high, low, nb)):
                middle[r, start : start + size, :] = value
        for base in range(1 << high):
            rows = [(base << low) + i for i in range(1 << low)]
            values = [middle[r, start : start + size, :] for r in rows]
            for r, value in zip(rows, swap_rows(values, low, 0, nb)):
                target[pl.ds(start * nb + r, size, stride=nb), :] = value


def skew_kernel(a_ref, out_ref, flat, middle, target):
    count = a_ref.shape[0] * (a_ref.shape[1] // a_ref.shape[2])
    nb = a_ref.shape[2]
    flat[...] = a_ref[...].reshape(count * nb, nb).astype(F32)
    skew(flat, middle, target, nb, count)
    out_ref[...] = target[...].astype(BF16)


def skew_scratch(count, nb):
    return [
        pltpu.VMEM((count * nb, nb), F32),
        pltpu.VMEM((nb, -(-count // 8) * 8, nb), F32),
        pltpu.VMEM((count * nb, nb), F32),
    ]


def weights_kernel(pair_col, pair_row, partner_col, h_ref, w_ref, w2_ref):
    slots = w_ref.shape[0]
    npairs = h_ref.shape[0]
    pick = (pair_col[...] == lax.broadcasted_iota(jnp.int32, (slots, npairs), 1)).astype(BF16)
    pick_t = (pair_row[...] == lax.broadcasted_iota(jnp.int32, (npairs, slots), 0)).astype(BF16)
    half = dot(pick, h_ref[...]).astype(BF16)
    w = dot(half, pick_t).astype(BF16)
    w_ref[...] = w
    mirror = (partner_col[...] == lax.broadcasted_iota(jnp.int32, (slots, slots), 1)).astype(BF16)
    w2_ref[...] = dot(mirror, w).astype(BF16)


def particle_kernel(
    c_ref, g0, g1, g2, g3, fl_ref, dl_ref, p_ref, out_ref, acat, dmat, fmat, flat, middle, target
):
    parts = (g0, g1, g2, g3)
    ncol = len(parts)
    nslot, nvirt, nb = p_ref.shape
    col = c_ref[0]
    for i in range(ncol):
        rows = pl.ds(pl.multiple_of((col ^ i) * nb, nb), nb)
        for k in range(ncol):
            fmat[i * nb : (i + 1) * nb, k * nb : (k + 1) * nb] = parts[k][nslot, rows, :]
            dmat[i * nb : (i + 1) * nb, k * nb : (k + 1) * nb] = parts[k][nslot + 1, rows, :]
    own = pl.ds(pl.multiple_of(col * nb, nb), nb)
    fl_own = fl_ref[own, :]
    dl_own = dl_ref[own, :]
    for s in range(nslot):
        for k in range(ncol):
            acat[:, k * nb : (k + 1) * nb] = parts[k][s]
        amp = acat[...]
        dressed = dot(amp, dmat[...]).astype(BF16)
        own_cols = dot(amp, fmat[:, :nb])
        own_cols = own_cols + dot(fl_ref[...], amp[:, :nb]) + dot(dl_ref[...], dressed[:, :nb])
        p_ref[s] = own_cols.astype(BF16)
        own_rows = dot(acat[own, :], fmat[...]) + dot(fl_own, amp) + dot(dl_own, dressed)
        own_rows = own_rows.astype(BF16).astype(F32)
        for k in range(ncol):
            at = pl.multiple_of((s * ncol + (col ^ k)) * nb, nb)
            flat[pl.ds(at, nb), :] = own_rows[:, k * nb : (k + 1) * nb].T
    skew(flat, middle, target, nb, nslot * ncol)
    out_ref[...] = target[...].astype(BF16)


def ladder_kernel(c_ref, j_ref, x_ref, w_ref, w2_ref, l_ref, m0, m1, m2, m3, wide, xcat, mirror):
    slots = w_ref.shape[0]
    nb = x_ref.shape[1]
    ncol = x_ref.shape[0] // slots
    wide[...] = x_ref[...].astype(F32)
    for d in range(ncol):
        xcat[:, d * nb : (d + 1) * nb] = wide[pl.ds(d, slots, stride=ncol), :].astype(BF16)
    l_ref[...] = dot(w_ref[...], xcat[...]).astype(BF16)
    other = dot(w2_ref[...], xcat[...]).astype(BF16)
    rows = lax.broadcasted_iota(jnp.int32, (nb, nb), 0)
    cols = lax.broadcasted_iota(jnp.int32, (nb, nb), 1)
    flip = (rows == (cols ^ j_ref[0])).astype(BF16)
    for d in range(ncol):
        mirror[d] = dot(other[:, d * nb : (d + 1) * nb], flip).astype(BF16)
    col = c_ref[0]
    for k, out in enumerate((m0, m1, m2, m3)):
        out[...] = mirror[col ^ k]


def combine_kernel(c_ref, y_ref, l_ref, m0, m1, m2, m3, partner_col, out_ref, wide, ycat, mirror):
    slots = l_ref.shape[0]
    nb = y_ref.shape[1]
    ncol = y_ref.shape[0] // slots
    wide[...] = y_ref[...].astype(F32)
    for d in range(ncol):
        ycat[:, d * nb : (d + 1) * nb] = wide[pl.ds(d, slots, stride=ncol), :].astype(BF16)
    pick = (partner_col[...] == lax.broadcasted_iota(jnp.int32, (slots, slots), 1)).astype(BF16)
    total = dot(pick, ycat[...]) + l_ref[...].astype(F32)
    col = c_ref[0]
    for k, part in enumerate((m0, m1, m2, m3)):
        mirror[col ^ k] = part[...]
    for d in range(ncol):
        wide[pl.ds(d, slots, stride=ncol), :] = total[:, d * nb : (d + 1) * nb] + mirror[d].astype(F32)
    out_ref[...] = wide[...].astype(BF16)


def finish_kernel(occ_ref, z_ref, p_ref, base_ref, out_ref, flat, middle, target):
    nslot, nvirt, nb = p_ref.shape
    flat[...] = z_ref[...].astype(F32)
    unskew(flat, middle, target, nb, nslot * (nvirt // nb))
    for s in range(nslot):
        total = p_ref[s].astype(F32) + target[s * nvirt : (s + 1) * nvirt, :]
        out_ref[s] = total / (base_ref[...] - occ_ref[s])


SMEM = pl.BlockSpec(memory_space=pltpu.SMEM)
VMEM = pl.BlockSpec(memory_space=pltpu.VMEM)


def call(kernel, outs, scratch, specs, name):
    return pl.pallas_call(
        kernel,
        out_shape=outs,
        in_specs=specs,
        out_specs=jax.tree.map(lambda _: VMEM, outs),
        scratch_shapes=scratch,
        name=name,
        compiler_params=pltpu.CompilerParams(vmem_limit_bytes=48 << 20),
    )


def body(
    amplitudes,
    fock_left,
    dress_left,
    fock_right,
    dress_right,
    hole_ladder,
    slot_pair,
    partner,
    occ_energy,
    virt_energy,
    virt_order,
):
    slot_dev, nvirt, nb = amplitudes.shape
    slots = slot_pair.shape[0]
    npairs = hole_ladder.shape[0]
    nocc = occ_energy.shape[0]
    ncol = nvirt // nb
    count = slot_dev * ncol
    col = lax.axis_index("col")
    pair = lax.axis_index("pair")
    col_s = jnp.reshape(col, (1,)).astype(jnp.int32)
    pair_s = jnp.reshape(pair, (1,)).astype(jnp.int32)
    shape = jax.ShapeDtypeStruct

    def exchange(rows):
        sent = rows.reshape(nb * slot_dev, ncol, nb)
        got = lax.all_to_all(sent, "pair", split_axis=0, concat_axis=0, tiled=True)
        return got.reshape(nb * count, nb)

    def swap(value, k):
        return lax.ppermute(value, "col", [(i, i ^ k) for i in range(ncol)])

    own = jnp.concatenate([amplitudes, fock_right[None], dress_right[None]])
    far = swap(own, 2)
    near = swap(own, 1)
    both = swap(far, 1)
    skewed = call(
        skew_kernel, shape((nb * count, nb), BF16), skew_scratch(count, nb), [VMEM], "skew"
    )(amplitudes)
    x = exchange(skewed)
    pair_col = slot_pair.reshape(slots, 1)
    pair_row = slot_pair.reshape(1, slots)
    partner_col = partner.reshape(slots, 1)
    w, w2 = call(
        weights_kernel, [shape((slots, slots), BF16)] * 2, [], [VMEM] * 4, "weights"
    )(pair_col, pair_row, partner_col, hole_ladder)
    particle, particle_rows = call(
        particle_kernel,
        [shape(amplitudes.shape, BF16), shape((nb * count, nb), BF16)],
        [pltpu.VMEM((nvirt, nvirt), BF16)] * 3 + skew_scratch(count, nb),
        [SMEM] + [VMEM] * 6,
        "particle",
    )(col_s, own, near, far, both, fock_left, dress_left)
    y = exchange(particle_rows)
    ladder, m0, m1, m2, m3 = call(
        ladder_kernel,
        [shape((slots, nvirt), BF16)] + [shape((slots, nb), BF16)] * 4,
        [
            pltpu.VMEM((slots * ncol, nb), F32),
            pltpu.VMEM((slots, nvirt), BF16),
            pltpu.VMEM((ncol, slots, nb), BF16),
        ],
        [SMEM] * 2 + [VMEM] * 3,
        "ladder",
    )(col_s, pair_s, x, w, w2)
    m1, m2, m3 = swap(m1, 1), swap(m2, 2), swap(m3, 3)
    back = call(
        combine_kernel,
        shape((nb * count, nb), BF16),
        [
            pltpu.VMEM((slots * ncol, nb), F32),
            pltpu.VMEM((slots, nvirt), BF16),
            pltpu.VMEM((ncol, slots, nb), BF16),
        ],
        [SMEM] + [VMEM] * 7,
        "combine",
    )(col_s, y, ladder, m0, m1, m2, m3, partner_col)
    z = exchange(back)
    own_pairs = lax.dynamic_slice_in_dim(slot_pair, pair * slot_dev, slot_dev)
    occ_iota = jnp.arange(nocc, dtype=jnp.int32)
    first_hot = (own_pairs[:, None] // nocc == occ_iota[None, :]).astype(F32)
    second_hot = (own_pairs[:, None] % nocc == occ_iota[None, :]).astype(F32)
    live = (own_pairs < npairs).astype(F32)
    occ_sum = live * (
        jnp.sum(first_hot * occ_energy[None, :], axis=1)
        + jnp.sum(second_hot * occ_energy[None, :], axis=1)
    )
    virt_iota = jnp.arange(nvirt, dtype=jnp.int32)
    row_hot = (virt_order[:, None] == virt_iota[None, :]).astype(F32)
    row_energy = jnp.sum(row_hot * virt_energy[None, :], axis=1)
    col_energy = lax.dynamic_slice_in_dim(row_energy, col * nb, nb)
    base = row_energy[:, None] + col_energy[None, :]
    return call(
        finish_kernel,
        shape(amplitudes.shape, F32),
        skew_scratch(count, nb),
        [SMEM] + [VMEM] * 3,
        "finish",
    )(occ_sum, z, particle, base)


def solution(mesh):
    placed = (
        P("pair", None, "col"),
        P(),
        P(),
        P(None, "col"),
        P(None, "col"),
        P(),
        P(),
        P(),
        P(),
        P(),
        P(),
    )
    return jax.shard_map(
        body, mesh=mesh, in_specs=placed, out_specs=P("pair", None, "col"), check_vma=False
    )
```

time: 325 us -> 177 us (0.54)
  the two profiles are of different devices: /device:TPU:2 before, /device:TPU:8 now
where the time goes in v1:
time: 177 us; the launch traced here: 176 us
  waiting for transfers between devices  90.1 us (51%)
  starting transfers between devices  62.5 us (35%)
  Pallas kernels  18.7 us (11%)
  local copies, waits for them, and re-layouts  3.56 us (2%)
    all_to_all x3, waiting for transfers between devices, exchange(): got = lax.all_to_all(sent, 'pair', split_axis=0, concat_axis=0, tiled=True)  54.4 us
    all_to_all x3, starting transfers between devices, exchange(): got = lax.all_to_all(sent, 'pair', split_axis=0, concat_axis=0, tiled=True)  45.4 us
    ppermute x6, waiting for transfers between devices, swap(): return lax.ppermute(value, 'col', [(i, i ^ k) for i in range(ncol)])  35.6 us
    ppermute x6, starting transfers between devices, swap(): return lax.ppermute(value, 'col', [(i, i ^ k) for i in range(ncol)])  17.1 us
    pallas_call x1, Pallas kernels, body(): call(particle_kernel, [shape(amplitudes.shape, BF16), shape((nb * count,...  8.09 us
  transfers between devices with their start and end apart: 9, of which 6 were waited for; matrix products, arithmetic and copies ran while one was open for 1% of the time, Pallas kernels for 7%

profile of v1, /device:TPU:8, one launch (start us, length us, event | category | flops | bytes accessed | tf_op | source)
XLA Modules:
  0.0 176.0 jit_solution(13979142668405101769)
XLA Ops:
  0.0 1.1 copy-done
  1.1 1.9 %skew.1 = bf16[2560,128]{1,0:T(8,128)(2,1)} custom-call(bf16[5,512,128]{2,1,0:T(8,128)(2,1)S(1)} %copy-done), custom_call_target="tpu_custom_call" | custom-call | tf_op jit(solution)/shard_map/skew/pallas_call | solution.py:224
  3.0 20.4 %all-to-all-start.1 = ((bf16[640,4,128]{2,1,0:T(4,128)(2,1)}), bf16[640,4,128]{2,1,0:T(4,128)(2,1)S(1)}, u32[]{:S(2)}, u32[]{:S(2)}) async-start(bf16[640,4,128]{2,1,0:T(4,128)(2,1)} %bitcast.6), calls=%async_computation.1 | async-start | bytes 1310720 | tf_op jit(solution)/shard_map/all_to_all | solution.py:214
  23.5 4.2 %collective-permute-start.1 = (bf16[7,512,128]{2,1,0:T(8,128)(2,1)S(1)}, bf16[7,512,128]{2,1,0:T(8,128)(2,1)S(1)}, u32[]{:S(2)}, u32[]{:S(2)}) collective-permute-start(bf16[7,512,128]{2,1,0:T(8,128)(2,1)S(1)} %pad_maximum_fusion.g0), channel_id=1, source_target_pairs={{0,2},{1,3},{2,0},{3,1},{4,6},{5,7},{6,4},{7,5},{8,10},{9,11},{10,... | collective-permute-start | bytes 2752520 | tf_op jit(solution)/shard_map/ppermute | solution.py:218
  27.8 1.9 %collective-permute-start = (bf16[7,512,128]{2,1,0:T(8,128)(2,1)S(1)}, bf16[7,512,128]{2,1,0:T(8,128)(2,1)}, u32[]{:S(2)}, u32[]{:S(2)}) collective-permute-start(bf16[7,512,128]{2,1,0:T(8,128)(2,1)S(1)} %pad_maximum_fusion.g0), channel_id=1, source_target_pairs={{0,1},{1,0},{2,3},{3,2},{4,5},{5,4},{6,7},{7,6},{8,9},{9,8},{10,11... | collective-permute-start | bytes 2752520 | tf_op jit(solution)/shard_map/ppermute | solution.py:218
  29.7 24.5 %collective-permute-done.1.g2 = bf16[7,512,128]{2,1,0:T(8,128)(2,1)S(1)} collective-permute-done((bf16[7,512,128]{2,1,0:T(8,128)(2,1)S(1)}, bf16[7,512,128]{2,1,0:T(8,128)(2,1)S(1)}, u32[]{:S(2)}, u32[]{:S(2)}) %collective-permute-start.1) | collective-permute-done | bytes 917536 | tf_op jit(solution)/shard_map/ppermute | solution.py:218
  54.2 1.9 %collective-permute-start.2 = (bf16[7,512,128]{2,1,0:T(8,128)(2,1)S(1)}, bf16[7,512,128]{2,1,0:T(8,128)(2,1)}, u32[]{:S(2)}, u32[]{:S(2)}) collective-permute-start(bf16[7,512,128]{2,1,0:T(8,128)(2,1)S(1)} %collective-permute-done.1.g2), channel_id=1, source_target_pairs={{0,1},{1,0},{2,3},{3,2},{4,5},{5,4},{6,7},{7,6},{8,9},{9,8},{10,11... | collective-permute-start | bytes 2752520 | tf_op jit(solution)/shard_map/ppermute | solution.py:218
  56.1 2.6 %collective-permute-done.2.g3 = bf16[7,512,128]{2,1,0:T(8,128)(2,1)} collective-permute-done((bf16[7,512,128]{2,1,0:T(8,128)(2,1)S(1)}, bf16[7,512,128]{2,1,0:T(8,128)(2,1)}, u32[]{:S(2)}, u32[]{:S(2)}) %collective-permute-start.2) | collective-permute-done | bytes 917536 | tf_op jit(solution)/shard_map/ppermute | solution.py:218
  58.7 1.0 copy-done.3
  59.7 1.0 copy-done.4
  60.8 8.1 %particle.1 = (bf16[5,512,128]{2,1,0:T(8,128)(2,1)S(1)}, bf16[2560,128]{1,0:T(8,128)(2,1)}) custom-call(s32[1]{0:T(128)} %bitcast.c_ref, bf16[7,512,128]{2,1,0:T(8,128)(2,1)S(1)} %pad_maximum_fusion.g0, bf16[7,512,128]{2,1,0:T(8,128)(2,1)} %collective-permute-done.g1, bf16[7,512,128]{2,1,0:T(8,128)(2,1)S(1)} %collective-permute-done.1.g2, ...), custom_call_target="tpu_custom_call" | custom-call | tf_op jit(solution)/shard_map/particle/pallas_call | solution.py:234
  68.9 17.1 %all-to-all-start = ((bf16[640,4,128]{2,1,0:T(4,128)(2,1)}), bf16[640,4,128]{2,1,0:T(4,128)(2,1)S(1)}, u32[]{:S(2)}, u32[]{:S(2)}) async-start(bf16[640,4,128]{2,1,0:T(4,128)(2,1)} %bitcast.3), calls=%async_computation | async-start | bytes 1310720 | tf_op jit(solution)/shard_map/all_to_all | solution.py:214
  86.3 2.5 %weights.1 = (bf16[640,640]{1,0:T(8,128)(2,1)S(1)}, bf16[640,640]{1,0:T(8,128)(2,1)S(1)}) custom-call(s32[640,1]{1,0:T(8,128)S(1)} %reshape.65.pair_col, s32[1,640]{1,0:T(1,128)S(1)} %reshape.61.pair_row, s32[640,1]{1,0:T(8,128)S(1)} %reshape.66.partner_col, bf16[576,576]{1,0:T(8,128)(2,1)S(1)} %copy-done.2), custom_call_target="tpu_custom_call" | custom-call | tf_op jit(solution)/shard_map/weights/pallas_call | solution.py:231
  88.8 1.6 ladder.1
  90.4 1.9 %collective-permute-start.3 = (bf16[640,128]{1,0:T(8,128)(2,1)S(1)}, bf16[640,128]{1,0:T(8,128)(2,1)S(1)}, u32[]{:S(2)}, u32[]{:S(2)}) collective-permute-start(bf16[640,128]{1,0:T(8,128)(2,1)S(1)} %get-tuple-element.19), channel_id=1, source_target_pairs={{0,1},{1,0},{2,3},{3,2},{4,5},{5,4},{6,7},{7,6},{8,9},{9,8},{10,11... | collective-permute-start | bytes 491528 | tf_op jit(solution)/shard_map/ppermute | solution.py:218
  92.3 4.0 %collective-permute-start.4 = (bf16[640,128]{1,0:T(8,128)(2,1)S(1)}, bf16[640,128]{1,0:T(8,128)(2,1)S(1)}, u32[]{:S(2)}, u32[]{:S(2)}) collective-permute-start(bf16[640,128]{1,0:T(8,128)(2,1)S(1)} %get-tuple-element.20), channel_id=1, source_target_pairs={{0,2},{1,3},{2,0},{3,1},{4,6},{5,7},{6,4},{7,5},{8,10},{9,11},{10,... | collective-permute-start | bytes 491528 | tf_op jit(solution)/shard_map/ppermute | solution.py:218
  96.3 3.2 %collective-permute-start.5 = (bf16[640,128]{1,0:T(8,128)(2,1)S(1)}, bf16[640,128]{1,0:T(8,128)(2,1)S(1)}, u32[]{:S(2)}, u32[]{:S(2)}) collective-permute-start(bf16[640,128]{1,0:T(8,128)(2,1)S(1)} %get-tuple-element.21), channel_id=1, source_target_pairs={{0,3},{1,2},{2,1},{3,0},{4,7},{5,6},{6,5},{7,4},{8,11},{9,10},{10,... | collective-permute-start | bytes 491528 | tf_op jit(solution)/shard_map/ppermute | solution.py:218
  99.5 4.4 %collective-permute-done.4.m2 = bf16[640,128]{1,0:T(8,128)(2,1)S(1)} collective-permute-done((bf16[640,128]{1,0:T(8,128)(2,1)S(1)}, bf16[640,128]{1,0:T(8,128)(2,1)S(1)}, u32[]{:S(2)}, u32[]{:S(2)}) %collective-permute-start.4) | collective-permute-done | bytes 163872 | tf_op jit(solution)/shard_map/ppermute | solution.py:218
  103.9 4.2 %collective-permute-done.5.m3 = bf16[640,128]{1,0:T(8,128)(2,1)S(1)} collective-permute-done((bf16[640,128]{1,0:T(8,128)(2,1)S(1)}, bf16[640,128]{1,0:T(8,128)(2,1)S(1)}, u32[]{:S(2)}, u32[]{:S(2)}) %collective-permute-start.5) | collective-permute-done | bytes 163872 | tf_op jit(solution)/shard_map/ppermute | solution.py:218
  108.1 16.4 %all-to-all-done = bf16[640,4,128]{2,1,0:T(4,128)(2,1)S(1)} async-done(((bf16[640,4,128]{2,1,0:T(4,128)(2,1)}), bf16[640,4,128]{2,1,0:T(4,128)(2,1)S(1)}, u32[]{:S(2)}, u32[]{:S(2)}) %all-to-all-start) | async-done | bytes 655392 | tf_op jit(solution)/shard_map/all_to_all | solution.py:214
  124.5 1.8 %combine.1 = bf16[2560,128]{1,0:T(8,128)(2,1)} custom-call(s32[1]{0:T(128)} %bitcast.c_ref, bf16[2560,128]{1,0:T(8,128)(2,1)S(1)} %bitcast.11, bf16[640,512]{1,0:T(8,128)(2,1)S(1)} %get-tuple-element.17.l_ref, bf16[640,128]{1,0:T(8,128)(2,1)S(1)} %get-tuple-element.18.m0, bf16[640,128]{1,0:T(8,128)(2,1)S(1)} %collective-permute-done.3.m1, ...), custom_call_target="tpu_custom_call" | custom-call | tf_op jit(solution)/shard_map/combine/pallas_call | solution.py:254
  126.3 7.9 %all-to-all-start.2 = ((bf16[640,4,128]{2,1,0:T(4,128)(2,1)}), bf16[640,4,128]{2,1,0:T(4,128)(2,1)S(1)}, u32[]{:S(2)}, u32[]{:S(2)}) async-start(bf16[640,4,128]{2,1,0:T(4,128)(2,1)} %bitcast.8), calls=%async_computation.2 | async-start | bytes 1310720 | tf_op jit(solution)/shard_map/all_to_all | solution.py:214
  135.1 38.0 %all-to-all-done.2 = bf16[640,4,128]{2,1,0:T(4,128)(2,1)S(1)} async-done(((bf16[640,4,128]{2,1,0:T(4,128)(2,1)}), bf16[640,4,128]{2,1,0:T(4,128)(2,1)S(1)}, u32[]{:S(2)}, u32[]{:S(2)}) %all-to-all-start.2) | async-done | bytes 655392 | tf_op jit(solution)/shard_map/all_to_all | solution.py:214
  173.1 2.9 %finish.1 = f32[5,512,128]{2,1,0:T(8,128)} custom-call(f32[5]{0:T(128)S(1)} %compare_select_fusion.occ_ref, bf16[2560,128]{1,0:T(8,128)(2,1)S(1)} %bitcast.12, bf16[5,512,128]{2,1,0:T(8,128)(2,1)S(1)} %get-tuple-element.22.p_ref, f32[512,128]{1,0:T(8,128)S(1)} %broadcast_add_fusion.base_ref), custom_call_target="tpu_custom_call" | custom-call | tf_op jit(solution)/shard_map/finish/pallas_call | solution.py:280
  (34 shorter events, 1.3 us)
Async XLA Ops:
  0.0 1.1 copy-start
  1.1 22.3 %copy-start.1 = (bf16[5,512,128]{2,1,0:T(8,128)(2,1)S(1)}, bf16[5,512,128]{2,1,0:T(8,128)(2,1)}, u32[]{:S(2)}) copy-start(bf16[5,512,128]{2,1,0:T(8,128)(2,1)} %a_ref.1) | copy-start | bytes 1966084
  1.1 22.3 %copy-start.5 = (bf16[512,128]{1,0:T(8,128)(2,1)S(1)}, bf16[512,128]{1,0:T(8,128)(2,1)}, u32[]{:S(2)}) copy-start(bf16[512,128]{1,0:T(8,128)(2,1)} %param.15) | copy-start | bytes 393220
  1.1 22.3 %copy-start.6 = (bf16[512,128]{1,0:T(8,128)(2,1)S(1)}, bf16[512,128]{1,0:T(8,128)(2,1)}, u32[]{:S(2)}) copy-start(bf16[512,128]{1,0:T(8,128)(2,1)} %param.14) | copy-start | bytes 393220
  3.0 65.8 %all-to-all-start.1 = ((bf16[640,4,128]{2,1,0:T(4,128)(2,1)}), bf16[640,4,128]{2,1,0:T(4,128)(2,1)S(1)}, u32[]{:S(2)}, u32[]{:S(2)}) async-start(bf16[640,4,128]{2,1,0:T(4,128)(2,1)} %bitcast.6), calls=%async_computation.1 | async-start | bytes 1310720 | tf_op jit(solution)/shard_map/all_to_all | solution.py:214
  23.5 30.6 %collective-permute-start.1 = (bf16[7,512,128]{2,1,0:T(8,128)(2,1)S(1)}, bf16[7,512,128]{2,1,0:T(8,128)(2,1)S(1)}, u32[]{:S(2)}, u32[]{:S(2)}) collective-permute-start(bf16[7,512,128]{2,1,0:T(8,128)(2,1)S(1)} %pad_maximum_fusion.g0), channel_id=1, source_target_pairs={{0,2},{1,3},{2,0},{3,1},{4,6},{5,7},{6,4},{7,5},{8,10},{9,11},{10,... | collective-permute-start | bytes 2752520 | tf_op jit(solution)/shard_map/ppermute | solution.py:218
  27.8 28.3 %collective-permute-start = (bf16[7,512,128]{2,1,0:T(8,128)(2,1)S(1)}, bf16[7,512,128]{2,1,0:T(8,128)(2,1)}, u32[]{:S(2)}, u32[]{:S(2)}) collective-permute-start(bf16[7,512,128]{2,1,0:T(8,128)(2,1)S(1)} %pad_maximum_fusion.g0), channel_id=1, source_target_pairs={{0,1},{1,0},{2,3},{3,2},{4,5},{5,4},{6,7},{7,6},{8,9},{9,8},{10,11... | collective-permute-start | bytes 2752520 | tf_op jit(solution)/shard_map/ppermute | solution.py:218
  54.2 4.5 %collective-permute-start.2 = (bf16[7,512,128]{2,1,0:T(8,128)(2,1)S(1)}, bf16[7,512,128]{2,1,0:T(8,128)(2,1)}, u32[]{:S(2)}, u32[]{:S(2)}) collective-permute-start(bf16[7,512,128]{2,1,0:T(8,128)(2,1)S(1)} %collective-permute-done.1.g2), channel_id=1, source_target_pairs={{0,1},{1,0},{2,3},{3,2},{4,5},{5,4},{6,7},{7,6},{8,9},{9,8},{10,11... | collective-permute-start | bytes 2752520 | tf_op jit(solution)/shard_map/ppermute | solution.py:218
  58.7 1.0 copy-start.3
  59.7 1.0 copy-start.4
  68.8 17.2 %copy-start.7 = (s32[640]{0:T(1024)S(1)}, s32[640]{0:T(1024)}, u32[]{:S(2)}) copy-start(s32[640]{0:T(1024)} %param.17) | copy-start | bytes 7684
  68.8 17.3 %copy-start.8 = (s32[640]{0:T(1024)S(1)}, s32[640]{0:T(1024)}, u32[]{:S(2)}) copy-start(s32[640]{0:T(1024)} %param.18) | copy-start | bytes 7684
  68.8 17.5 %copy-start.2 = (bf16[576,576]{1,0:T(8,128)(2,1)S(1)}, bf16[576,576]{1,0:T(8,128)(2,1)}, u32[]{:S(2)}) copy-start(bf16[576,576]{1,0:T(8,128)(2,1)} %h_ref.1) | copy-start | bytes 1990660
  68.9 55.7 %all-to-all-start = ((bf16[640,4,128]{2,1,0:T(4,128)(2,1)}), bf16[640,4,128]{2,1,0:T(4,128)(2,1)S(1)}, u32[]{:S(2)}, u32[]{:S(2)}) async-start(bf16[640,4,128]{2,1,0:T(4,128)(2,1)} %bitcast.3), calls=%async_computation | async-start | bytes 1310720 | tf_op jit(solution)/shard_map/all_to_all | solution.py:214
  90.4 9.1 %collective-permute-start.3 = (bf16[640,128]{1,0:T(8,128)(2,1)S(1)}, bf16[640,128]{1,0:T(8,128)(2,1)S(1)}, u32[]{:S(2)}, u32[]{:S(2)}) collective-permute-start(bf16[640,128]{1,0:T(8,128)(2,1)S(1)} %get-tuple-element.19), channel_id=1, source_target_pairs={{0,1},{1,0},{2,3},{3,2},{4,5},{5,4},{6,7},{7,6},{8,9},{9,8},{10,11... | collective-permute-start | bytes 491528 | tf_op jit(solution)/shard_map/ppermute | solution.py:218
  92.3 11.6 %collective-permute-start.4 = (bf16[640,128]{1,0:T(8,128)(2,1)S(1)}, bf16[640,128]{1,0:T(8,128)(2,1)S(1)}, u32[]{:S(2)}, u32[]{:S(2)}) collective-permute-start(bf16[640,128]{1,0:T(8,128)(2,1)S(1)} %get-tuple-element.20), channel_id=1, source_target_pairs={{0,2},{1,3},{2,0},{3,1},{4,6},{5,7},{6,4},{7,5},{8,10},{9,11},{10,... | collective-permute-start | bytes 491528 | tf_op jit(solution)/shard_map/ppermute | solution.py:218
  96.3 11.8 %collective-permute-start.5 = (bf16[640,128]{1,0:T(8,128)(2,1)S(1)}, bf16[640,128]{1,0:T(8,128)(2,1)S(1)}, u32[]{:S(2)}, u32[]{:S(2)}) collective-permute-start(bf16[640,128]{1,0:T(8,128)(2,1)S(1)} %get-tuple-element.21), channel_id=1, source_target_pairs={{0,3},{1,2},{2,1},{3,0},{4,7},{5,6},{6,5},{7,4},{8,11},{9,10},{10,... | collective-permute-start | bytes 491528 | tf_op jit(solution)/shard_map/ppermute | solution.py:218
  126.3 8.0 %copy-start.9 = (f32[512]{0:T(512)S(1)}, f32[512]{0:T(512)}, u32[]{:S(2)}) copy-start(f32[512]{0:T(512)} %param.20) | copy-start | bytes 6148
  126.3 8.0 %copy-start.10 = (s32[512]{0:T(512)S(1)}, s32[512]{0:T(512)}, u32[]{:S(2)}) copy-start(s32[512]{0:T(512)} %param.21) | copy-start | bytes 6148
  126.3 8.4 %copy-start.11 = (f32[24]{0:T(128)S(1)}, f32[24]{0:T(128)}, u32[]{:S(2)}) copy-start(f32[24]{0:T(128)} %param.19) | copy-start | bytes 292
  126.3 46.8 %all-to-all-start.2 = ((bf16[640,4,128]{2,1,0:T(4,128)(2,1)}), bf16[640,4,128]{2,1,0:T(4,128)(2,1)S(1)}, u32[]{:S(2)}, u32[]{:S(2)}) async-start(bf16[640,4,128]{2,1,0:T(4,128)(2,1)} %bitcast.8), calls=%async_computation.2 | async-start | bytes 1310720 | tf_op jit(solution)/shard_map/all_to_all | solution.py:214

commit v2 on v1

--- a/solution.py
+++ b/solution.py
@@ -1,5 +1,3 @@
-import functools
-
 import jax
 import jax.numpy as jnp
 from jax import lax
@@ -19,7 +17,7 @@
     return [(start, min(8, total - start)) for start in range(0, total, 8)]
 
 
-def swap_rows(values, bits, first_bit, lanes):
+def swap_rows(values, bits, first_bit):
     for step in range(bits):
         take = ((lax.broadcasted_iota(jnp.int32, values[0].shape, 1) >> (first_bit + step)) & 1) == 1
         bit = 1 << step
@@ -39,12 +37,12 @@
         for base in range(1 << high):
             rows = [(base << low) + i for i in range(1 << low)]
             values = [source[pl.ds(start * nb + r, size, stride=nb), :] for r in rows]
-            for r, value in zip(rows, swap_rows(values, low, 0, nb)):
+            for r, value in zip(rows, swap_rows(values, low, 0)):
                 middle[r, start : start + size, :] = value
         for base in range(1 << low):
             rows = [base + (i << low) for i in range(1 << high)]
             values = [middle[r, start : start + size, :] for r in rows]
-            for r, value in zip(rows, swap_rows(values, high, low, nb)):
+            for r, value in zip(rows, swap_rows(values, high, low)):
                 target[r * count + start : r * count + start + size, :] = value
 
 
@@ -54,12 +52,12 @@
         for base in range(1 << low):
             rows = [base + (i << low) for i in range(1 << high)]
             values = [source[r * count + start : r * count + start + size, :] for r in rows]
-            for r, value in zip(rows, swap_rows(values, high, low, nb)):
+            for r, value in zip(rows, swap_rows(values, high, low)):
                 middle[r, start : start + size, :] = value
         for base in range(1 << high):
             rows = [(base << low) + i for i in range(1 << low)]
             values = [middle[r, start : start + size, :] for r in rows]
-            for r, value in zip(rows, swap_rows(values, low, 0, nb)):
+            for r, value in zip(rows, swap_rows(values, low, 0)):
                 target[pl.ds(start * nb + r, size, stride=nb), :] = value
 
 
@@ -96,7 +94,7 @@
 ):
     parts = (g0, g1, g2, g3)
     ncol = len(parts)
-    nslot, nvirt, nb = p_ref.shape
+    nslot, _, nb = p_ref.shape
     col = c_ref[0]
     for i in range(ncol):
         rows = pl.ds(pl.multiple_of((col ^ i) * nb, nb), nb)
@@ -172,19 +170,18 @@
 VMEM = pl.BlockSpec(memory_space=pltpu.VMEM)
 
 
-def call(kernel, outs, scratch, specs, name):
+def call(kernel, outs, scratch, specs):
     return pl.pallas_call(
         kernel,
         out_shape=outs,
         in_specs=specs,
         out_specs=jax.tree.map(lambda _: VMEM, outs),
         scratch_shapes=scratch,
-        name=name,
-        compiler_params=pltpu.CompilerParams(vmem_limit_bytes=48 << 20),
-    )
-
-
-def body(
+        compiler_params=pltpu.CompilerParams(vmem_limit_bytes=20 << 20),
+    )
+
+
+def update_of(
     amplitudes,
     fock_left,
     dress_left,
@@ -222,21 +219,20 @@
     near = swap(own, 1)
     both = swap(far, 1)
     skewed = call(
-        skew_kernel, shape((nb * count, nb), BF16), skew_scratch(count, nb), [VMEM], "skew"
+        skew_kernel, shape((nb * count, nb), BF16), skew_scratch(count, nb), [VMEM]
     )(amplitudes)
     x = exchange(skewed)
     pair_col = slot_pair.reshape(slots, 1)
     pair_row = slot_pair.reshape(1, slots)
     partner_col = partner.reshape(slots, 1)
     w, w2 = call(
-        weights_kernel, [shape((slots, slots), BF16)] * 2, [], [VMEM] * 4, "weights"
+        weights_kernel, [shape((slots, slots), BF16)] * 2, [], [VMEM] * 4
     )(pair_col, pair_row, partner_col, hole_ladder)
     particle, particle_rows = call(
         particle_kernel,
         [shape(amplitudes.shape, BF16), shape((nb * count, nb), BF16)],
         [pltpu.VMEM((nvirt, nvirt), BF16)] * 3 + skew_scratch(count, nb),
         [SMEM] + [VMEM] * 6,
-        "particle",
     )(col_s, own, near, far, both, fock_left, dress_left)
     y = exchange(particle_rows)
     ladder, m0, m1, m2, m3 = call(
@@ -248,7 +244,6 @@
             pltpu.VMEM((ncol, slots, nb), BF16),
         ],
         [SMEM] * 2 + [VMEM] * 3,
-        "ladder",
     )(col_s, pair_s, x, w, w2)
     m1, m2, m3 = swap(m1, 1), swap(m2, 2), swap(m3, 3)
     back = call(
@@ -260,7 +255,6 @@
             pltpu.VMEM((ncol, slots, nb), BF16),
         ],
         [SMEM] + [VMEM] * 7,
-        "combine",
     )(col_s, y, ladder, m0, m1, m2, m3, partner_col)
     z = exchange(back)
     own_pairs = lax.dynamic_slice_in_dim(slot_pair, pair * slot_dev, slot_dev)
@@ -278,11 +272,7 @@
     col_energy = lax.dynamic_slice_in_dim(row_energy, col * nb, nb)
     base = row_energy[:, None] + col_energy[None, :]
     return call(
-        finish_kernel,
-        shape(amplitudes.shape, F32),
-        skew_scratch(count, nb),
-        [SMEM] + [VMEM] * 3,
-        "finish",
+        finish_kernel, shape(amplitudes.shape, F32), skew_scratch(count, nb), [SMEM] + [VMEM] * 3
     )(occ_sum, z, particle, base)
 
 
@@ -301,5 +291,5 @@
         P(),
     )
     return jax.shard_map(
-        body, mesh=mesh, in_specs=placed, out_specs=P("pair", None, "col"), check_vma=False
-    )
+        update_of, mesh=mesh, in_specs=placed, out_specs=P("pair", None, "col"), check_vma=False
+    )

time: 177 us -> 177 us (level)
  no operation moved by 1% of the time
where the time goes in v2:
time: 177 us; the launch traced here: 176 us
  waiting for transfers between devices  90.1 us (51%)
  starting transfers between devices  62.5 us (35%)
  Pallas kernels  18.7 us (11%)
  local copies, waits for them, and re-layouts  3.56 us (2%)
    all_to_all x3, waiting for transfers between devices, exchange(): got = lax.all_to_all(sent, 'pair', split_axis=0, concat_axis=0, tiled=True)  54.4 us
    all_to_all x3, starting transfers between devices, exchange(): got = lax.all_to_all(sent, 'pair', split_axis=0, concat_axis=0, tiled=True)  45.4 us
    ppermute x6, waiting for transfers between devices, swap(): return lax.ppermute(value, 'col', [(i, i ^ k) for i in range(ncol)])  35.6 us
    ppermute x6, starting transfers between devices, swap(): return lax.ppermute(value, 'col', [(i, i ^ k) for i in range(ncol)])  17.1 us
    pallas_call x1, Pallas kernels, update_of(): call(particle_kernel, [shape(amplitudes.shape, BF16), shape((nb * count,...  8.09 us
  transfers between devices with their start and end apart: 9, of which 6 were waited for; matrix products, arithmetic and copies ran while one was open for 1% of the time, Pallas kernels for 7%

profile of v2, /device:TPU:8, one launch (start us, length us, event | category | flops | bytes accessed | tf_op | source)
XLA Modules:
  0.0 176.0 jit_solution(9545880281993850598)
XLA Ops:
  0.0 1.1 copy-done
  1.1 1.9 %shard_map.110 = bf16[2560,128]{1,0:T(8,128)(2,1)} custom-call(bf16[5,512,128]{2,1,0:T(8,128)(2,1)S(1)} %copy-done), custom_call_target="tpu_custom_call" | custom-call | tf_op jit(solution)/shard_map/pallas_call | solution.py:221
  3.0 20.4 %all-to-all-start.1 = ((bf16[640,4,128]{2,1,0:T(4,128)(2,1)}), bf16[640,4,128]{2,1,0:T(4,128)(2,1)S(1)}, u32[]{:S(2)}, u32[]{:S(2)}) async-start(bf16[640,4,128]{2,1,0:T(4,128)(2,1)} %bitcast.6), calls=%async_computation.1 | async-start | bytes 1310720 | tf_op jit(solution)/shard_map/all_to_all | solution.py:211
  23.5 4.2 %collective-permute-start.1 = (bf16[7,512,128]{2,1,0:T(8,128)(2,1)S(1)}, bf16[7,512,128]{2,1,0:T(8,128)(2,1)S(1)}, u32[]{:S(2)}, u32[]{:S(2)}) collective-permute-start(bf16[7,512,128]{2,1,0:T(8,128)(2,1)S(1)} %pad_maximum_fusion.g0), channel_id=1, source_target_pairs={{0,2},{1,3},{2,0},{3,1},{4,6},{5,7},{6,4},{7,5},{8,10},{9,11},{10,... | collective-permute-start | bytes 2752520 | tf_op jit(solution)/shard_map/ppermute | solution.py:215
  27.8 1.9 %collective-permute-start = (bf16[7,512,128]{2,1,0:T(8,128)(2,1)S(1)}, bf16[7,512,128]{2,1,0:T(8,128)(2,1)}, u32[]{:S(2)}, u32[]{:S(2)}) collective-permute-start(bf16[7,512,128]{2,1,0:T(8,128)(2,1)S(1)} %pad_maximum_fusion.g0), channel_id=1, source_target_pairs={{0,1},{1,0},{2,3},{3,2},{4,5},{5,4},{6,7},{7,6},{8,9},{9,8},{10,11... | collective-permute-start | bytes 2752520 | tf_op jit(solution)/shard_map/ppermute | solution.py:215
  29.7 24.5 %collective-permute-done.1.g2 = bf16[7,512,128]{2,1,0:T(8,128)(2,1)S(1)} collective-permute-done((bf16[7,512,128]{2,1,0:T(8,128)(2,1)S(1)}, bf16[7,512,128]{2,1,0:T(8,128)(2,1)S(1)}, u32[]{:S(2)}, u32[]{:S(2)}) %collective-permute-start.1) | collective-permute-done | bytes 917536 | tf_op jit(solution)/shard_map/ppermute | solution.py:215
  54.2 1.9 %collective-permute-start.2 = (bf16[7,512,128]{2,1,0:T(8,128)(2,1)S(1)}, bf16[7,512,128]{2,1,0:T(8,128)(2,1)}, u32[]{:S(2)}, u32[]{:S(2)}) collective-permute-start(bf16[7,512,128]{2,1,0:T(8,128)(2,1)S(1)} %collective-permute-done.1.g2), channel_id=1, source_target_pairs={{0,1},{1,0},{2,3},{3,2},{4,5},{5,4},{6,7},{7,6},{8,9},{9,8},{10,11... | collective-permute-start | bytes 2752520 | tf_op jit(solution)/shard_map/ppermute | solution.py:215
  56.1 2.6 %collective-permute-done.2.g3 = bf16[7,512,128]{2,1,0:T(8,128)(2,1)} collective-permute-done((bf16[7,512,128]{2,1,0:T(8,128)(2,1)S(1)}, bf16[7,512,128]{2,1,0:T(8,128)(2,1)}, u32[]{:S(2)}, u32[]{:S(2)}) %collective-permute-start.2) | collective-permute-done | bytes 917536 | tf_op jit(solution)/shard_map/ppermute | solution.py:215
  58.7 1.0 copy-done.3
  59.7 1.0 copy-done.4
  60.8 8.1 %shard_map.109 = (bf16[5,512,128]{2,1,0:T(8,128)(2,1)S(1)}, bf16[2560,128]{1,0:T(8,128)(2,1)}) custom-call(s32[1]{0:T(128)} %bitcast.c_ref, bf16[7,512,128]{2,1,0:T(8,128)(2,1)S(1)} %pad_maximum_fusion.g0, bf16[7,512,128]{2,1,0:T(8,128)(2,1)} %collective-permute-done.g1, bf16[7,512,128]{2,1,0:T(8,128)(2,1)S(1)} %collective-permute-done.1.g2, ...), custom_call_target="tpu_custom_call" | custom-call | tf_op jit(solution)/shard_map/pallas_call | solution.py:231
  68.9 17.1 %all-to-all-start = ((bf16[640,4,128]{2,1,0:T(4,128)(2,1)}), bf16[640,4,128]{2,1,0:T(4,128)(2,1)S(1)}, u32[]{:S(2)}, u32[]{:S(2)}) async-start(bf16[640,4,128]{2,1,0:T(4,128)(2,1)} %bitcast.3), calls=%async_computation | async-start | bytes 1310720 | tf_op jit(solution)/shard_map/all_to_all | solution.py:211
  86.3 2.5 %shard_map.111 = (bf16[640,640]{1,0:T(8,128)(2,1)S(1)}, bf16[640,640]{1,0:T(8,128)(2,1)S(1)}) custom-call(s32[640,1]{1,0:T(8,128)S(1)} %reshape.65.pair_col, s32[1,640]{1,0:T(1,128)S(1)} %reshape.61.pair_row, s32[640,1]{1,0:T(8,128)S(1)} %reshape.66.partner_col, bf16[576,576]{1,0:T(8,128)(2,1)S(1)} %copy-done.2), custom_call_target="tpu_custom_call" | custom-call | tf_op jit(solution)/shard_map/pallas_call | solution.py:228
  88.8 1.6 shard_map.112
  90.4 1.9 %collective-permute-start.3 = (bf16[640,128]{1,0:T(8,128)(2,1)S(1)}, bf16[640,128]{1,0:T(8,128)(2,1)S(1)}, u32[]{:S(2)}, u32[]{:S(2)}) collective-permute-start(bf16[640,128]{1,0:T(8,128)(2,1)S(1)} %get-tuple-element.19), channel_id=1, source_target_pairs={{0,1},{1,0},{2,3},{3,2},{4,5},{5,4},{6,7},{7,6},{8,9},{9,8},{10,11... | collective-permute-start | bytes 491528 | tf_op jit(solution)/shard_map/ppermute | solution.py:215
  92.3 4.0 %collective-permute-start.4 = (bf16[640,128]{1,0:T(8,128)(2,1)S(1)}, bf16[640,128]{1,0:T(8,128)(2,1)S(1)}, u32[]{:S(2)}, u32[]{:S(2)}) collective-permute-start(bf16[640,128]{1,0:T(8,128)(2,1)S(1)} %get-tuple-element.20), channel_id=1, source_target_pairs={{0,2},{1,3},{2,0},{3,1},{4,6},{5,7},{6,4},{7,5},{8,10},{9,11},{10,... | collective-permute-start | bytes 491528 | tf_op jit(solution)/shard_map/ppermute | solution.py:215
  96.3 3.2 %collective-permute-start.5 = (bf16[640,128]{1,0:T(8,128)(2,1)S(1)}, bf16[640,128]{1,0:T(8,128)(2,1)S(1)}, u32[]{:S(2)}, u32[]{:S(2)}) collective-permute-start(bf16[640,128]{1,0:T(8,128)(2,1)S(1)} %get-tuple-element.21), channel_id=1, source_target_pairs={{0,3},{1,2},{2,1},{3,0},{4,7},{5,6},{6,5},{7,4},{8,11},{9,10},{10,... | collective-permute-start | bytes 491528 | tf_op jit(solution)/shard_map/ppermute | solution.py:215
  99.5 4.4 %collective-permute-done.4.m2 = bf16[640,128]{1,0:T(8,128)(2,1)S(1)} collective-permute-done((bf16[640,128]{1,0:T(8,128)(2,1)S(1)}, bf16[640,128]{1,0:T(8,128)(2,1)S(1)}, u32[]{:S(2)}, u32[]{:S(2)}) %collective-permute-start.4) | collective-permute-done | bytes 163872 | tf_op jit(solution)/shard_map/ppermute | solution.py:215
  103.9 4.2 %collective-permute-done.5.m3 = bf16[640,128]{1,0:T(8,128)(2,1)S(1)} collective-permute-done((bf16[640,128]{1,0:T(8,128)(2,1)S(1)}, bf16[640,128]{1,0:T(8,128)(2,1)S(1)}, u32[]{:S(2)}, u32[]{:S(2)}) %collective-permute-start.5) | collective-permute-done | bytes 163872 | tf_op jit(solution)/shard_map/ppermute | solution.py:215
  108.1 16.4 %all-to-all-done = bf16[640,4,128]{2,1,0:T(4,128)(2,1)S(1)} async-done(((bf16[640,4,128]{2,1,0:T(4,128)(2,1)}), bf16[640,4,128]{2,1,0:T(4,128)(2,1)S(1)}, u32[]{:S(2)}, u32[]{:S(2)}) %all-to-all-start) | async-done | bytes 655392 | tf_op jit(solution)/shard_map/all_to_all | solution.py:211
  124.5 1.8 %shard_map.113 = bf16[2560,128]{1,0:T(8,128)(2,1)} custom-call(s32[1]{0:T(128)} %bitcast.c_ref, bf16[2560,128]{1,0:T(8,128)(2,1)S(1)} %bitcast.11, bf16[640,512]{1,0:T(8,128)(2,1)S(1)} %get-tuple-element.17.l_ref, bf16[640,128]{1,0:T(8,128)(2,1)S(1)} %get-tuple-element.18.m0, bf16[640,128]{1,0:T(8,128)(2,1)S(1)} %collective-permute-done.3.m1, ...), custom_call_target="tpu_custom_call" | custom-call | tf_op jit(solution)/shard_map/pallas_call | solution.py:249
  126.3 7.9 %all-to-all-start.2 = ((bf16[640,4,128]{2,1,0:T(4,128)(2,1)}), bf16[640,4,128]{2,1,0:T(4,128)(2,1)S(1)}, u32[]{:S(2)}, u32[]{:S(2)}) async-start(bf16[640,4,128]{2,1,0:T(4,128)(2,1)} %bitcast.8), calls=%async_computation.2 | async-start | bytes 1310720 | tf_op jit(solution)/shard_map/all_to_all | solution.py:211
  135.1 38.0 %all-to-all-done.2 = bf16[640,4,128]{2,1,0:T(4,128)(2,1)S(1)} async-done(((bf16[640,4,128]{2,1,0:T(4,128)(2,1)}), bf16[640,4,128]{2,1,0:T(4,128)(2,1)S(1)}, u32[]{:S(2)}, u32[]{:S(2)}) %all-to-all-start.2) | async-done | bytes 655392 | tf_op jit(solution)/shard_map/all_to_all | solution.py:211
  173.1 2.9 %shard_map.114 = f32[5,512,128]{2,1,0:T(8,128)} custom-call(f32[5]{0:T(128)S(1)} %compare_select_fusion.occ_ref, bf16[2560,128]{1,0:T(8,128)(2,1)S(1)} %bitcast.12, bf16[5,512,128]{2,1,0:T(8,128)(2,1)S(1)} %get-tuple-element.22.p_ref, f32[512,128]{1,0:T(8,128)S(1)} %broadcast_add_fusion.base_ref), custom_call_target="tpu_custom_call" | custom-call | tf_op jit(solution)/shard_map/pallas_call | solution.py:274
  (34 shorter events, 1.3 us)
Async XLA Ops:
  0.0 1.1 copy-start
  1.1 22.3 %copy-start.1 = (bf16[5,512,128]{2,1,0:T(8,128)(2,1)S(1)}, bf16[5,512,128]{2,1,0:T(8,128)(2,1)}, u32[]{:S(2)}) copy-start(bf16[5,512,128]{2,1,0:T(8,128)(2,1)} %a_ref.1) | copy-start | bytes 1966084
  1.1 22.3 %copy-start.5 = (bf16[512,128]{1,0:T(8,128)(2,1)S(1)}, bf16[512,128]{1,0:T(8,128)(2,1)}, u32[]{:S(2)}) copy-start(bf16[512,128]{1,0:T(8,128)(2,1)} %param.15) | copy-start | bytes 393220
  1.1 22.3 %copy-start.6 = (bf16[512,128]{1,0:T(8,128)(2,1)S(1)}, bf16[512,128]{1,0:T(8,128)(2,1)}, u32[]{:S(2)}) copy-start(bf16[512,128]{1,0:T(8,128)(2,1)} %param.14) | copy-start | bytes 393220
  3.0 65.8 %all-to-all-start.1 = ((bf16[640,4,128]{2,1,0:T(4,128)(2,1)}), bf16[640,4,128]{2,1,0:T(4,128)(2,1)S(1)}, u32[]{:S(2)}, u32[]{:S(2)}) async-start(bf16[640,4,128]{2,1,0:T(4,128)(2,1)} %bitcast.6), calls=%async_computation.1 | async-start | bytes 1310720 | tf_op jit(solution)/shard_map/all_to_all | solution.py:211
  23.5 30.6 %collective-permute-start.1 = (bf16[7,512,128]{2,1,0:T(8,128)(2,1)S(1)}, bf16[7,512,128]{2,1,0:T(8,128)(2,1)S(1)}, u32[]{:S(2)}, u32[]{:S(2)}) collective-permute-start(bf16[7,512,128]{2,1,0:T(8,128)(2,1)S(1)} %pad_maximum_fusion.g0), channel_id=1, source_target_pairs={{0,2},{1,3},{2,0},{3,1},{4,6},{5,7},{6,4},{7,5},{8,10},{9,11},{10,... | collective-permute-start | bytes 2752520 | tf_op jit(solution)/shard_map/ppermute | solution.py:215
  27.8 28.3 %collective-permute-start = (bf16[7,512,128]{2,1,0:T(8,128)(2,1)S(1)}, bf16[7,512,128]{2,1,0:T(8,128)(2,1)}, u32[]{:S(2)}, u32[]{:S(2)}) collective-permute-start(bf16[7,512,128]{2,1,0:T(8,128)(2,1)S(1)} %pad_maximum_fusion.g0), channel_id=1, source_target_pairs={{0,1},{1,0},{2,3},{3,2},{4,5},{5,4},{6,7},{7,6},{8,9},{9,8},{10,11... | collective-permute-start | bytes 2752520 | tf_op jit(solution)/shard_map/ppermute | solution.py:215
  54.2 4.5 %collective-permute-start.2 = (bf16[7,512,128]{2,1,0:T(8,128)(2,1)S(1)}, bf16[7,512,128]{2,1,0:T(8,128)(2,1)}, u32[]{:S(2)}, u32[]{:S(2)}) collective-permute-start(bf16[7,512,128]{2,1,0:T(8,128)(2,1)S(1)} %collective-permute-done.1.g2), channel_id=1, source_target_pairs={{0,1},{1,0},{2,3},{3,2},{4,5},{5,4},{6,7},{7,6},{8,9},{9,8},{10,11... | collective-permute-start | bytes 2752520 | tf_op jit(solution)/shard_map/ppermute | solution.py:215
  58.7 1.0 copy-start.3
  59.7 1.0 copy-start.4
  68.8 17.2 %copy-start.7 = (s32[640]{0:T(1024)S(1)}, s32[640]{0:T(1024)}, u32[]{:S(2)}) copy-start(s32[640]{0:T(1024)} %param.17) | copy-start | bytes 7684
  68.8 17.3 %copy-start.8 = (s32[640]{0:T(1024)S(1)}, s32[640]{0:T(1024)}, u32[]{:S(2)}) copy-start(s32[640]{0:T(1024)} %param.18) | copy-start | bytes 7684
  68.8 17.5 %copy-start.2 = (bf16[576,576]{1,0:T(8,128)(2,1)S(1)}, bf16[576,576]{1,0:T(8,128)(2,1)}, u32[]{:S(2)}) copy-start(bf16[576,576]{1,0:T(8,128)(2,1)} %h_ref.1) | copy-start | bytes 1990660
  68.9 55.7 %all-to-all-start = ((bf16[640,4,128]{2,1,0:T(4,128)(2,1)}), bf16[640,4,128]{2,1,0:T(4,128)(2,1)S(1)}, u32[]{:S(2)}, u32[]{:S(2)}) async-start(bf16[640,4,128]{2,1,0:T(4,128)(2,1)} %bitcast.3), calls=%async_computation | async-start | bytes 1310720 | tf_op jit(solution)/shard_map/all_to_all | solution.py:211
  90.4 9.1 %collective-permute-start.3 = (bf16[640,128]{1,0:T(8,128)(2,1)S(1)}, bf16[640,128]{1,0:T(8,128)(2,1)S(1)}, u32[]{:S(2)}, u32[]{:S(2)}) collective-permute-start(bf16[640,128]{1,0:T(8,128)(2,1)S(1)} %get-tuple-element.19), channel_id=1, source_target_pairs={{0,1},{1,0},{2,3},{3,2},{4,5},{5,4},{6,7},{7,6},{8,9},{9,8},{10,11... | collective-permute-start | bytes 491528 | tf_op jit(solution)/shard_map/ppermute | solution.py:215
  92.3 11.6 %collective-permute-start.4 = (bf16[640,128]{1,0:T(8,128)(2,1)S(1)}, bf16[640,128]{1,0:T(8,128)(2,1)S(1)}, u32[]{:S(2)}, u32[]{:S(2)}) collective-permute-start(bf16[640,128]{1,0:T(8,128)(2,1)S(1)} %get-tuple-element.20), channel_id=1, source_target_pairs={{0,2},{1,3},{2,0},{3,1},{4,6},{5,7},{6,4},{7,5},{8,10},{9,11},{10,... | collective-permute-start | bytes 491528 | tf_op jit(solution)/shard_map/ppermute | solution.py:215
  96.3 11.8 %collective-permute-start.5 = (bf16[640,128]{1,0:T(8,128)(2,1)S(1)}, bf16[640,128]{1,0:T(8,128)(2,1)S(1)}, u32[]{:S(2)}, u32[]{:S(2)}) collective-permute-start(bf16[640,128]{1,0:T(8,128)(2,1)S(1)} %get-tuple-element.21), channel_id=1, source_target_pairs={{0,3},{1,2},{2,1},{3,0},{4,7},{5,6},{6,5},{7,4},{8,11},{9,10},{10,... | collective-permute-start | bytes 491528 | tf_op jit(solution)/shard_map/ppermute | solution.py:215
  126.3 8.0 %copy-start.9 = (f32[512]{0:T(512)S(1)}, f32[512]{0:T(512)}, u32[]{:S(2)}) copy-start(f32[512]{0:T(512)} %param.20) | copy-start | bytes 6148
  126.3 8.0 %copy-start.10 = (s32[512]{0:T(512)S(1)}, s32[512]{0:T(512)}, u32[]{:S(2)}) copy-start(s32[512]{0:T(512)} %param.21) | copy-start | bytes 6148
  126.3 8.4 %copy-start.11 = (f32[24]{0:T(128)S(1)}, f32[24]{0:T(128)}, u32[]{:S(2)}) copy-start(f32[24]{0:T(128)} %param.19) | copy-start | bytes 292
  126.3 46.8 %all-to-all-start.2 = ((bf16[640,4,128]{2,1,0:T(4,128)(2,1)}), bf16[640,4,128]{2,1,0:T(4,128)(2,1)S(1)}, u32[]{:S(2)}, u32[]{:S(2)}) async-start(bf16[640,4,128]{2,1,0:T(4,128)(2,1)} %bitcast.8), calls=%async_computation.2 | async-start | bytes 1310720 | tf_op jit(solution)/shard_map/all_to_all | solution.py:211

commit v3 on v2

--- a/solution.py
+++ b/solution.py
@@ -31,9 +31,10 @@
     return low, total - low
 
 
-def skew(source, middle, target, nb, count):
+def skew(source, middle, target, nb, count, ready):
     low, high = split_bits(nb)
     for start, size in chunks_of(count):
+        ready(start, size)
         for base in range(1 << high):
             rows = [(base << low) + i for i in range(1 << low)]
             values = [source[pl.ds(start * nb + r, size, stride=nb), :] for r in rows]
@@ -46,7 +47,7 @@
                 target[r * count + start : r * count + start + size, :] = value
 
 
-def unskew(source, middle, target, nb, count):
+def unskew(source, middle, target, nb, count, done):
     low, high = split_bits(nb)
     for start, size in chunks_of(count):
         for base in range(1 << low):
@@ -59,13 +60,22 @@
             values = [middle[r, start : start + size, :] for r in rows]
             for r, value in zip(rows, swap_rows(values, low, 0)):
                 target[pl.ds(start * nb + r, size, stride=nb), :] = value
-
-
-def skew_kernel(a_ref, out_ref, flat, middle, target):
-    count = a_ref.shape[0] * (a_ref.shape[1] // a_ref.shape[2])
-    nb = a_ref.shape[2]
-    flat[...] = a_ref[...].reshape(count * nb, nb).astype(F32)
-    skew(flat, middle, target, nb, count)
+        done(start, size)
+
+
+def skew_kernel(a_hbm, out_ref, raw, sems, flat, middle, target):
+    nslot, nvirt, nb = raw.shape
+    ncol = nvirt // nb
+    copies = [pltpu.make_async_copy(a_hbm.at[s], raw.at[s], sems.at[s]) for s in range(nslot)]
+    for copy in copies:
+        copy.start()
+
+    def ready(start, size):
+        for s in range(start // ncol, (start + size) // ncol):
+            copies[s].wait()
+            flat[s * nvirt : (s + 1) * nvirt, :] = raw[s].astype(F32)
+
+    skew(flat, middle, target, nb, nslot * ncol, ready)
     out_ref[...] = target[...].astype(BF16)
 
 
@@ -89,36 +99,62 @@
     w2_ref[...] = dot(mirror, w).astype(BF16)
 
 
-def particle_kernel(
-    c_ref, g0, g1, g2, g3, fl_ref, dl_ref, p_ref, out_ref, acat, dmat, fmat, flat, middle, target
+def gather_columns(parts, s, acat):
+    nb = parts[0].shape[2]
+    for k, part in enumerate(parts):
+        acat[:, k * nb : (k + 1) * nb] = part[s]
+    return acat[...]
+
+
+def rows_kernel(
+    c_ref, g0, g1, g2, g3, w0, w1, w2, w3, fl_ref, dl_ref, out_ref,
+    left, right, acat, low, flat, middle, target,
 ):
     parts = (g0, g1, g2, g3)
+    wide = (w0, w1, w2, w3)
     ncol = len(parts)
-    nslot, _, nb = p_ref.shape
+    nslot, nvirt, nb = g0.shape
+    col = c_ref[0]
+    own = pl.ds(pl.multiple_of(col * nb, nb), nb)
+    left[:nb, :] = fl_ref[own, :]
+    left[nb:, :] = dl_ref[own, :]
+    for i in range(ncol):
+        rows = pl.ds(pl.multiple_of((col ^ i) * nb, nb), nb)
+        for k in range(ncol):
+            right[i * nb : (i + 1) * nb, k * nb : (k + 1) * nb] = wide[k][1, rows, :]
+            right[nvirt + i * nb : nvirt + (i + 1) * nb, k * nb : (k + 1) * nb] = wide[k][0, rows, :]
+
+    def ready(start, size):
+        for s in range(start // ncol, (start + size) // ncol):
+            amp = gather_columns(parts, s, acat)
+            first = dot(left[...], amp)
+            low[:, :nvirt] = first[nb:].astype(BF16)
+            for k, part in enumerate(parts):
+                low[:, nvirt + k * nb : nvirt + (k + 1) * nb] = part[s, own, :]
+            total = first[:nb] + dot(low[...], right[...])
+            for k in range(ncol):
+                at = pl.multiple_of((s * ncol + (col ^ k)) * nb, nb)
+                flat[pl.ds(at, nb), :] = total[:, k * nb : (k + 1) * nb].T
+
+    skew(flat, middle, target, nb, nslot * ncol, ready)
+    out_ref[...] = target[...].astype(BF16)
+
+
+def cols_kernel(c_ref, g0, g1, g2, g3, w0, fl_ref, dl_ref, p_ref, right, acat):
+    parts = (g0, g1, g2, g3)
+    ncol = len(parts)
+    nslot, _, nb = g0.shape
     col = c_ref[0]
     for i in range(ncol):
         rows = pl.ds(pl.multiple_of((col ^ i) * nb, nb), nb)
-        for k in range(ncol):
-            fmat[i * nb : (i + 1) * nb, k * nb : (k + 1) * nb] = parts[k][nslot, rows, :]
-            dmat[i * nb : (i + 1) * nb, k * nb : (k + 1) * nb] = parts[k][nslot + 1, rows, :]
-    own = pl.ds(pl.multiple_of(col * nb, nb), nb)
-    fl_own = fl_ref[own, :]
-    dl_own = dl_ref[own, :]
+        right[i * nb : (i + 1) * nb, :nb] = w0[1, rows, :]
+        right[i * nb : (i + 1) * nb, nb:] = w0[0, rows, :]
     for s in range(nslot):
-        for k in range(ncol):
-            acat[:, k * nb : (k + 1) * nb] = parts[k][s]
-        amp = acat[...]
-        dressed = dot(amp, dmat[...]).astype(BF16)
-        own_cols = dot(amp, fmat[:, :nb])
-        own_cols = own_cols + dot(fl_ref[...], amp[:, :nb]) + dot(dl_ref[...], dressed[:, :nb])
-        p_ref[s] = own_cols.astype(BF16)
-        own_rows = dot(acat[own, :], fmat[...]) + dot(fl_own, amp) + dot(dl_own, dressed)
-        own_rows = own_rows.astype(BF16).astype(F32)
-        for k in range(ncol):
-            at = pl.multiple_of((s * ncol + (col ^ k)) * nb, nb)
-            flat[pl.ds(at, nb), :] = own_rows[:, k * nb : (k + 1) * nb].T
-    skew(flat, middle, target, nb, nslot * ncol)
-    out_ref[...] = target[...].astype(BF16)
+        amp = gather_columns(parts, s, acat)
+        both = dot(amp, right[...])
+        dressed = both[:, :nb].astype(BF16)
+        total = both[:, nb:] + dot(fl_ref[...], g0[s]) + dot(dl_ref[...], dressed)
+        p_ref[s] = total.astype(BF16)
 
 
 def ladder_kernel(c_ref, j_ref, x_ref, w_ref, w2_ref, l_ref, m0, m1, m2, m3, wide, xcat, mirror):
@@ -140,42 +176,65 @@
         out[...] = mirror[col ^ k]
 
 
-def combine_kernel(c_ref, y_ref, l_ref, m0, m1, m2, m3, partner_col, out_ref, wide, ycat, mirror):
+def combine_kernel(
+    c_ref, y_ref, l_hbm, m0, m1, m2, m3, partner_col, out_ref, wide, ycat, mirror, l_ref, sems
+):
     slots = l_ref.shape[0]
     nb = y_ref.shape[1]
     ncol = y_ref.shape[0] // slots
+    col = c_ref[0]
+    copies = [pltpu.make_async_copy(l_hbm, l_ref, sems.at[ncol])]
+    for k, part in enumerate((m0, m1, m2, m3)):
+        copies.append(pltpu.make_async_copy(part, mirror.at[col ^ k], sems.at[k]))
+    for copy in copies:
+        copy.start()
     wide[...] = y_ref[...].astype(F32)
     for d in range(ncol):
         ycat[:, d * nb : (d + 1) * nb] = wide[pl.ds(d, slots, stride=ncol), :].astype(BF16)
     pick = (partner_col[...] == lax.broadcasted_iota(jnp.int32, (slots, slots), 1)).astype(BF16)
-    total = dot(pick, ycat[...]) + l_ref[...].astype(F32)
-    col = c_ref[0]
-    for k, part in enumerate((m0, m1, m2, m3)):
-        mirror[col ^ k] = part[...]
+    total = dot(pick, ycat[...])
+    for copy in copies:
+        copy.wait()
     for d in range(ncol):
-        wide[pl.ds(d, slots, stride=ncol), :] = total[:, d * nb : (d + 1) * nb] + mirror[d].astype(F32)
+        at = slice(d * nb, (d + 1) * nb)
+        wide[pl.ds(d, slots, stride=ncol), :] = (
+            total[:, at] + l_ref[:, at].astype(F32) + mirror[d].astype(F32)
+        )
     out_ref[...] = wide[...].astype(BF16)
 
 
-def finish_kernel(occ_ref, z_ref, p_ref, base_ref, out_ref, flat, middle, target):
+def finish_kernel(occ_ref, z_ref, p_ref, base_ref, out_hbm, stage, sems, flat, middle, target):
     nslot, nvirt, nb = p_ref.shape
+    ncol = nvirt // nb
     flat[...] = z_ref[...].astype(F32)
-    unskew(flat, middle, target, nb, nslot * (nvirt // nb))
-    for s in range(nslot):
-        total = p_ref[s].astype(F32) + target[s * nvirt : (s + 1) * nvirt, :]
-        out_ref[s] = total / (base_ref[...] - occ_ref[s])
+    copies = [pltpu.make_async_copy(stage.at[s], out_hbm.at[s], sems.at[s]) for s in range(nslot)]
+
+    def done(start, size):
+        for s in range(start // ncol, (start + size) // ncol):
+            total = p_ref[s].astype(F32) + target[s * nvirt : (s + 1) * nvirt, :]
+            stage[s] = total / (base_ref[...] - occ_ref[s])
+            copies[s].start()
+
+    unskew(flat, middle, target, nb, nslot * ncol, done)
+    for copy in copies:
+        copy.wait()
 
 
 SMEM = pl.BlockSpec(memory_space=pltpu.SMEM)
 VMEM = pl.BlockSpec(memory_space=pltpu.VMEM)
-
-
-def call(kernel, outs, scratch, specs):
+HBM = pl.BlockSpec(memory_space=pltpu.HBM)
+
+
+def stay(value):
+    return pltpu.with_memory_space_constraint(value, pltpu.HBM)
+
+
+def call(kernel, outs, scratch, specs, result=VMEM):
     return pl.pallas_call(
         kernel,
         out_shape=outs,
         in_specs=specs,
-        out_specs=jax.tree.map(lambda _: VMEM, outs),
+        out_specs=jax.tree.map(lambda _: result, outs),
         scratch_shapes=scratch,
         compiler_params=pltpu.CompilerParams(vmem_limit_bytes=20 << 20),
     )
@@ -214,13 +273,14 @@
     def swap(value, k):
         return lax.ppermute(value, "col", [(i, i ^ k) for i in range(ncol)])
 
-    own = jnp.concatenate([amplitudes, fock_right[None], dress_right[None]])
-    far = swap(own, 2)
-    near = swap(own, 1)
-    both = swap(far, 1)
+    far = swap(amplitudes, 2)
+    dma = pltpu.SemaphoreType.DMA
     skewed = call(
-        skew_kernel, shape((nb * count, nb), BF16), skew_scratch(count, nb), [VMEM]
-    )(amplitudes)
+        skew_kernel,
+        shape((nb * count, nb), BF16),
+        [pltpu.VMEM(amplitudes.shape, BF16), dma((slot_dev,))] + skew_scratch(count, nb),
+        [HBM],
+    )(stay(amplitudes))
     x = exchange(skewed)
     pair_col = slot_pair.reshape(slots, 1)
     pair_row = slot_pair.reshape(1, slots)
@@ -228,13 +288,34 @@
     w, w2 = call(
         weights_kernel, [shape((slots, slots), BF16)] * 2, [], [VMEM] * 4
     )(pair_col, pair_row, partner_col, hole_ladder)
-    particle, particle_rows = call(
-        particle_kernel,
-        [shape(amplitudes.shape, BF16), shape((nb * count, nb), BF16)],
-        [pltpu.VMEM((nvirt, nvirt), BF16)] * 3 + skew_scratch(count, nb),
-        [SMEM] + [VMEM] * 6,
-    )(col_s, own, near, far, both, fock_left, dress_left)
+    near = swap(amplitudes, 1)
+    both = swap(far, 1)
+    wide = jnp.stack([fock_right, dress_right])
+    wide_far = swap(wide, 2)
+    wide_near = swap(wide, 1)
+    wide_both = swap(wide_far, 1)
+    particle_rows = call(
+        rows_kernel,
+        shape((nb * count, nb), BF16),
+        [
+            pltpu.VMEM((2 * nb, nvirt), BF16),
+            pltpu.VMEM((2 * nvirt, nvirt), BF16),
+            pltpu.VMEM((nvirt, nvirt), BF16),
+            pltpu.VMEM((nb, 2 * nvirt), BF16),
+        ]
+        + skew_scratch(count, nb),
+        [SMEM] + [VMEM] * 10,
+    )(
+        col_s, amplitudes, near, far, both, wide, wide_near, wide_far, wide_both,
+        fock_left, dress_left,
+    )
     y = exchange(particle_rows)
+    particle = call(
+        cols_kernel,
+        shape(amplitudes.shape, BF16),
+        [pltpu.VMEM((nvirt, 2 * nb), BF16), pltpu.VMEM((nvirt, nvirt), BF16)],
+        [SMEM] + [VMEM] * 7,
+    )(col_s, amplitudes, near, far, both, wide, fock_left, dress_left)
     ladder, m0, m1, m2, m3 = call(
         ladder_kernel,
         [shape((slots, nvirt), BF16)] + [shape((slots, nb), BF16)] * 4,
@@ -253,9 +334,11 @@
             pltpu.VMEM((slots * ncol, nb), F32),
             pltpu.VMEM((slots, nvirt), BF16),
             pltpu.VMEM((ncol, slots, nb), BF16),
+            pltpu.VMEM((slots, nvirt), BF16),
+            dma((ncol + 1,)),
         ],
-        [SMEM] + [VMEM] * 7,
-    )(col_s, y, ladder, m0, m1, m2, m3, partner_col)
+        [SMEM, VMEM] + [HBM] * 5 + [VMEM],
+    )(col_s, y, stay(ladder), stay(m0), stay(m1), stay(m2), stay(m3), partner_col)
     z = exchange(back)
     own_pairs = lax.dynamic_slice_in_dim(slot_pair, pair * slot_dev, slot_dev)
     occ_iota = jnp.arange(nocc, dtype=jnp.int32)
@@ -272,7 +355,11 @@
     col_energy = lax.dynamic_slice_in_dim(row_energy, col * nb, nb)
     base = row_energy[:, None] + col_energy[None, :]
     return call(
-        finish_kernel, shape(amplitudes.shape, F32), skew_scratch(count, nb), [SMEM] + [VMEM] * 3
+        finish_kernel,
+        shape(amplitudes.shape, F32),
+        [pltpu.VMEM(amplitudes.shape, F32), dma((slot_dev,))] + skew_scratch(count, nb),
+        [SMEM] + [VMEM] * 3,
+        HBM,
     )(occ_sum, z, particle, base)
 
 

time: 177 us -> 182 us (1.028)
  the two profiles are of different devices: /device:TPU:8 before, /device:TPU:16 now
where the time goes in v3:
time: 182 us; the launch traced here: 181 us
  waiting for transfers between devices  82.5 us (45%)
  starting transfers between devices  67 us (37%)
  Pallas kernels  21.8 us (12%)
  local copies, waits for them, and re-layouts  8.52 us (5%)
    all_to_all x3, waiting for transfers between devices, exchange(): got = lax.all_to_all(sent, 'pair', split_axis=0, concat_axis=0, tiled=True)  46.5 us
    all_to_all x3, starting transfers between devices, exchange(): got = lax.all_to_all(sent, 'pair', split_axis=0, concat_axis=0, tiled=True)  44.9 us
    ppermute x9, waiting for transfers between devices, swap(): return lax.ppermute(value, 'col', [(i, i ^ k) for i in range(ncol)])  36 us
    ppermute x9, starting transfers between devices, swap(): return lax.ppermute(value, 'col', [(i, i ^ k) for i in range(ncol)])  22.1 us
    unnamed x40, local copies, waits for them, and re-layouts  8.16 us
    pallas_call x1, Pallas kernels, update_of(): call(rows_kernel, shape((nb * count, nb), BF16), [pltpu.VMEM((2 * nb, nvi...  5.35 us
    pallas_call x1, Pallas kernels, update_of(): call(cols_kernel, shape(amplitudes.shape, BF16), [pltpu.VMEM((nvirt, 2 *...  3.71 us
  transfers between devices with their start and end apart: 12, of which 7 were waited for; matrix products, arithmetic and copies ran while one was open for 1% of the time, Pallas kernels for 7%

profile of v3, /device:TPU:16, one launch (start us, length us, event | category | flops | bytes accessed | tf_op | source)
XLA Modules:
  0.0 181.2 jit_solution(15039786105581345691)
XLA Ops:
  0.0 3.0 %shard_map.110 = bf16[2560,128]{1,0:T(8,128)(2,1)} custom-call(bf16[5,512,128]{2,1,0:T(8,128)(2,1)} %g0.3), custom_call_target="tpu_custom_call" | custom-call | tf_op jit(solution)/shard_map/pallas_call | solution.py:278
  3.0 20.5 %all-to-all-start.1 = ((bf16[640,4,128]{2,1,0:T(4,128)(2,1)}), bf16[640,4,128]{2,1,0:T(4,128)(2,1)S(1)}, u32[]{:S(2)}, u32[]{:S(2)}) async-start(bf16[640,4,128]{2,1,0:T(4,128)(2,1)} %bitcast.6), calls=%async_computation.1 | async-start | bytes 1310720 | tf_op jit(solution)/shard_map/all_to_all | solution.py:270
  23.6 2.5 %collective-permute-start.1 = (bf16[5,512,128]{2,1,0:T(8,128)(2,1)S(1)}, bf16[5,512,128]{2,1,0:T(8,128)(2,1)S(1)}, u32[]{:S(2)}, u32[]{:S(2)}) collective-permute-start(bf16[5,512,128]{2,1,0:T(8,128)(2,1)S(1)} %copy-done), channel_id=1, source_target_pairs={{0,2},{1,3},{2,0},{3,1},{4,6},{5,7},{6,4},{7,5},{8,10},{9,11},{10,... | collective-permute-start | bytes 1966088 | tf_op jit(solution)/shard_map/ppermute | solution.py:274
  26.1 1.9 %collective-permute-start = (bf16[5,512,128]{2,1,0:T(8,128)(2,1)S(1)}, bf16[5,512,128]{2,1,0:T(8,128)(2,1)S(1)}, u32[]{:S(2)}, u32[]{:S(2)}) collective-permute-start(bf16[5,512,128]{2,1,0:T(8,128)(2,1)S(1)} %copy-done), channel_id=1, source_target_pairs={{0,1},{1,0},{2,3},{3,2},{4,5},{5,4},{6,7},{7,6},{8,9},{9,8},{10,11... | collective-permute-start | bytes 1966088 | tf_op jit(solution)/shard_map/ppermute | solution.py:274
  28.0 19.3 %collective-permute-done.1.g2 = bf16[5,512,128]{2,1,0:T(8,128)(2,1)S(1)} collective-permute-done((bf16[5,512,128]{2,1,0:T(8,128)(2,1)S(1)}, bf16[5,512,128]{2,1,0:T(8,128)(2,1)S(1)}, u32[]{:S(2)}, u32[]{:S(2)}) %collective-permute-start.1) | collective-permute-done | bytes 655392 | tf_op jit(solution)/shard_map/ppermute | solution.py:274
  47.3 1.9 %collective-permute-start.2 = (bf16[5,512,128]{2,1,0:T(8,128)(2,1)S(1)}, bf16[5,512,128]{2,1,0:T(8,128)(2,1)}, u32[]{:S(2)}, u32[]{:S(2)}) collective-permute-start(bf16[5,512,128]{2,1,0:T(8,128)(2,1)S(1)} %collective-permute-done.1.g2), channel_id=1, source_target_pairs={{0,1},{1,0},{2,3},{3,2},{4,5},{5,4},{6,7},{7,6},{8,9},{9,8},{10,11... | collective-permute-start | bytes 1966088 | tf_op jit(solution)/shard_map/ppermute | solution.py:274
  49.3 2.6 %collective-permute-start.4 = (bf16[2,512,128]{2,1,0:T(8,128)(2,1)S(1)}, bf16[2,512,128]{2,1,0:T(8,128)(2,1)S(1)}, u32[]{:S(2)}, u32[]{:S(2)}) collective-permute-start(bf16[2,512,128]{2,1,0:T(8,128)(2,1)S(1)} %pad_maximum_fusion.w0), channel_id=1, source_target_pairs={{0,2},{1,3},{2,0},{3,1},{4,6},{5,7},{6,4},{7,5},{8,10},{9,11},{10,... | collective-permute-start | bytes 786440 | tf_op jit(solution)/shard_map/ppermute | solution.py:274
  51.9 2.1 %collective-permute-start.3 = (bf16[2,512,128]{2,1,0:T(8,128)(2,1)S(1)}, bf16[2,512,128]{2,1,0:T(8,128)(2,1)S(1)}, u32[]{:S(2)}, u32[]{:S(2)}) collective-permute-start(bf16[2,512,128]{2,1,0:T(8,128)(2,1)S(1)} %pad_maximum_fusion.w0), channel_id=1, source_target_pairs={{0,1},{1,0},{2,3},{3,2},{4,5},{5,4},{6,7},{7,6},{8,9},{9,8},{10,11... | collective-permute-start | bytes 786440 | tf_op jit(solution)/shard_map/ppermute | solution.py:274
  54.1 7.5 %collective-permute-done.4.w2 = bf16[2,512,128]{2,1,0:T(8,128)(2,1)S(1)} collective-permute-done((bf16[2,512,128]{2,1,0:T(8,128)(2,1)S(1)}, bf16[2,512,128]{2,1,0:T(8,128)(2,1)S(1)}, u32[]{:S(2)}, u32[]{:S(2)}) %collective-permute-start.4) | collective-permute-done | bytes 262176 | tf_op jit(solution)/shard_map/ppermute | solution.py:274
  61.6 1.9 %collective-permute-start.5 = (bf16[2,512,128]{2,1,0:T(8,128)(2,1)S(1)}, bf16[2,512,128]{2,1,0:T(8,128)(2,1)}, u32[]{:S(2)}, u32[]{:S(2)}) collective-permute-start(bf16[2,512,128]{2,1,0:T(8,128)(2,1)S(1)} %collective-permute-done.4.w2), channel_id=1, source_target_pairs={{0,1},{1,0},{2,3},{3,2},{4,5},{5,4},{6,7},{7,6},{8,9},{9,8},{10,11... | collective-permute-start | bytes 786440 | tf_op jit(solution)/shard_map/ppermute | solution.py:274
  67.5 5.4 %shard_map.109 = bf16[2560,128]{1,0:T(8,128)(2,1)} custom-call(s32[1]{0:T(128)} %bitcast.c_ref, bf16[5,512,128]{2,1,0:T(8,128)(2,1)S(1)} %copy-done, bf16[5,512,128]{2,1,0:T(8,128)(2,1)S(1)} %collective-permute-done.g1, bf16[5,512,128]{2,1,0:T(8,128)(2,1)S(1)} %collective-permute-done.1.g2, bf16[5,512,128]{2,1,0:T(8,128)(2,1)} %collective-permute-done.2.g3, ...), custom_call_target="tpu_custom_call" | custom-call | tf_op jit(solution)/shard_map/pallas_call | solution.py:297
  72.8 17.4 %all-to-all-start = ((bf16[640,4,128]{2,1,0:T(4,128)(2,1)}), bf16[640,4,128]{2,1,0:T(4,128)(2,1)S(1)}, u32[]{:S(2)}, u32[]{:S(2)}) async-start(bf16[640,4,128]{2,1,0:T(4,128)(2,1)} %bitcast.3), calls=%async_computation | async-start | bytes 1310720 | tf_op jit(solution)/shard_map/all_to_all | solution.py:270
  91.6 2.4 %shard_map.111 = (bf16[640,640]{1,0:T(8,128)(2,1)S(1)}, bf16[640,640]{1,0:T(8,128)(2,1)S(1)}) custom-call(s32[640,1]{1,0:T(8,128)S(1)} %reshape.65.pair_col, s32[1,640]{1,0:T(1,128)S(1)} %reshape.61.pair_row, s32[640,1]{1,0:T(8,128)S(1)} %reshape.66.partner_col, bf16[576,576]{1,0:T(8,128)(2,1)S(1)} %copy-done.7), custom_call_target="tpu_custom_call" | custom-call | tf_op jit(solution)/shard_map/pallas_call | solution.py:288
  97.2 1.9 %collective-permute-start.6 = (bf16[640,128]{1,0:T(8,128)(2,1)S(1)}, bf16[640,128]{1,0:T(8,128)(2,1)S(1)}, u32[]{:S(2)}, u32[]{:S(2)}) collective-permute-start(bf16[640,128]{1,0:T(8,128)(2,1)S(1)} %get-tuple-element.16), channel_id=1, source_target_pairs={{0,1},{1,0},{2,3},{3,2},{4,5},{5,4},{6,7},{7,6},{8,9},{9,8},{10,11... | collective-permute-start | bytes 491528 | tf_op jit(solution)/shard_map/ppermute | solution.py:274
  99.1 2.6 %collective-permute-start.7 = (bf16[640,128]{1,0:T(8,128)(2,1)S(1)}, bf16[640,128]{1,0:T(8,128)(2,1)S(1)}, u32[]{:S(2)}, u32[]{:S(2)}) collective-permute-start(bf16[640,128]{1,0:T(8,128)(2,1)S(1)} %get-tuple-element.17), channel_id=1, source_target_pairs={{0,2},{1,3},{2,0},{3,1},{4,6},{5,7},{6,4},{7,5},{8,10},{9,11},{10,... | collective-permute-start | bytes 491528 | tf_op jit(solution)/shard_map/ppermute | solution.py:274
  101.7 4.6 %collective-permute-start.8 = (bf16[640,128]{1,0:T(8,128)(2,1)S(1)}, bf16[640,128]{1,0:T(8,128)(2,1)S(1)}, u32[]{:S(2)}, u32[]{:S(2)}) collective-permute-start(bf16[640,128]{1,0:T(8,128)(2,1)S(1)} %get-tuple-element.18), channel_id=1, source_target_pairs={{0,3},{1,2},{2,1},{3,0},{4,7},{5,6},{6,5},{7,4},{8,11},{9,10},{10,... | collective-permute-start | bytes 491528 | tf_op jit(solution)/shard_map/ppermute | solution.py:274
  106.3 4.4 %collective-permute-done.7.m2 = bf16[640,128]{1,0:T(8,128)(2,1)S(1)} collective-permute-done((bf16[640,128]{1,0:T(8,128)(2,1)S(1)}, bf16[640,128]{1,0:T(8,128)(2,1)S(1)}, u32[]{:S(2)}, u32[]{:S(2)}) %collective-permute-start.7) | collective-permute-done | bytes 163872 | tf_op jit(solution)/shard_map/ppermute | solution.py:274
  110.7 3.2 %collective-permute-done.8.m3 = bf16[640,128]{1,0:T(8,128)(2,1)S(1)} collective-permute-done((bf16[640,128]{1,0:T(8,128)(2,1)S(1)}, bf16[640,128]{1,0:T(8,128)(2,1)S(1)}, u32[]{:S(2)}, u32[]{:S(2)}) %collective-permute-start.8) | collective-permute-done | bytes 163872 | tf_op jit(solution)/shard_map/ppermute | solution.py:274
  114.0 15.5 %all-to-all-done = bf16[640,4,128]{2,1,0:T(4,128)(2,1)S(1)} async-done(((bf16[640,4,128]{2,1,0:T(4,128)(2,1)}), bf16[640,4,128]{2,1,0:T(4,128)(2,1)S(1)}, u32[]{:S(2)}, u32[]{:S(2)}) %all-to-all-start) | async-done | bytes 655392 | tf_op jit(solution)/shard_map/all_to_all | solution.py:270
  129.4 3.0 %shard_map.113 = bf16[2560,128]{1,0:T(8,128)(2,1)} custom-call(s32[1]{0:T(128)} %bitcast.c_ref, bf16[2560,128]{1,0:T(8,128)(2,1)S(1)} %bitcast.11, bf16[640,512]{1,0:T(8,128)(2,1)} %copy-done.8, bf16[640,128]{1,0:T(8,128)(2,1)} %copy-done.9, bf16[640,128]{1,0:T(8,128)(2,1)} %copy-done.10, bf16[640,128]{1,0:T(8,128)(2,1)} %copy-done.11, ...), custom_call_target="tpu_custom_call" | custom-call | tf_op jit(solution)/shard_map/pallas_call | solution.py:330
  132.5 7.1 %all-to-all-start.2 = ((bf16[640,4,128]{2,1,0:T(4,128)(2,1)}), bf16[640,4,128]{2,1,0:T(4,128)(2,1)S(1)}, u32[]{:S(2)}, u32[]{:S(2)}) async-start(bf16[640,4,128]{2,1,0:T(4,128)(2,1)} %bitcast.8), calls=%async_computation.2 | async-start | bytes 1310720 | tf_op jit(solution)/shard_map/all_to_all | solution.py:270
  143.6 3.7 %shard_map.114.p_ref = bf16[5,512,128]{2,1,0:T(8,128)(2,1)S(1)} custom-call(s32[1]{0:T(128)} %bitcast.c_ref, bf16[5,512,128]{2,1,0:T(8,128)(2,1)S(1)} %copy-done, bf16[5,512,128]{2,1,0:T(8,128)(2,1)S(1)} %copy-done.2, bf16[5,512,128]{2,1,0:T(8,128)(2,1)S(1)} %collective-permute-done.1.g2, bf16[5,512,128]{2,1,0:T(8,128)(2,1)} %collective-permute-done.2.g3, ...), custom_call_target="tpu_custom_call" | custom-call | tf_op jit(solution)/shard_map/pallas_call | solution.py:313
  147.3 31.0 %all-to-all-done.2 = bf16[640,4,128]{2,1,0:T(4,128)(2,1)S(1)} async-done(((bf16[640,4,128]{2,1,0:T(4,128)(2,1)}), bf16[640,4,128]{2,1,0:T(4,128)(2,1)S(1)}, u32[]{:S(2)}, u32[]{:S(2)}) %all-to-all-start.2) | async-done | bytes 655392 | tf_op jit(solution)/shard_map/all_to_all | solution.py:270
  178.4 2.6 %shard_map.115 = f32[5,512,128]{2,1,0:T(8,128)} custom-call(f32[5]{0:T(128)S(1)} %compare_select_fusion.occ_ref, bf16[2560,128]{1,0:T(8,128)(2,1)S(1)} %bitcast.12, bf16[5,512,128]{2,1,0:T(8,128)(2,1)S(1)} %shard_map.114.p_ref, f32[512,128]{1,0:T(8,128)S(1)} %broadcast_add_fusion.base_ref), custom_call_target="tpu_custom_call" | custom-call | tf_op jit(solution)/shard_map/pallas_call | solution.py:357
  (57 shorter events, 12.5 us)
Async XLA Ops:
  0.0 23.6 %copy-start = (bf16[5,512,128]{2,1,0:T(8,128)(2,1)S(1)}, bf16[5,512,128]{2,1,0:T(8,128)(2,1)}, u32[]{:S(2)}) copy-start(bf16[5,512,128]{2,1,0:T(8,128)(2,1)} %g0.3) | copy-start | bytes 1966084
  0.0 49.2 %copy-start.13 = (bf16[512,128]{1,0:T(8,128)(2,1)S(1)}, bf16[512,128]{1,0:T(8,128)(2,1)}, u32[]{:S(2)}) copy-start(bf16[512,128]{1,0:T(8,128)(2,1)} %param.15) | copy-start | bytes 393220
  0.0 49.2 %copy-start.14 = (bf16[512,128]{1,0:T(8,128)(2,1)S(1)}, bf16[512,128]{1,0:T(8,128)(2,1)}, u32[]{:S(2)}) copy-start(bf16[512,128]{1,0:T(8,128)(2,1)} %param.14) | copy-start | bytes 393220
  3.0 69.8 %all-to-all-start.1 = ((bf16[640,4,128]{2,1,0:T(4,128)(2,1)}), bf16[640,4,128]{2,1,0:T(4,128)(2,1)S(1)}, u32[]{:S(2)}, u32[]{:S(2)}) async-start(bf16[640,4,128]{2,1,0:T(4,128)(2,1)} %bitcast.6), calls=%async_computation.1 | async-start | bytes 1310720 | tf_op jit(solution)/shard_map/all_to_all | solution.py:270
  23.6 23.7 %collective-permute-start.1 = (bf16[5,512,128]{2,1,0:T(8,128)(2,1)S(1)}, bf16[5,512,128]{2,1,0:T(8,128)(2,1)S(1)}, u32[]{:S(2)}, u32[]{:S(2)}) collective-permute-start(bf16[5,512,128]{2,1,0:T(8,128)(2,1)S(1)} %copy-done), channel_id=1, source_target_pairs={{0,2},{1,3},{2,0},{3,1},{4,6},{5,7},{6,4},{7,5},{8,10},{9,11},{10,... | collective-permute-start | bytes 1966088 | tf_op jit(solution)/shard_map/ppermute | solution.py:274
  26.1 39.0 %collective-permute-start = (bf16[5,512,128]{2,1,0:T(8,128)(2,1)S(1)}, bf16[5,512,128]{2,1,0:T(8,128)(2,1)S(1)}, u32[]{:S(2)}, u32[]{:S(2)}) collective-permute-start(bf16[5,512,128]{2,1,0:T(8,128)(2,1)S(1)} %copy-done), channel_id=1, source_target_pairs={{0,1},{1,0},{2,3},{3,2},{4,5},{5,4},{6,7},{7,6},{8,9},{9,8},{10,11... | collective-permute-start | bytes 1966088 | tf_op jit(solution)/shard_map/ppermute | solution.py:274
  47.3 17.8 %collective-permute-start.2 = (bf16[5,512,128]{2,1,0:T(8,128)(2,1)S(1)}, bf16[5,512,128]{2,1,0:T(8,128)(2,1)}, u32[]{:S(2)}, u32[]{:S(2)}) collective-permute-start(bf16[5,512,128]{2,1,0:T(8,128)(2,1)S(1)} %collective-permute-done.1.g2), channel_id=1, source_target_pairs={{0,1},{1,0},{2,3},{3,2},{4,5},{5,4},{6,7},{7,6},{8,9},{9,8},{10,11... | collective-permute-start | bytes 1966088 | tf_op jit(solution)/shard_map/ppermute | solution.py:274
  49.3 12.3 %collective-permute-start.4 = (bf16[2,512,128]{2,1,0:T(8,128)(2,1)S(1)}, bf16[2,512,128]{2,1,0:T(8,128)(2,1)S(1)}, u32[]{:S(2)}, u32[]{:S(2)}) collective-permute-start(bf16[2,512,128]{2,1,0:T(8,128)(2,1)S(1)} %pad_maximum_fusion.w0), channel_id=1, source_target_pairs={{0,2},{1,3},{2,0},{3,1},{4,6},{5,7},{6,4},{7,5},{8,10},{9,11},{10,... | collective-permute-start | bytes 786440 | tf_op jit(solution)/shard_map/ppermute | solution.py:274
  51.9 11.6 %collective-permute-start.3 = (bf16[2,512,128]{2,1,0:T(8,128)(2,1)S(1)}, bf16[2,512,128]{2,1,0:T(8,128)(2,1)S(1)}, u32[]{:S(2)}, u32[]{:S(2)}) collective-permute-start(bf16[2,512,128]{2,1,0:T(8,128)(2,1)S(1)} %pad_maximum_fusion.w0), channel_id=1, source_target_pairs={{0,1},{1,0},{2,3},{3,2},{4,5},{5,4},{6,7},{7,6},{8,9},{9,8},{10,11... | collective-permute-start | bytes 786440 | tf_op jit(solution)/shard_map/ppermute | solution.py:274
  61.6 3.6 %collective-permute-start.5 = (bf16[2,512,128]{2,1,0:T(8,128)(2,1)S(1)}, bf16[2,512,128]{2,1,0:T(8,128)(2,1)}, u32[]{:S(2)}, u32[]{:S(2)}) collective-permute-start(bf16[2,512,128]{2,1,0:T(8,128)(2,1)S(1)} %collective-permute-done.4.w2), channel_id=1, source_target_pairs={{0,1},{1,0},{2,3},{3,2},{4,5},{5,4},{6,7},{7,6},{8,9},{9,8},{10,11... | collective-permute-start | bytes 786440 | tf_op jit(solution)/shard_map/ppermute | solution.py:274
  65.1 7.7 %copy-start.1 = (bf16[5,512,128]{2,1,0:T(8,128)(2,1)}, bf16[5,512,128]{2,1,0:T(8,128)(2,1)S(1)}, u32[]{:S(2)}) copy-start(bf16[5,512,128]{2,1,0:T(8,128)(2,1)S(1)} %collective-permute-done.g1) | copy-start | bytes 1966084
  72.8 17.4 %copy-start.15 = (s32[640]{0:T(1024)S(1)}, s32[640]{0:T(1024)}, u32[]{:S(2)}) copy-start(s32[640]{0:T(1024)} %param.17) | copy-start | bytes 7684
  72.8 17.6 %copy-start.16 = (s32[640]{0:T(1024)S(1)}, s32[640]{0:T(1024)}, u32[]{:S(2)}) copy-start(s32[640]{0:T(1024)} %param.18) | copy-start | bytes 7684
  72.8 56.6 %all-to-all-start = ((bf16[640,4,128]{2,1,0:T(4,128)(2,1)}), bf16[640,4,128]{2,1,0:T(4,128)(2,1)S(1)}, u32[]{:S(2)}, u32[]{:S(2)}) async-start(bf16[640,4,128]{2,1,0:T(4,128)(2,1)} %bitcast.3), calls=%async_computation | async-start | bytes 1310720 | tf_op jit(solution)/shard_map/all_to_all | solution.py:270
  97.2 9.1 %collective-permute-start.6 = (bf16[640,128]{1,0:T(8,128)(2,1)S(1)}, bf16[640,128]{1,0:T(8,128)(2,1)S(1)}, u32[]{:S(2)}, u32[]{:S(2)}) collective-permute-start(bf16[640,128]{1,0:T(8,128)(2,1)S(1)} %get-tuple-element.16), channel_id=1, source_target_pairs={{0,1},{1,0},{2,3},{3,2},{4,5},{5,4},{6,7},{7,6},{8,9},{9,8},{10,11... | collective-permute-start | bytes 491528 | tf_op jit(solution)/shard_map/ppermute | solution.py:274
  99.1 11.6 %collective-permute-start.7 = (bf16[640,128]{1,0:T(8,128)(2,1)S(1)}, bf16[640,128]{1,0:T(8,128)(2,1)S(1)}, u32[]{:S(2)}, u32[]{:S(2)}) collective-permute-start(bf16[640,128]{1,0:T(8,128)(2,1)S(1)} %get-tuple-element.17), channel_id=1, source_target_pairs={{0,2},{1,3},{2,0},{3,1},{4,6},{5,7},{6,4},{7,5},{8,10},{9,11},{10,... | collective-permute-start | bytes 491528 | tf_op jit(solution)/shard_map/ppermute | solution.py:274
  101.7 12.3 %collective-permute-start.8 = (bf16[640,128]{1,0:T(8,128)(2,1)S(1)}, bf16[640,128]{1,0:T(8,128)(2,1)S(1)}, u32[]{:S(2)}, u32[]{:S(2)}) collective-permute-start(bf16[640,128]{1,0:T(8,128)(2,1)S(1)} %get-tuple-element.18), channel_id=1, source_target_pairs={{0,3},{1,2},{2,1},{3,0},{4,7},{5,6},{6,5},{7,4},{8,11},{9,10},{10,... | collective-permute-start | bytes 491528 | tf_op jit(solution)/shard_map/ppermute | solution.py:274
  106.3 23.1 %copy-start.10 = (bf16[640,128]{1,0:T(8,128)(2,1)}, bf16[640,128]{1,0:T(8,128)(2,1)S(1)}, u32[]{:S(2)}) copy-start(bf16[640,128]{1,0:T(8,128)(2,1)S(1)} %collective-permute-done.6.m1) | copy-start | bytes 491524
  110.7 18.7 %copy-start.11 = (bf16[640,128]{1,0:T(8,128)(2,1)}, bf16[640,128]{1,0:T(8,128)(2,1)S(1)}, u32[]{:S(2)}) copy-start(bf16[640,128]{1,0:T(8,128)(2,1)S(1)} %collective-permute-done.7.m2) | copy-start | bytes 491524
  114.0 15.5 %copy-start.12 = (bf16[640,128]{1,0:T(8,128)(2,1)}, bf16[640,128]{1,0:T(8,128)(2,1)S(1)}, u32[]{:S(2)}) copy-start(bf16[640,128]{1,0:T(8,128)(2,1)S(1)} %collective-permute-done.8.m3) | copy-start | bytes 491524
  132.5 7.1 %copy-start.17 = (f32[512]{0:T(512)S(1)}, f32[512]{0:T(512)}, u32[]{:S(2)}) copy-start(f32[512]{0:T(512)} %param.20) | copy-start | bytes 6148
  132.5 7.1 %copy-start.18 = (s32[512]{0:T(512)S(1)}, s32[512]{0:T(512)}, u32[]{:S(2)}) copy-start(s32[512]{0:T(512)} %param.21) | copy-start | bytes 6148
  132.5 7.5 %copy-start.19 = (f32[24]{0:T(128)S(1)}, f32[24]{0:T(128)}, u32[]{:S(2)}) copy-start(f32[24]{0:T(128)} %param.19) | copy-start | bytes 292
  132.5 45.9 %all-to-all-start.2 = ((bf16[640,4,128]{2,1,0:T(4,128)(2,1)}), bf16[640,4,128]{2,1,0:T(4,128)(2,1)S(1)}, u32[]{:S(2)}, u32[]{:S(2)}) async-start(bf16[640,4,128]{2,1,0:T(4,128)(2,1)} %bitcast.8), calls=%async_computation.2 | async-start | bytes 1310720 | tf_op jit(solution)/shard_map/all_to_all | solution.py:270
  (8 other events, 8.1 us)

commit v4 on v3

--- a/solution.py
+++ b/solution.py
@@ -63,17 +63,13 @@
         done(start, size)
 
 
-def skew_kernel(a_hbm, out_ref, raw, sems, flat, middle, target):
-    nslot, nvirt, nb = raw.shape
+def skew_kernel(a_ref, out_ref, flat, middle, target):
+    nslot, nvirt, nb = a_ref.shape
     ncol = nvirt // nb
-    copies = [pltpu.make_async_copy(a_hbm.at[s], raw.at[s], sems.at[s]) for s in range(nslot)]
-    for copy in copies:
-        copy.start()
 
     def ready(start, size):
         for s in range(start // ncol, (start + size) // ncol):
-            copies[s].wait()
-            flat[s * nvirt : (s + 1) * nvirt, :] = raw[s].astype(F32)
+            flat[s * nvirt : (s + 1) * nvirt, :] = a_ref[s].astype(F32)
 
     skew(flat, middle, target, nb, nslot * ncol, ready)
     out_ref[...] = target[...].astype(BF16)
@@ -108,7 +104,7 @@
 
 def rows_kernel(
     c_ref, g0, g1, g2, g3, w0, w1, w2, w3, fl_ref, dl_ref, out_ref,
-    left, right, acat, low, flat, middle, target,
+    left, dmat, fmat, stack, low, flat, middle, target,
 ):
     parts = (g0, g1, g2, g3)
     wide = (w0, w1, w2, w3)
@@ -116,22 +112,22 @@
     nslot, nvirt, nb = g0.shape
     col = c_ref[0]
     own = pl.ds(pl.multiple_of(col * nb, nb), nb)
-    left[:nb, :] = fl_ref[own, :]
-    left[nb:, :] = dl_ref[own, :]
+    left[:, :nvirt] = fl_ref[own, :]
+    left[:, nvirt:] = dl_ref[own, :]
     for i in range(ncol):
         rows = pl.ds(pl.multiple_of((col ^ i) * nb, nb), nb)
         for k in range(ncol):
-            right[i * nb : (i + 1) * nb, k * nb : (k + 1) * nb] = wide[k][1, rows, :]
-            right[nvirt + i * nb : nvirt + (i + 1) * nb, k * nb : (k + 1) * nb] = wide[k][0, rows, :]
+            at = (slice(i * nb, (i + 1) * nb), slice(k * nb, (k + 1) * nb))
+            fmat[at] = wide[k][0, rows, :]
+            dmat[at] = wide[k][1, rows, :]
 
     def ready(start, size):
         for s in range(start // ncol, (start + size) // ncol):
-            amp = gather_columns(parts, s, acat)
-            first = dot(left[...], amp)
-            low[:, :nvirt] = first[nb:].astype(BF16)
             for k, part in enumerate(parts):
-                low[:, nvirt + k * nb : nvirt + (k + 1) * nb] = part[s, own, :]
-            total = first[:nb] + dot(low[...], right[...])
+                stack[:nvirt, k * nb : (k + 1) * nb] = part[s]
+                low[:, k * nb : (k + 1) * nb] = part[s, own, :]
+            stack[nvirt:, :] = dot(stack[:nvirt, :], dmat[...]).astype(BF16)
+            total = dot(left[...], stack[...]) + dot(low[...], fmat[...])
             for k in range(ncol):
                 at = pl.multiple_of((s * ncol + (col ^ k)) * nb, nb)
                 flat[pl.ds(at, nb), :] = total[:, k * nb : (k + 1) * nb].T
@@ -164,7 +160,9 @@
     wide[...] = x_ref[...].astype(F32)
     for d in range(ncol):
         xcat[:, d * nb : (d + 1) * nb] = wide[pl.ds(d, slots, stride=ncol), :].astype(BF16)
-    l_ref[...] = dot(w_ref[...], xcat[...]).astype(BF16)
+    plain = dot(w_ref[...], xcat[...])
+    for d in range(ncol):
+        l_ref[d] = plain[:, d * nb : (d + 1) * nb].astype(BF16)
     other = dot(w2_ref[...], xcat[...]).astype(BF16)
     rows = lax.broadcasted_iota(jnp.int32, (nb, nb), 0)
     cols = lax.broadcasted_iota(jnp.int32, (nb, nb), 1)
@@ -176,16 +174,15 @@
         out[...] = mirror[col ^ k]
 
 
-def combine_kernel(
-    c_ref, y_ref, l_hbm, m0, m1, m2, m3, partner_col, out_ref, wide, ycat, mirror, l_ref, sems
-):
-    slots = l_ref.shape[0]
-    nb = y_ref.shape[1]
-    ncol = y_ref.shape[0] // slots
+def mirror_kernel(c_ref, l_ref, m0, m1, m2, m3, out_ref):
     col = c_ref[0]
-    copies = [pltpu.make_async_copy(l_hbm, l_ref, sems.at[ncol])]
     for k, part in enumerate((m0, m1, m2, m3)):
-        copies.append(pltpu.make_async_copy(part, mirror.at[col ^ k], sems.at[k]))
+        out_ref[col ^ k] = (l_ref[col ^ k].astype(F32) + part[...].astype(F32)).astype(BF16)
+
+
+def combine_kernel(y_ref, s_hbm, partner_col, out_ref, wide, ycat, both, sems):
+    ncol, slots, nb = both.shape
+    copies = [pltpu.make_async_copy(s_hbm.at[d], both.at[d], sems.at[d]) for d in range(ncol)]
     for copy in copies:
         copy.start()
     wide[...] = y_ref[...].astype(F32)
@@ -193,12 +190,10 @@
         ycat[:, d * nb : (d + 1) * nb] = wide[pl.ds(d, slots, stride=ncol), :].astype(BF16)
     pick = (partner_col[...] == lax.broadcasted_iota(jnp.int32, (slots, slots), 1)).astype(BF16)
     total = dot(pick, ycat[...])
-    for copy in copies:
-        copy.wait()
-    for d in range(ncol):
-        at = slice(d * nb, (d + 1) * nb)
+    for d in range(ncol):
+        copies[d].wait()
         wide[pl.ds(d, slots, stride=ncol), :] = (
-            total[:, at] + l_ref[:, at].astype(F32) + mirror[d].astype(F32)
+            total[:, d * nb : (d + 1) * nb] + both[d].astype(F32)
         )
     out_ref[...] = wide[...].astype(BF16)
 
@@ -276,11 +271,8 @@
     far = swap(amplitudes, 2)
     dma = pltpu.SemaphoreType.DMA
     skewed = call(
-        skew_kernel,
-        shape((nb * count, nb), BF16),
-        [pltpu.VMEM(amplitudes.shape, BF16), dma((slot_dev,))] + skew_scratch(count, nb),
-        [HBM],
-    )(stay(amplitudes))
+        skew_kernel, shape((nb * count, nb), BF16), skew_scratch(count, nb), [VMEM]
+    )(amplitudes)
     x = exchange(skewed)
     pair_col = slot_pair.reshape(slots, 1)
     pair_row = slot_pair.reshape(1, slots)
@@ -298,10 +290,11 @@
         rows_kernel,
         shape((nb * count, nb), BF16),
         [
-            pltpu.VMEM((2 * nb, nvirt), BF16),
+            pltpu.VMEM((nb, 2 * nvirt), BF16),
+            pltpu.VMEM((nvirt, nvirt), BF16),
+            pltpu.VMEM((nvirt, nvirt), BF16),
             pltpu.VMEM((2 * nvirt, nvirt), BF16),
-            pltpu.VMEM((nvirt, nvirt), BF16),
-            pltpu.VMEM((nb, 2 * nvirt), BF16),
+            pltpu.VMEM((nb, nvirt), BF16),
         ]
         + skew_scratch(count, nb),
         [SMEM] + [VMEM] * 10,
@@ -318,7 +311,7 @@
     )(col_s, amplitudes, near, far, both, wide, fock_left, dress_left)
     ladder, m0, m1, m2, m3 = call(
         ladder_kernel,
-        [shape((slots, nvirt), BF16)] + [shape((slots, nb), BF16)] * 4,
+        [shape((ncol, slots, nb), BF16)] + [shape((slots, nb), BF16)] * 4,
         [
             pltpu.VMEM((slots * ncol, nb), F32),
             pltpu.VMEM((slots, nvirt), BF16),
@@ -327,6 +320,9 @@
         [SMEM] * 2 + [VMEM] * 3,
     )(col_s, pair_s, x, w, w2)
     m1, m2, m3 = swap(m1, 1), swap(m2, 2), swap(m3, 3)
+    both_terms = call(
+        mirror_kernel, shape((ncol, slots, nb), BF16), [], [SMEM] + [VMEM] * 5
+    )(col_s, ladder, m0, m1, m2, m3)
     back = call(
         combine_kernel,
         shape((nb * count, nb), BF16),
@@ -334,11 +330,10 @@
             pltpu.VMEM((slots * ncol, nb), F32),
             pltpu.VMEM((slots, nvirt), BF16),
             pltpu.VMEM((ncol, slots, nb), BF16),
-            pltpu.VMEM((slots, nvirt), BF16),
-            dma((ncol + 1,)),
+            dma((ncol,)),
         ],
-        [SMEM, VMEM] + [HBM] * 5 + [VMEM],
-    )(col_s, y, stay(ladder), stay(m0), stay(m1), stay(m2), stay(m3), partner_col)
+        [VMEM, HBM, VMEM],
+    )(y, stay(both_terms), partner_col)
     z = exchange(back)
     own_pairs = lax.dynamic_slice_in_dim(slot_pair, pair * slot_dev, slot_dev)
     occ_iota = jnp.arange(nocc, dtype=jnp.int32)

time: 182 us -> 182 us (level)
    pallas_call x3 -> x4, Pallas kernels: 9.95 us -> 9.44 us  [the longest x1 5.76 us: update_of(): call(rows_kernel, shape((nb * count, nb), BF16), [pltpu.VMEM((nb, 2 * nvi...]
    unnamed x40 -> x34, local copies, waits for them, and re-layouts: 8.16 us -> 8.57 us
  transfers between devices with their start and end apart: 12 -> 12, of which waited for: 7 -> 7; matrix products, arithmetic and copies ran while one was open for 1% -> 1% of each run, Pallas kernels for 7% -> 8%
where the time goes in v4:
time: 182 us; the launch traced here: 181 us
  waiting for transfers between devices  83.1 us (46%)
  starting transfers between devices  66.9 us (37%)
  Pallas kernels  20.8 us (11%)
  local copies, waits for them, and re-layouts  8.93 us (5%)
    all_to_all x3, waiting for transfers between devices, exchange(): got = lax.all_to_all(sent, 'pair', split_axis=0, concat_axis=0, tiled=True)  46.8 us
    all_to_all x3, starting transfers between devices, exchange(): got = lax.all_to_all(sent, 'pair', split_axis=0, concat_axis=0, tiled=True)  44.8 us
    ppermute x9, waiting for transfers between devices, swap(): return lax.ppermute(value, 'col', [(i, i ^ k) for i in range(ncol)])  36.3 us
    ppermute x9, starting transfers between devices, swap(): return lax.ppermute(value, 'col', [(i, i ^ k) for i in range(ncol)])  22.1 us
    unnamed x34, local copies, waits for them, and re-layouts  8.57 us
    pallas_call x1, Pallas kernels, update_of(): call(rows_kernel, shape((nb * count, nb), BF16), [pltpu.VMEM((nb, 2 * nvi...  5.76 us
    pallas_call x1, Pallas kernels, update_of(): call(cols_kernel, shape(amplitudes.shape, BF16), [pltpu.VMEM((nvirt, 2 *...  3.71 us
  transfers between devices with their start and end apart: 12, of which 7 were waited for; matrix products, arithmetic and copies ran while one was open for 1% of the time, Pallas kernels for 8%

profile of v4, /device:TPU:16, one launch (start us, length us, event | category | flops | bytes accessed | tf_op | source)
XLA Modules:
  0.0 181.0 jit_solution(11030560461145379432)
XLA Ops:
  1.1 2.0 %shard_map.110 = bf16[2560,128]{1,0:T(8,128)(2,1)} custom-call(bf16[5,512,128]{2,1,0:T(8,128)(2,1)S(1)} %copy-done), custom_call_target="tpu_custom_call" | custom-call | tf_op jit(solution)/shard_map/pallas_call | solution.py:273
  3.1 20.5 %all-to-all-start.1 = ((bf16[640,4,128]{2,1,0:T(4,128)(2,1)}), bf16[640,4,128]{2,1,0:T(4,128)(2,1)S(1)}, u32[]{:S(2)}, u32[]{:S(2)}) async-start(bf16[640,4,128]{2,1,0:T(4,128)(2,1)} %bitcast.6), calls=%async_computation.1 | async-start | bytes 1310720 | tf_op jit(solution)/shard_map/all_to_all | solution.py:265
  23.6 2.5 %collective-permute-start.1 = (bf16[5,512,128]{2,1,0:T(8,128)(2,1)S(1)}, bf16[5,512,128]{2,1,0:T(8,128)(2,1)S(1)}, u32[]{:S(2)}, u32[]{:S(2)}) collective-permute-start(bf16[5,512,128]{2,1,0:T(8,128)(2,1)S(1)} %copy-done.1), channel_id=1, source_target_pairs={{0,2},{1,3},{2,0},{3,1},{4,6},{5,7},{6,4},{7,5},{8,10},{9,11},{10,... | collective-permute-start | bytes 1966088 | tf_op jit(solution)/shard_map/ppermute | solution.py:269
  26.1 1.9 %collective-permute-start = (bf16[5,512,128]{2,1,0:T(8,128)(2,1)S(1)}, bf16[5,512,128]{2,1,0:T(8,128)(2,1)S(1)}, u32[]{:S(2)}, u32[]{:S(2)}) collective-permute-start(bf16[5,512,128]{2,1,0:T(8,128)(2,1)S(1)} %copy-done.1), channel_id=1, source_target_pairs={{0,1},{1,0},{2,3},{3,2},{4,5},{5,4},{6,7},{7,6},{8,9},{9,8},{10,11... | collective-permute-start | bytes 1966088 | tf_op jit(solution)/shard_map/ppermute | solution.py:269
  28.0 19.3 %collective-permute-done.1.g2 = bf16[5,512,128]{2,1,0:T(8,128)(2,1)S(1)} collective-permute-done((bf16[5,512,128]{2,1,0:T(8,128)(2,1)S(1)}, bf16[5,512,128]{2,1,0:T(8,128)(2,1)S(1)}, u32[]{:S(2)}, u32[]{:S(2)}) %collective-permute-start.1) | collective-permute-done | bytes 655392 | tf_op jit(solution)/shard_map/ppermute | solution.py:269
  47.3 1.9 %collective-permute-start.2 = (bf16[5,512,128]{2,1,0:T(8,128)(2,1)S(1)}, bf16[5,512,128]{2,1,0:T(8,128)(2,1)}, u32[]{:S(2)}, u32[]{:S(2)}) collective-permute-start(bf16[5,512,128]{2,1,0:T(8,128)(2,1)S(1)} %collective-permute-done.1.g2), channel_id=1, source_target_pairs={{0,1},{1,0},{2,3},{3,2},{4,5},{5,4},{6,7},{7,6},{8,9},{9,8},{10,11... | collective-permute-start | bytes 1966088 | tf_op jit(solution)/shard_map/ppermute | solution.py:269
  49.3 2.6 %collective-permute-start.4 = (bf16[2,512,128]{2,1,0:T(8,128)(2,1)S(1)}, bf16[2,512,128]{2,1,0:T(8,128)(2,1)S(1)}, u32[]{:S(2)}, u32[]{:S(2)}) collective-permute-start(bf16[2,512,128]{2,1,0:T(8,128)(2,1)S(1)} %pad_maximum_fusion.w0), channel_id=1, source_target_pairs={{0,2},{1,3},{2,0},{3,1},{4,6},{5,7},{6,4},{7,5},{8,10},{9,11},{10,... | collective-permute-start | bytes 786440 | tf_op jit(solution)/shard_map/ppermute | solution.py:269
  51.9 2.1 %collective-permute-start.3 = (bf16[2,512,128]{2,1,0:T(8,128)(2,1)S(1)}, bf16[2,512,128]{2,1,0:T(8,128)(2,1)S(1)}, u32[]{:S(2)}, u32[]{:S(2)}) collective-permute-start(bf16[2,512,128]{2,1,0:T(8,128)(2,1)S(1)} %pad_maximum_fusion.w0), channel_id=1, source_target_pairs={{0,1},{1,0},{2,3},{3,2},{4,5},{5,4},{6,7},{7,6},{8,9},{9,8},{10,11... | collective-permute-start | bytes 786440 | tf_op jit(solution)/shard_map/ppermute | solution.py:269
  54.0 7.5 %collective-permute-done.4.w2 = bf16[2,512,128]{2,1,0:T(8,128)(2,1)S(1)} collective-permute-done((bf16[2,512,128]{2,1,0:T(8,128)(2,1)S(1)}, bf16[2,512,128]{2,1,0:T(8,128)(2,1)S(1)}, u32[]{:S(2)}, u32[]{:S(2)}) %collective-permute-start.4) | collective-permute-done | bytes 262176 | tf_op jit(solution)/shard_map/ppermute | solution.py:269
  61.6 1.9 %collective-permute-start.5 = (bf16[2,512,128]{2,1,0:T(8,128)(2,1)S(1)}, bf16[2,512,128]{2,1,0:T(8,128)(2,1)}, u32[]{:S(2)}, u32[]{:S(2)}) collective-permute-start(bf16[2,512,128]{2,1,0:T(8,128)(2,1)S(1)} %collective-permute-done.4.w2), channel_id=1, source_target_pairs={{0,1},{1,0},{2,3},{3,2},{4,5},{5,4},{6,7},{7,6},{8,9},{9,8},{10,11... | collective-permute-start | bytes 786440 | tf_op jit(solution)/shard_map/ppermute | solution.py:269
  67.4 5.8 %shard_map.109 = bf16[2560,128]{1,0:T(8,128)(2,1)} custom-call(s32[1]{0:T(128)} %bitcast.c_ref, bf16[5,512,128]{2,1,0:T(8,128)(2,1)S(1)} %copy-done.1, bf16[5,512,128]{2,1,0:T(8,128)(2,1)S(1)} %collective-permute-done.g1, bf16[5,512,128]{2,1,0:T(8,128)(2,1)S(1)} %collective-permute-done.1.g2, bf16[5,512,128]{2,1,0:T(8,128)(2,1)} %collective-permute-done.2.g3, ...), custom_call_target="tpu_custom_call" | custom-call | tf_op jit(solution)/shard_map/pallas_call | solution.py:289
  73.2 17.3 %all-to-all-start = ((bf16[640,4,128]{2,1,0:T(4,128)(2,1)}), bf16[640,4,128]{2,1,0:T(4,128)(2,1)S(1)}, u32[]{:S(2)}, u32[]{:S(2)}) async-start(bf16[640,4,128]{2,1,0:T(4,128)(2,1)} %bitcast.3), calls=%async_computation | async-start | bytes 1310720 | tf_op jit(solution)/shard_map/all_to_all | solution.py:265
  92.0 2.4 %shard_map.111 = (bf16[640,640]{1,0:T(8,128)(2,1)S(1)}, bf16[640,640]{1,0:T(8,128)(2,1)S(1)}) custom-call(s32[640,1]{1,0:T(8,128)S(1)} %reshape.65.pair_col, s32[1,640]{1,0:T(1,128)S(1)} %reshape.61.pair_row, s32[640,1]{1,0:T(8,128)S(1)} %reshape.66.partner_col, bf16[576,576]{1,0:T(8,128)(2,1)S(1)} %copy-done.9), custom_call_target="tpu_custom_call" | custom-call | tf_op jit(solution)/shard_map/pallas_call | solution.py:280
  96.1 1.9 %collective-permute-start.6 = (bf16[640,128]{1,0:T(8,128)(2,1)S(1)}, bf16[640,128]{1,0:T(8,128)(2,1)S(1)}, u32[]{:S(2)}, u32[]{:S(2)}) collective-permute-start(bf16[640,128]{1,0:T(8,128)(2,1)S(1)} %get-tuple-element.16), channel_id=1, source_target_pairs={{0,1},{1,0},{2,3},{3,2},{4,5},{5,4},{6,7},{7,6},{8,9},{9,8},{10,11... | collective-permute-start | bytes 491528 | tf_op jit(solution)/shard_map/ppermute | solution.py:269
  98.0 2.6 %collective-permute-start.7 = (bf16[640,128]{1,0:T(8,128)(2,1)S(1)}, bf16[640,128]{1,0:T(8,128)(2,1)S(1)}, u32[]{:S(2)}, u32[]{:S(2)}) collective-permute-start(bf16[640,128]{1,0:T(8,128)(2,1)S(1)} %get-tuple-element.17), channel_id=1, source_target_pairs={{0,2},{1,3},{2,0},{3,1},{4,6},{5,7},{6,4},{7,5},{8,10},{9,11},{10,... | collective-permute-start | bytes 491528 | tf_op jit(solution)/shard_map/ppermute | solution.py:269
  100.6 4.6 %collective-permute-start.8 = (bf16[640,128]{1,0:T(8,128)(2,1)S(1)}, bf16[640,128]{1,0:T(8,128)(2,1)S(1)}, u32[]{:S(2)}, u32[]{:S(2)}) collective-permute-start(bf16[640,128]{1,0:T(8,128)(2,1)S(1)} %get-tuple-element.18), channel_id=1, source_target_pairs={{0,3},{1,2},{2,1},{3,0},{4,7},{5,6},{6,5},{7,4},{8,11},{9,10},{10,... | collective-permute-start | bytes 491528 | tf_op jit(solution)/shard_map/ppermute | solution.py:269
  105.2 4.5 %collective-permute-done.7.m2 = bf16[640,128]{1,0:T(8,128)(2,1)S(1)} collective-permute-done((bf16[640,128]{1,0:T(8,128)(2,1)S(1)}, bf16[640,128]{1,0:T(8,128)(2,1)S(1)}, u32[]{:S(2)}, u32[]{:S(2)}) %collective-permute-start.7) | collective-permute-done | bytes 163872 | tf_op jit(solution)/shard_map/ppermute | solution.py:269
  109.7 3.4 %collective-permute-done.8.m3 = bf16[640,128]{1,0:T(8,128)(2,1)S(1)} collective-permute-done((bf16[640,128]{1,0:T(8,128)(2,1)S(1)}, bf16[640,128]{1,0:T(8,128)(2,1)S(1)}, u32[]{:S(2)}, u32[]{:S(2)}) %collective-permute-start.8) | collective-permute-done | bytes 163872 | tf_op jit(solution)/shard_map/ppermute | solution.py:269
  114.1 15.7 %all-to-all-done = bf16[640,4,128]{2,1,0:T(4,128)(2,1)S(1)} async-done(((bf16[640,4,128]{2,1,0:T(4,128)(2,1)}), bf16[640,4,128]{2,1,0:T(4,128)(2,1)S(1)}, u32[]{:S(2)}, u32[]{:S(2)}) %all-to-all-start) | async-done | bytes 655392 | tf_op jit(solution)/shard_map/all_to_all | solution.py:265
  129.8 2.6 %shard_map.114 = bf16[2560,128]{1,0:T(8,128)(2,1)} custom-call(bf16[2560,128]{1,0:T(8,128)(2,1)S(1)} %bitcast.11, bf16[4,640,128]{2,1,0:T(8,128)(2,1)} %copy-done.2, s32[640,1]{1,0:T(8,128)S(1)} %reshape.66.partner_col), custom_call_target="tpu_custom_call" | custom-call | tf_op jit(solution)/shard_map/pallas_call | solution.py:326
  132.4 6.9 %all-to-all-start.2 = ((bf16[640,4,128]{2,1,0:T(4,128)(2,1)}), bf16[640,4,128]{2,1,0:T(4,128)(2,1)S(1)}, u32[]{:S(2)}, u32[]{:S(2)}) async-start(bf16[640,4,128]{2,1,0:T(4,128)(2,1)} %bitcast.8), calls=%async_computation.2 | async-start | bytes 1310720 | tf_op jit(solution)/shard_map/all_to_all | solution.py:265
  143.4 3.7 %shard_map.115.p_ref = bf16[5,512,128]{2,1,0:T(8,128)(2,1)S(1)} custom-call(s32[1]{0:T(128)} %bitcast.c_ref, bf16[5,512,128]{2,1,0:T(8,128)(2,1)S(1)} %copy-done.1, bf16[5,512,128]{2,1,0:T(8,128)(2,1)S(1)} %copy-done.4, bf16[5,512,128]{2,1,0:T(8,128)(2,1)S(1)} %collective-permute-done.1.g2, bf16[5,512,128]{2,1,0:T(8,128)(2,1)} %collective-permute-done.2.g3, ...), custom_call_target="tpu_custom_call" | custom-call | tf_op jit(solution)/shard_map/pallas_call | solution.py:306
  147.1 31.1 %all-to-all-done.2 = bf16[640,4,128]{2,1,0:T(4,128)(2,1)S(1)} async-done(((bf16[640,4,128]{2,1,0:T(4,128)(2,1)}), bf16[640,4,128]{2,1,0:T(4,128)(2,1)S(1)}, u32[]{:S(2)}, u32[]{:S(2)}) %all-to-all-start.2) | async-done | bytes 655392 | tf_op jit(solution)/shard_map/all_to_all | solution.py:265
  178.2 2.6 %shard_map.116 = f32[5,512,128]{2,1,0:T(8,128)} custom-call(f32[5]{0:T(128)S(1)} %compare_select_fusion.occ_ref, bf16[2560,128]{1,0:T(8,128)(2,1)S(1)} %bitcast.12, bf16[5,512,128]{2,1,0:T(8,128)(2,1)S(1)} %shard_map.115.p_ref, f32[512,128]{1,0:T(8,128)S(1)} %broadcast_add_fusion.base_ref), custom_call_target="tpu_custom_call" | custom-call | tf_op jit(solution)/shard_map/pallas_call | solution.py:352
  (52 shorter events, 13.1 us)
Async XLA Ops:
  1.1 22.5 %copy-start.1 = (bf16[5,512,128]{2,1,0:T(8,128)(2,1)S(1)}, bf16[5,512,128]{2,1,0:T(8,128)(2,1)}, u32[]{:S(2)}) copy-start(bf16[5,512,128]{2,1,0:T(8,128)(2,1)} %g0.3) | copy-start | bytes 1966084
  1.1 48.1 %copy-start.10 = (bf16[512,128]{1,0:T(8,128)(2,1)S(1)}, bf16[512,128]{1,0:T(8,128)(2,1)}, u32[]{:S(2)}) copy-start(bf16[512,128]{1,0:T(8,128)(2,1)} %param.15) | copy-start | bytes 393220
  1.1 48.2 %copy-start.11 = (bf16[512,128]{1,0:T(8,128)(2,1)S(1)}, bf16[512,128]{1,0:T(8,128)(2,1)}, u32[]{:S(2)}) copy-start(bf16[512,128]{1,0:T(8,128)(2,1)} %param.14) | copy-start | bytes 393220
  3.1 70.2 %all-to-all-start.1 = ((bf16[640,4,128]{2,1,0:T(4,128)(2,1)}), bf16[640,4,128]{2,1,0:T(4,128)(2,1)S(1)}, u32[]{:S(2)}, u32[]{:S(2)}) async-start(bf16[640,4,128]{2,1,0:T(4,128)(2,1)} %bitcast.6), calls=%async_computation.1 | async-start | bytes 1310720 | tf_op jit(solution)/shard_map/all_to_all | solution.py:265
  23.6 23.7 %collective-permute-start.1 = (bf16[5,512,128]{2,1,0:T(8,128)(2,1)S(1)}, bf16[5,512,128]{2,1,0:T(8,128)(2,1)S(1)}, u32[]{:S(2)}, u32[]{:S(2)}) collective-permute-start(bf16[5,512,128]{2,1,0:T(8,128)(2,1)S(1)} %copy-done.1), channel_id=1, source_target_pairs={{0,2},{1,3},{2,0},{3,1},{4,6},{5,7},{6,4},{7,5},{8,10},{9,11},{10,... | collective-permute-start | bytes 1966088 | tf_op jit(solution)/shard_map/ppermute | solution.py:269
  26.1 39.0 %collective-permute-start = (bf16[5,512,128]{2,1,0:T(8,128)(2,1)S(1)}, bf16[5,512,128]{2,1,0:T(8,128)(2,1)S(1)}, u32[]{:S(2)}, u32[]{:S(2)}) collective-permute-start(bf16[5,512,128]{2,1,0:T(8,128)(2,1)S(1)} %copy-done.1), channel_id=1, source_target_pairs={{0,1},{1,0},{2,3},{3,2},{4,5},{5,4},{6,7},{7,6},{8,9},{9,8},{10,11... | collective-permute-start | bytes 1966088 | tf_op jit(solution)/shard_map/ppermute | solution.py:269
  47.3 17.8 %collective-permute-start.2 = (bf16[5,512,128]{2,1,0:T(8,128)(2,1)S(1)}, bf16[5,512,128]{2,1,0:T(8,128)(2,1)}, u32[]{:S(2)}, u32[]{:S(2)}) collective-permute-start(bf16[5,512,128]{2,1,0:T(8,128)(2,1)S(1)} %collective-permute-done.1.g2), channel_id=1, source_target_pairs={{0,1},{1,0},{2,3},{3,2},{4,5},{5,4},{6,7},{7,6},{8,9},{9,8},{10,11... | collective-permute-start | bytes 1966088 | tf_op jit(solution)/shard_map/ppermute | solution.py:269
  49.3 12.3 %collective-permute-start.4 = (bf16[2,512,128]{2,1,0:T(8,128)(2,1)S(1)}, bf16[2,512,128]{2,1,0:T(8,128)(2,1)S(1)}, u32[]{:S(2)}, u32[]{:S(2)}) collective-permute-start(bf16[2,512,128]{2,1,0:T(8,128)(2,1)S(1)} %pad_maximum_fusion.w0), channel_id=1, source_target_pairs={{0,2},{1,3},{2,0},{3,1},{4,6},{5,7},{6,4},{7,5},{8,10},{9,11},{10,... | collective-permute-start | bytes 786440 | tf_op jit(solution)/shard_map/ppermute | solution.py:269
  51.9 11.6 %collective-permute-start.3 = (bf16[2,512,128]{2,1,0:T(8,128)(2,1)S(1)}, bf16[2,512,128]{2,1,0:T(8,128)(2,1)S(1)}, u32[]{:S(2)}, u32[]{:S(2)}) collective-permute-start(bf16[2,512,128]{2,1,0:T(8,128)(2,1)S(1)} %pad_maximum_fusion.w0), channel_id=1, source_target_pairs={{0,1},{1,0},{2,3},{3,2},{4,5},{5,4},{6,7},{7,6},{8,9},{9,8},{10,11... | collective-permute-start | bytes 786440 | tf_op jit(solution)/shard_map/ppermute | solution.py:269
  61.6 3.6 %collective-permute-start.5 = (bf16[2,512,128]{2,1,0:T(8,128)(2,1)S(1)}, bf16[2,512,128]{2,1,0:T(8,128)(2,1)}, u32[]{:S(2)}, u32[]{:S(2)}) collective-permute-start(bf16[2,512,128]{2,1,0:T(8,128)(2,1)S(1)} %collective-permute-done.4.w2), channel_id=1, source_target_pairs={{0,1},{1,0},{2,3},{3,2},{4,5},{5,4},{6,7},{7,6},{8,9},{9,8},{10,11... | collective-permute-start | bytes 786440 | tf_op jit(solution)/shard_map/ppermute | solution.py:269
  65.1 8.1 %copy-start.3 = (bf16[5,512,128]{2,1,0:T(8,128)(2,1)}, bf16[5,512,128]{2,1,0:T(8,128)(2,1)S(1)}, u32[]{:S(2)}) copy-start(bf16[5,512,128]{2,1,0:T(8,128)(2,1)S(1)} %collective-permute-done.g1) | copy-start | bytes 1966084
  65.1 1.3 copy-start.5
  73.2 17.4 %copy-start.12 = (s32[640]{0:T(1024)S(1)}, s32[640]{0:T(1024)}, u32[]{:S(2)}) copy-start(s32[640]{0:T(1024)} %param.17) | copy-start | bytes 7684
  73.2 17.5 %copy-start.13 = (s32[640]{0:T(1024)S(1)}, s32[640]{0:T(1024)}, u32[]{:S(2)}) copy-start(s32[640]{0:T(1024)} %param.18) | copy-start | bytes 7684
  73.2 56.6 %all-to-all-start = ((bf16[640,4,128]{2,1,0:T(4,128)(2,1)}), bf16[640,4,128]{2,1,0:T(4,128)(2,1)S(1)}, u32[]{:S(2)}, u32[]{:S(2)}) async-start(bf16[640,4,128]{2,1,0:T(4,128)(2,1)} %bitcast.3), calls=%async_computation | async-start | bytes 1310720 | tf_op jit(solution)/shard_map/all_to_all | solution.py:265
  90.9 1.1 copy-start.9
  96.1 9.1 %collective-permute-start.6 = (bf16[640,128]{1,0:T(8,128)(2,1)S(1)}, bf16[640,128]{1,0:T(8,128)(2,1)S(1)}, u32[]{:S(2)}, u32[]{:S(2)}) collective-permute-start(bf16[640,128]{1,0:T(8,128)(2,1)S(1)} %get-tuple-element.16), channel_id=1, source_target_pairs={{0,1},{1,0},{2,3},{3,2},{4,5},{5,4},{6,7},{7,6},{8,9},{9,8},{10,11... | collective-permute-start | bytes 491528 | tf_op jit(solution)/shard_map/ppermute | solution.py:269
  98.0 11.7 %collective-permute-start.7 = (bf16[640,128]{1,0:T(8,128)(2,1)S(1)}, bf16[640,128]{1,0:T(8,128)(2,1)S(1)}, u32[]{:S(2)}, u32[]{:S(2)}) collective-permute-start(bf16[640,128]{1,0:T(8,128)(2,1)S(1)} %get-tuple-element.17), channel_id=1, source_target_pairs={{0,2},{1,3},{2,0},{3,1},{4,6},{5,7},{6,4},{7,5},{8,10},{9,11},{10,... | collective-permute-start | bytes 491528 | tf_op jit(solution)/shard_map/ppermute | solution.py:269
  100.6 12.5 %collective-permute-start.8 = (bf16[640,128]{1,0:T(8,128)(2,1)S(1)}, bf16[640,128]{1,0:T(8,128)(2,1)S(1)}, u32[]{:S(2)}, u32[]{:S(2)}) collective-permute-start(bf16[640,128]{1,0:T(8,128)(2,1)S(1)} %get-tuple-element.18), channel_id=1, source_target_pairs={{0,3},{1,2},{2,1},{3,0},{4,7},{5,6},{6,5},{7,4},{8,11},{9,10},{10,... | collective-permute-start | bytes 491528 | tf_op jit(solution)/shard_map/ppermute | solution.py:269
  129.8 9.5 %copy-start.14 = (f32[512]{0:T(512)S(1)}, f32[512]{0:T(512)}, u32[]{:S(2)}) copy-start(f32[512]{0:T(512)} %param.20) | copy-start | bytes 6148
  129.8 9.5 %copy-start.15 = (s32[512]{0:T(512)S(1)}, s32[512]{0:T(512)}, u32[]{:S(2)}) copy-start(s32[512]{0:T(512)} %param.21) | copy-start | bytes 6148
  129.8 9.9 %copy-start.16 = (f32[24]{0:T(128)S(1)}, f32[24]{0:T(128)}, u32[]{:S(2)}) copy-start(f32[24]{0:T(128)} %param.19) | copy-start | bytes 292
  132.4 45.8 %all-to-all-start.2 = ((bf16[640,4,128]{2,1,0:T(4,128)(2,1)}), bf16[640,4,128]{2,1,0:T(4,128)(2,1)S(1)}, u32[]{:S(2)}, u32[]{:S(2)}) async-start(bf16[640,4,128]{2,1,0:T(4,128)(2,1)} %bitcast.8), calls=%async_computation.2 | async-start | bytes 1310720 | tf_op jit(solution)/shard_map/all_to_all | solution.py:265
  140.2 1.1 copy-start.4
  (5 other events, 5.1 us)

commit v5 on v4

--- a/solution.py
+++ b/solution.py
@@ -7,6 +7,7 @@
 
 F32 = jnp.float32
 BF16 = jnp.bfloat16
+PAD = 8
 
 
 def dot(left, right):
@@ -15,6 +16,10 @@
 
 def chunks_of(total):
     return [(start, min(8, total - start)) for start in range(0, total, 8)]
+
+
+def pitch_of(nb):
+    return nb + PAD
 
 
 def swap_rows(values, bits, first_bit):
@@ -31,24 +36,28 @@
     return low, total - low
 
 
-def skew(source, middle, target, nb, count, ready):
+def skew(source, middle, target, nb, count, ready, done):
     low, high = split_bits(nb)
+    pitch = pitch_of(nb)
     for start, size in chunks_of(count):
         ready(start, size)
-        for base in range(1 << high):
-            rows = [(base << low) + i for i in range(1 << low)]
-            values = [source[pl.ds(start * nb + r, size, stride=nb), :] for r in rows]
-            for r, value in zip(rows, swap_rows(values, low, 0)):
-                middle[r, start : start + size, :] = value
         for base in range(1 << low):
             rows = [base + (i << low) for i in range(1 << high)]
+            values = [source[pl.ds(start * pitch + r, size, stride=pitch), :] for r in rows]
+            for r, value in zip(rows, swap_rows(values, high, low)):
+                middle[r, start : start + size, :] = value
+    for base in range(1 << high):
+        rows = [(base << low) + i for i in range(1 << low)]
+        for start, size in chunks_of(count):
             values = [middle[r, start : start + size, :] for r in rows]
-            for r, value in zip(rows, swap_rows(values, high, low)):
+            for r, value in zip(rows, swap_rows(values, low, 0)):
                 target[r * count + start : r * count + start + size, :] = value
+        done(rows[0] * count, len(rows) * count)
 
 
 def unskew(source, middle, target, nb, count, done):
     low, high = split_bits(nb)
+    pitch = pitch_of(nb)
     for start, size in chunks_of(count):
         for base in range(1 << low):
             rows = [base + (i << low) for i in range(1 << high)]
@@ -59,27 +68,49 @@
             rows = [(base << low) + i for i in range(1 << low)]
             values = [middle[r, start : start + size, :] for r in rows]
             for r, value in zip(rows, swap_rows(values, low, 0)):
-                target[pl.ds(start * nb + r, size, stride=nb), :] = value
+                target[pl.ds(start * pitch + r, size, stride=pitch), :] = value
         done(start, size)
 
 
-def skew_kernel(a_ref, out_ref, flat, middle, target):
-    nslot, nvirt, nb = a_ref.shape
+def pieces(source, target, sems, count):
+    size = source.shape[0] // count
+    return [
+        pltpu.make_async_copy(
+            source.at[pl.ds(i * size, size)], target.at[pl.ds(i * size, size)], sems.at[i]
+        )
+        for i in range(count)
+    ]
+
+
+def skew_kernel(a_hbm, out_hbm, raw, packed, sems_in, sems_out, flat, middle, target):
+    nslot, nvirt, nb = raw.shape
     ncol = nvirt // nb
+    fetches = pieces(a_hbm, raw, sems_in, nslot)
+    for copy in fetches:
+        copy.start()
+    stores = pieces(packed, out_hbm, sems_out, sems_out.shape[0])
 
     def ready(start, size):
         for s in range(start // ncol, (start + size) // ncol):
-            flat[s * nvirt : (s + 1) * nvirt, :] = a_ref[s].astype(F32)
-
-    skew(flat, middle, target, nb, nslot * ncol, ready)
-    out_ref[...] = target[...].astype(BF16)
+            fetches[s].wait()
+            for d in range(ncol):
+                at = (s * ncol + d) * pitch_of(nb)
+                flat[at : at + nb, :] = raw[s, d * nb : (d + 1) * nb, :].astype(F32)
+
+    def done(start, size):
+        packed[start : start + size, :] = target[start : start + size, :].astype(BF16)
+        stores[start // size].start()
+
+    skew(flat, middle, target, nb, nslot * ncol, ready, done)
+    for copy in stores:
+        copy.wait()
 
 
 def skew_scratch(count, nb):
     return [
-        pltpu.VMEM((count * nb, nb), F32),
+        pltpu.VMEM((count * pitch_of(nb), nb), F32),
         pltpu.VMEM((nb, -(-count // 8) * 8, nb), F32),
-        pltpu.VMEM((count * nb, nb), F32),
+        pltpu.VMEM((count * pitch_of(nb), nb), F32),
     ]
 
 
@@ -129,11 +160,13 @@
             stack[nvirt:, :] = dot(stack[:nvirt, :], dmat[...]).astype(BF16)
             total = dot(left[...], stack[...]) + dot(low[...], fmat[...])
             for k in range(ncol):
-                at = pl.multiple_of((s * ncol + (col ^ k)) * nb, nb)
+                at = pl.multiple_of((s * ncol + (col ^ k)) * pitch_of(nb), 8)
                 flat[pl.ds(at, nb), :] = total[:, k * nb : (k + 1) * nb].T
 
-    skew(flat, middle, target, nb, nslot * ncol, ready)
-    out_ref[...] = target[...].astype(BF16)
+    def done(start, size):
+        out_ref[start : start + size, :] = target[start : start + size, :].astype(BF16)
+
+    skew(flat, middle, target, nb, nslot * ncol, ready, done)
 
 
 def cols_kernel(c_ref, g0, g1, g2, g3, w0, fl_ref, dl_ref, p_ref, right, acat):
@@ -180,34 +213,48 @@
         out_ref[col ^ k] = (l_ref[col ^ k].astype(F32) + part[...].astype(F32)).astype(BF16)
 
 
-def combine_kernel(y_ref, s_hbm, partner_col, out_ref, wide, ycat, both, sems):
+def combine_kernel(
+    y_ref, s_hbm, partner_col, out_hbm, wide, ycat, both, packed, sems_in, sems_out
+):
     ncol, slots, nb = both.shape
-    copies = [pltpu.make_async_copy(s_hbm.at[d], both.at[d], sems.at[d]) for d in range(ncol)]
-    for copy in copies:
+    fetches = pieces(s_hbm, both, sems_in, ncol)
+    for copy in fetches:
         copy.start()
+    stores = pieces(packed, out_hbm, sems_out, sems_out.shape[0])
     wide[...] = y_ref[...].astype(F32)
     for d in range(ncol):
         ycat[:, d * nb : (d + 1) * nb] = wide[pl.ds(d, slots, stride=ncol), :].astype(BF16)
-    pick = (partner_col[...] == lax.broadcasted_iota(jnp.int32, (slots, slots), 1)).astype(BF16)
-    total = dot(pick, ycat[...])
-    for d in range(ncol):
-        copies[d].wait()
-        wide[pl.ds(d, slots, stride=ncol), :] = (
-            total[:, d * nb : (d + 1) * nb] + both[d].astype(F32)
-        )
-    out_ref[...] = wide[...].astype(BF16)
+    pick = partner_col[...] == lax.broadcasted_iota(jnp.int32, (slots, slots), 1)
+    total = dot(pick.astype(BF16), ycat[...])
+    for copy in fetches:
+        copy.wait()
+    part = slots // len(stores)
+    for i, store in enumerate(stores):
+        at = slice(i * part, (i + 1) * part)
+        for d in range(ncol):
+            wide[pl.ds(i * part * ncol + d, part, stride=ncol), :] = total[
+                at, d * nb : (d + 1) * nb
+            ] + both[d, at, :].astype(F32)
+        rows = slice(i * part * ncol, (i + 1) * part * ncol)
+        packed[rows, :] = wide[rows, :].astype(BF16)
+        store.start()
+    for store in stores:
+        store.wait()
 
 
 def finish_kernel(occ_ref, z_ref, p_ref, base_ref, out_hbm, stage, sems, flat, middle, target):
     nslot, nvirt, nb = p_ref.shape
     ncol = nvirt // nb
-    flat[...] = z_ref[...].astype(F32)
+    flat[: z_ref.shape[0], :] = z_ref[...].astype(F32)
     copies = [pltpu.make_async_copy(stage.at[s], out_hbm.at[s], sems.at[s]) for s in range(nslot)]
 
     def done(start, size):
         for s in range(start // ncol, (start + size) // ncol):
-            total = p_ref[s].astype(F32) + target[s * nvirt : (s + 1) * nvirt, :]
-            stage[s] = total / (base_ref[...] - occ_ref[s])
+            for d in range(ncol):
+                at = (s * ncol + d) * pitch_of(nb)
+                rows = slice(d * nb, (d + 1) * nb)
+                total = p_ref[s, rows, :].astype(F32) + target[at : at + nb, :]
+                stage[s, rows, :] = total / (base_ref[rows, :] - occ_ref[s])
             copies[s].start()
 
     unskew(flat, middle, target, nb, nslot * ncol, done)
@@ -271,8 +318,18 @@
     far = swap(amplitudes, 2)
     dma = pltpu.SemaphoreType.DMA
     skewed = call(
-        skew_kernel, shape((nb * count, nb), BF16), skew_scratch(count, nb), [VMEM]
-    )(amplitudes)
+        skew_kernel,
+        shape((nb * count, nb), BF16),
+        [
+            pltpu.VMEM(amplitudes.shape, BF16),
+            pltpu.VMEM((nb * count, nb), BF16),
+            dma((slot_dev,)),
+            dma((1 << split_bits(nb)[1],)),
+        ]
+        + skew_scratch(count, nb),
+        [HBM],
+        HBM,
+    )(stay(amplitudes))
     x = exchange(skewed)
     pair_col = slot_pair.reshape(slots, 1)
     pair_row = slot_pair.reshape(1, slots)
@@ -330,9 +387,12 @@
             pltpu.VMEM((slots * ncol, nb), F32),
             pltpu.VMEM((slots, nvirt), BF16),
             pltpu.VMEM((ncol, slots, nb), BF16),
+            pltpu.VMEM((nb * count, nb), BF16),
             dma((ncol,)),
+            dma((2,)),
         ],
         [VMEM, HBM, VMEM],
+        HBM,
     )(y, stay(both_terms), partner_col)
     z = exchange(back)
     own_pairs = lax.dynamic_slice_in_dim(slot_pair, pair * slot_dev, slot_dev)

time: 182 us -> 180 us (0.989)
    unnamed x34 -> x32, local copies, waits for them, and re-layouts: 8.57 us -> 7.47 us
  transfers between devices with their start and end apart: 12 -> 12, of which waited for: 7 -> 7; matrix products, arithmetic and copies ran while one was open for 1% -> 1% of each run, Pallas kernels for 8% -> 7%
where the time goes in v5:
time: 180 us; the launch traced here: 179 us
  waiting for transfers between devices  83.1 us (46%)
  starting transfers between devices  66.9 us (37%)
  Pallas kernels  20.3 us (11%)
  local copies, waits for them, and re-layouts  7.83 us (4%)
    all_to_all x3, waiting for transfers between devices, exchange(): got = lax.all_to_all(sent, 'pair', split_axis=0, concat_axis=0, tiled=True)  46.8 us
    all_to_all x3, starting transfers between devices, exchange(): got = lax.all_to_all(sent, 'pair', split_axis=0, concat_axis=0, tiled=True)  44.6 us
    ppermute x9, waiting for transfers between devices, swap(): return lax.ppermute(value, 'col', [(i, i ^ k) for i in range(ncol)])  36.3 us
    ppermute x9, starting transfers between devices, swap(): return lax.ppermute(value, 'col', [(i, i ^ k) for i in range(ncol)])  22.3 us
    unnamed x32, local copies, waits for them, and re-layouts  7.47 us
    pallas_call x1, Pallas kernels, update_of(): call(rows_kernel, shape((nb * count, nb), BF16), [pltpu.VMEM((nb, 2 * nvi...  5.33 us
    pallas_call x1, Pallas kernels, update_of(): call(cols_kernel, shape(amplitudes.shape, BF16), [pltpu.VMEM((nvirt, 2 *...  3.71 us
  transfers between devices with their start and end apart: 12, of which 7 were waited for; matrix products, arithmetic and copies ran while one was open for 1% of the time, Pallas kernels for 7%

profile of v5, /device:TPU:16, one launch (start us, length us, event | category | flops | bytes accessed | tf_op | source)
XLA Modules:
  0.0 179.3 jit_solution(11281284702687824263)
XLA Ops:
  0.0 2.4 %shard_map.110 = bf16[2560,128]{1,0:T(8,128)(2,1)} custom-call(bf16[5,512,128]{2,1,0:T(8,128)(2,1)} %g0.3), custom_call_target="tpu_custom_call" | custom-call | tf_op jit(solution)/shard_map/pallas_call | solution.py:320
  2.5 20.5 %all-to-all-start.1 = ((bf16[640,4,128]{2,1,0:T(4,128)(2,1)}), bf16[640,4,128]{2,1,0:T(4,128)(2,1)S(1)}, u32[]{:S(2)}, u32[]{:S(2)}) async-start(bf16[640,4,128]{2,1,0:T(4,128)(2,1)} %bitcast.6), calls=%async_computation.1 | async-start | bytes 1310720 | tf_op jit(solution)/shard_map/all_to_all | solution.py:312
  23.0 2.5 %collective-permute-start.1 = (bf16[5,512,128]{2,1,0:T(8,128)(2,1)S(1)}, bf16[5,512,128]{2,1,0:T(8,128)(2,1)S(1)}, u32[]{:S(2)}, u32[]{:S(2)}) collective-permute-start(bf16[5,512,128]{2,1,0:T(8,128)(2,1)S(1)} %copy-done), channel_id=1, source_target_pairs={{0,2},{1,3},{2,0},{3,1},{4,6},{5,7},{6,4},{7,5},{8,10},{9,11},{10,... | collective-permute-start | bytes 1966088 | tf_op jit(solution)/shard_map/ppermute | solution.py:316
  25.5 1.9 %collective-permute-start = (bf16[5,512,128]{2,1,0:T(8,128)(2,1)S(1)}, bf16[5,512,128]{2,1,0:T(8,128)(2,1)S(1)}, u32[]{:S(2)}, u32[]{:S(2)}) collective-permute-start(bf16[5,512,128]{2,1,0:T(8,128)(2,1)S(1)} %copy-done), channel_id=1, source_target_pairs={{0,1},{1,0},{2,3},{3,2},{4,5},{5,4},{6,7},{7,6},{8,9},{9,8},{10,11... | collective-permute-start | bytes 1966088 | tf_op jit(solution)/shard_map/ppermute | solution.py:316
  27.5 19.3 %collective-permute-done.1.g2 = bf16[5,512,128]{2,1,0:T(8,128)(2,1)S(1)} collective-permute-done((bf16[5,512,128]{2,1,0:T(8,128)(2,1)S(1)}, bf16[5,512,128]{2,1,0:T(8,128)(2,1)S(1)}, u32[]{:S(2)}, u32[]{:S(2)}) %collective-permute-start.1) | collective-permute-done | bytes 655392 | tf_op jit(solution)/shard_map/ppermute | solution.py:316
  46.7 1.9 %collective-permute-start.2 = (bf16[5,512,128]{2,1,0:T(8,128)(2,1)S(1)}, bf16[5,512,128]{2,1,0:T(8,128)(2,1)}, u32[]{:S(2)}, u32[]{:S(2)}) collective-permute-start(bf16[5,512,128]{2,1,0:T(8,128)(2,1)S(1)} %collective-permute-done.1.g2), channel_id=1, source_target_pairs={{0,1},{1,0},{2,3},{3,2},{4,5},{5,4},{6,7},{7,6},{8,9},{9,8},{10,11... | collective-permute-start | bytes 1966088 | tf_op jit(solution)/shard_map/ppermute | solution.py:316
  48.7 2.6 %collective-permute-start.4 = (bf16[2,512,128]{2,1,0:T(8,128)(2,1)S(1)}, bf16[2,512,128]{2,1,0:T(8,128)(2,1)S(1)}, u32[]{:S(2)}, u32[]{:S(2)}) collective-permute-start(bf16[2,512,128]{2,1,0:T(8,128)(2,1)S(1)} %pad_maximum_fusion.w0), channel_id=1, source_target_pairs={{0,2},{1,3},{2,0},{3,1},{4,6},{5,7},{6,4},{7,5},{8,10},{9,11},{10,... | collective-permute-start | bytes 786440 | tf_op jit(solution)/shard_map/ppermute | solution.py:316
  51.3 2.1 %collective-permute-start.3 = (bf16[2,512,128]{2,1,0:T(8,128)(2,1)S(1)}, bf16[2,512,128]{2,1,0:T(8,128)(2,1)S(1)}, u32[]{:S(2)}, u32[]{:S(2)}) collective-permute-start(bf16[2,512,128]{2,1,0:T(8,128)(2,1)S(1)} %pad_maximum_fusion.w0), channel_id=1, source_target_pairs={{0,1},{1,0},{2,3},{3,2},{4,5},{5,4},{6,7},{7,6},{8,9},{9,8},{10,11... | collective-permute-start | bytes 786440 | tf_op jit(solution)/shard_map/ppermute | solution.py:316
  53.5 7.5 %collective-permute-done.4.w2 = bf16[2,512,128]{2,1,0:T(8,128)(2,1)S(1)} collective-permute-done((bf16[2,512,128]{2,1,0:T(8,128)(2,1)S(1)}, bf16[2,512,128]{2,1,0:T(8,128)(2,1)S(1)}, u32[]{:S(2)}, u32[]{:S(2)}) %collective-permute-start.4) | collective-permute-done | bytes 262176 | tf_op jit(solution)/shard_map/ppermute | solution.py:316
  61.0 1.9 %collective-permute-start.5 = (bf16[2,512,128]{2,1,0:T(8,128)(2,1)S(1)}, bf16[2,512,128]{2,1,0:T(8,128)(2,1)}, u32[]{:S(2)}, u32[]{:S(2)}) collective-permute-start(bf16[2,512,128]{2,1,0:T(8,128)(2,1)S(1)} %collective-permute-done.4.w2), channel_id=1, source_target_pairs={{0,1},{1,0},{2,3},{3,2},{4,5},{5,4},{6,7},{7,6},{8,9},{9,8},{10,11... | collective-permute-start | bytes 786440 | tf_op jit(solution)/shard_map/ppermute | solution.py:316
  66.9 5.3 %shard_map.109 = bf16[2560,128]{1,0:T(8,128)(2,1)} custom-call(s32[1]{0:T(128)} %bitcast.c_ref, bf16[5,512,128]{2,1,0:T(8,128)(2,1)S(1)} %copy-done, bf16[5,512,128]{2,1,0:T(8,128)(2,1)S(1)} %collective-permute-done.g1, bf16[5,512,128]{2,1,0:T(8,128)(2,1)S(1)} %collective-permute-done.1.g2, bf16[5,512,128]{2,1,0:T(8,128)(2,1)} %collective-permute-done.2.g3, ...), custom_call_target="tpu_custom_call" | custom-call | tf_op jit(solution)/shard_map/pallas_call | solution.py:346
  72.2 17.2 %all-to-all-start = ((bf16[640,4,128]{2,1,0:T(4,128)(2,1)}), bf16[640,4,128]{2,1,0:T(4,128)(2,1)S(1)}, u32[]{:S(2)}, u32[]{:S(2)}) async-start(bf16[640,4,128]{2,1,0:T(4,128)(2,1)} %bitcast.3), calls=%async_computation | async-start | bytes 1310720 | tf_op jit(solution)/shard_map/all_to_all | solution.py:312
  90.8 2.4 %shard_map.111 = (bf16[640,640]{1,0:T(8,128)(2,1)S(1)}, bf16[640,640]{1,0:T(8,128)(2,1)S(1)}) custom-call(s32[640,1]{1,0:T(8,128)S(1)} %reshape.65.pair_col, s32[1,640]{1,0:T(1,128)S(1)} %reshape.61.pair_row, s32[640,1]{1,0:T(8,128)S(1)} %reshape.66.partner_col, bf16[576,576]{1,0:T(8,128)(2,1)S(1)} %copy-done.8), custom_call_target="tpu_custom_call" | custom-call | tf_op jit(solution)/shard_map/pallas_call | solution.py:337
  94.9 1.9 %collective-permute-start.6 = (bf16[640,128]{1,0:T(8,128)(2,1)S(1)}, bf16[640,128]{1,0:T(8,128)(2,1)S(1)}, u32[]{:S(2)}, u32[]{:S(2)}) collective-permute-start(bf16[640,128]{1,0:T(8,128)(2,1)S(1)} %get-tuple-element.16), channel_id=1, source_target_pairs={{0,1},{1,0},{2,3},{3,2},{4,5},{5,4},{6,7},{7,6},{8,9},{9,8},{10,11... | collective-permute-start | bytes 491528 | tf_op jit(solution)/shard_map/ppermute | solution.py:316
  96.8 2.7 %collective-permute-start.7 = (bf16[640,128]{1,0:T(8,128)(2,1)S(1)}, bf16[640,128]{1,0:T(8,128)(2,1)S(1)}, u32[]{:S(2)}, u32[]{:S(2)}) collective-permute-start(bf16[640,128]{1,0:T(8,128)(2,1)S(1)} %get-tuple-element.17), channel_id=1, source_target_pairs={{0,2},{1,3},{2,0},{3,1},{4,6},{5,7},{6,4},{7,5},{8,10},{9,11},{10,... | collective-permute-start | bytes 491528 | tf_op jit(solution)/shard_map/ppermute | solution.py:316
  99.5 4.6 %collective-permute-start.8 = (bf16[640,128]{1,0:T(8,128)(2,1)S(1)}, bf16[640,128]{1,0:T(8,128)(2,1)S(1)}, u32[]{:S(2)}, u32[]{:S(2)}) collective-permute-start(bf16[640,128]{1,0:T(8,128)(2,1)S(1)} %get-tuple-element.18), channel_id=1, source_target_pairs={{0,3},{1,2},{2,1},{3,0},{4,7},{5,6},{6,5},{7,4},{8,11},{9,10},{10,... | collective-permute-start | bytes 491528 | tf_op jit(solution)/shard_map/ppermute | solution.py:316
  104.2 4.5 %collective-permute-done.7.m2 = bf16[640,128]{1,0:T(8,128)(2,1)S(1)} collective-permute-done((bf16[640,128]{1,0:T(8,128)(2,1)S(1)}, bf16[640,128]{1,0:T(8,128)(2,1)S(1)}, u32[]{:S(2)}, u32[]{:S(2)}) %collective-permute-start.7) | collective-permute-done | bytes 163872 | tf_op jit(solution)/shard_map/ppermute | solution.py:316
  108.7 3.4 %collective-permute-done.8.m3 = bf16[640,128]{1,0:T(8,128)(2,1)S(1)} collective-permute-done((bf16[640,128]{1,0:T(8,128)(2,1)S(1)}, bf16[640,128]{1,0:T(8,128)(2,1)S(1)}, u32[]{:S(2)}, u32[]{:S(2)}) %collective-permute-start.8) | collective-permute-done | bytes 163872 | tf_op jit(solution)/shard_map/ppermute | solution.py:316
  113.1 15.8 %all-to-all-done = bf16[640,4,128]{2,1,0:T(4,128)(2,1)S(1)} async-done(((bf16[640,4,128]{2,1,0:T(4,128)(2,1)}), bf16[640,4,128]{2,1,0:T(4,128)(2,1)S(1)}, u32[]{:S(2)}, u32[]{:S(2)}) %all-to-all-start) | async-done | bytes 655392 | tf_op jit(solution)/shard_map/all_to_all | solution.py:312
  128.9 2.6 %shard_map.114 = bf16[2560,128]{1,0:T(8,128)(2,1)} custom-call(bf16[2560,128]{1,0:T(8,128)(2,1)S(1)} %bitcast.11, bf16[4,640,128]{2,1,0:T(8,128)(2,1)} %copy-done.1, s32[640,1]{1,0:T(8,128)S(1)} %reshape.66.partner_col), custom_call_target="tpu_custom_call" | custom-call | tf_op jit(solution)/shard_map/pallas_call | solution.py:383
  131.5 6.9 %all-to-all-start.2 = ((bf16[640,4,128]{2,1,0:T(4,128)(2,1)}), bf16[640,4,128]{2,1,0:T(4,128)(2,1)S(1)}, u32[]{:S(2)}, u32[]{:S(2)}) async-start(bf16[640,4,128]{2,1,0:T(4,128)(2,1)} %bitcast.8), calls=%async_computation.2 | async-start | bytes 1310720 | tf_op jit(solution)/shard_map/all_to_all | solution.py:312
  142.4 3.7 %shard_map.115.p_ref = bf16[5,512,128]{2,1,0:T(8,128)(2,1)S(1)} custom-call(s32[1]{0:T(128)} %bitcast.c_ref, bf16[5,512,128]{2,1,0:T(8,128)(2,1)S(1)} %copy-done, bf16[5,512,128]{2,1,0:T(8,128)(2,1)S(1)} %copy-done.3, bf16[5,512,128]{2,1,0:T(8,128)(2,1)S(1)} %collective-permute-done.1.g2, bf16[5,512,128]{2,1,0:T(8,128)(2,1)} %collective-permute-done.2.g3, ...), custom_call_target="tpu_custom_call" | custom-call | tf_op jit(solution)/shard_map/pallas_call | solution.py:363
  146.1 31.0 %all-to-all-done.2 = bf16[640,4,128]{2,1,0:T(4,128)(2,1)S(1)} async-done(((bf16[640,4,128]{2,1,0:T(4,128)(2,1)}), bf16[640,4,128]{2,1,0:T(4,128)(2,1)S(1)}, u32[]{:S(2)}, u32[]{:S(2)}) %all-to-all-start.2) | async-done | bytes 655392 | tf_op jit(solution)/shard_map/all_to_all | solution.py:312
  177.1 2.0 %shard_map.116 = f32[5,512,128]{2,1,0:T(8,128)} custom-call(f32[5]{0:T(128)S(1)} %compare_select_fusion.occ_ref, bf16[2560,128]{1,0:T(8,128)(2,1)S(1)} %bitcast.12, bf16[5,512,128]{2,1,0:T(8,128)(2,1)S(1)} %shard_map.115.p_ref, f32[512,128]{1,0:T(8,128)S(1)} %broadcast_add_fusion.base_ref), custom_call_target="tpu_custom_call" | custom-call | tf_op jit(solution)/shard_map/pallas_call | solution.py:412
  (50 shorter events, 12.0 us)
Async XLA Ops:
  0.0 23.0 %copy-start = (bf16[5,512,128]{2,1,0:T(8,128)(2,1)S(1)}, bf16[5,512,128]{2,1,0:T(8,128)(2,1)}, u32[]{:S(2)}) copy-start(bf16[5,512,128]{2,1,0:T(8,128)(2,1)} %g0.3) | copy-start | bytes 1966084
  0.0 48.7 %copy-start.10 = (bf16[512,128]{1,0:T(8,128)(2,1)S(1)}, bf16[512,128]{1,0:T(8,128)(2,1)}, u32[]{:S(2)}) copy-start(bf16[512,128]{1,0:T(8,128)(2,1)} %param.14) | copy-start | bytes 393220
  0.0 48.7 %copy-start.9 = (bf16[512,128]{1,0:T(8,128)(2,1)S(1)}, bf16[512,128]{1,0:T(8,128)(2,1)}, u32[]{:S(2)}) copy-start(bf16[512,128]{1,0:T(8,128)(2,1)} %param.15) | copy-start | bytes 393220
  2.5 69.8 %all-to-all-start.1 = ((bf16[640,4,128]{2,1,0:T(4,128)(2,1)}), bf16[640,4,128]{2,1,0:T(4,128)(2,1)S(1)}, u32[]{:S(2)}, u32[]{:S(2)}) async-start(bf16[640,4,128]{2,1,0:T(4,128)(2,1)} %bitcast.6), calls=%async_computation.1 | async-start | bytes 1310720 | tf_op jit(solution)/shard_map/all_to_all | solution.py:312
  23.0 23.7 %collective-permute-start.1 = (bf16[5,512,128]{2,1,0:T(8,128)(2,1)S(1)}, bf16[5,512,128]{2,1,0:T(8,128)(2,1)S(1)}, u32[]{:S(2)}, u32[]{:S(2)}) collective-permute-start(bf16[5,512,128]{2,1,0:T(8,128)(2,1)S(1)} %copy-done), channel_id=1, source_target_pairs={{0,2},{1,3},{2,0},{3,1},{4,6},{5,7},{6,4},{7,5},{8,10},{9,11},{10,... | collective-permute-start | bytes 1966088 | tf_op jit(solution)/shard_map/ppermute | solution.py:316
  25.5 39.0 %collective-permute-start = (bf16[5,512,128]{2,1,0:T(8,128)(2,1)S(1)}, bf16[5,512,128]{2,1,0:T(8,128)(2,1)S(1)}, u32[]{:S(2)}, u32[]{:S(2)}) collective-permute-start(bf16[5,512,128]{2,1,0:T(8,128)(2,1)S(1)} %copy-done), channel_id=1, source_target_pairs={{0,1},{1,0},{2,3},{3,2},{4,5},{5,4},{6,7},{7,6},{8,9},{9,8},{10,11... | collective-permute-start | bytes 1966088 | tf_op jit(solution)/shard_map/ppermute | solution.py:316
  46.7 17.8 %collective-permute-start.2 = (bf16[5,512,128]{2,1,0:T(8,128)(2,1)S(1)}, bf16[5,512,128]{2,1,0:T(8,128)(2,1)}, u32[]{:S(2)}, u32[]{:S(2)}) collective-permute-start(bf16[5,512,128]{2,1,0:T(8,128)(2,1)S(1)} %collective-permute-done.1.g2), channel_id=1, source_target_pairs={{0,1},{1,0},{2,3},{3,2},{4,5},{5,4},{6,7},{7,6},{8,9},{9,8},{10,11... | collective-permute-start | bytes 1966088 | tf_op jit(solution)/shard_map/ppermute | solution.py:316
  48.7 12.3 %collective-permute-start.4 = (bf16[2,512,128]{2,1,0:T(8,128)(2,1)S(1)}, bf16[2,512,128]{2,1,0:T(8,128)(2,1)S(1)}, u32[]{:S(2)}, u32[]{:S(2)}) collective-permute-start(bf16[2,512,128]{2,1,0:T(8,128)(2,1)S(1)} %pad_maximum_fusion.w0), channel_id=1, source_target_pairs={{0,2},{1,3},{2,0},{3,1},{4,6},{5,7},{6,4},{7,5},{8,10},{9,11},{10,... | collective-permute-start | bytes 786440 | tf_op jit(solution)/shard_map/ppermute | solution.py:316
  51.3 11.6 %collective-permute-start.3 = (bf16[2,512,128]{2,1,0:T(8,128)(2,1)S(1)}, bf16[2,512,128]{2,1,0:T(8,128)(2,1)S(1)}, u32[]{:S(2)}, u32[]{:S(2)}) collective-permute-start(bf16[2,512,128]{2,1,0:T(8,128)(2,1)S(1)} %pad_maximum_fusion.w0), channel_id=1, source_target_pairs={{0,1},{1,0},{2,3},{3,2},{4,5},{5,4},{6,7},{7,6},{8,9},{9,8},{10,11... | collective-permute-start | bytes 786440 | tf_op jit(solution)/shard_map/ppermute | solution.py:316
  61.0 3.6 %collective-permute-start.5 = (bf16[2,512,128]{2,1,0:T(8,128)(2,1)S(1)}, bf16[2,512,128]{2,1,0:T(8,128)(2,1)}, u32[]{:S(2)}, u32[]{:S(2)}) collective-permute-start(bf16[2,512,128]{2,1,0:T(8,128)(2,1)S(1)} %collective-permute-done.4.w2), channel_id=1, source_target_pairs={{0,1},{1,0},{2,3},{3,2},{4,5},{5,4},{6,7},{7,6},{8,9},{9,8},{10,11... | collective-permute-start | bytes 786440 | tf_op jit(solution)/shard_map/ppermute | solution.py:316
  64.5 7.7 %copy-start.2 = (bf16[5,512,128]{2,1,0:T(8,128)(2,1)}, bf16[5,512,128]{2,1,0:T(8,128)(2,1)S(1)}, u32[]{:S(2)}) copy-start(bf16[5,512,128]{2,1,0:T(8,128)(2,1)S(1)} %collective-permute-done.g1) | copy-start | bytes 1966084
  64.5 1.3 copy-start.4
  72.2 17.2 %copy-start.11 = (s32[640]{0:T(1024)S(1)}, s32[640]{0:T(1024)}, u32[]{:S(2)}) copy-start(s32[640]{0:T(1024)} %param.17) | copy-start | bytes 7684
  72.2 17.4 %copy-start.12 = (s32[640]{0:T(1024)S(1)}, s32[640]{0:T(1024)}, u32[]{:S(2)}) copy-start(s32[640]{0:T(1024)} %param.18) | copy-start | bytes 7684
  72.2 56.6 %all-to-all-start = ((bf16[640,4,128]{2,1,0:T(4,128)(2,1)}), bf16[640,4,128]{2,1,0:T(4,128)(2,1)S(1)}, u32[]{:S(2)}, u32[]{:S(2)}) async-start(bf16[640,4,128]{2,1,0:T(4,128)(2,1)} %bitcast.3), calls=%async_computation | async-start | bytes 1310720 | tf_op jit(solution)/shard_map/all_to_all | solution.py:312
  89.7 1.1 copy-start.8
  94.9 9.3 %collective-permute-start.6 = (bf16[640,128]{1,0:T(8,128)(2,1)S(1)}, bf16[640,128]{1,0:T(8,128)(2,1)S(1)}, u32[]{:S(2)}, u32[]{:S(2)}) collective-permute-start(bf16[640,128]{1,0:T(8,128)(2,1)S(1)} %get-tuple-element.16), channel_id=1, source_target_pairs={{0,1},{1,0},{2,3},{3,2},{4,5},{5,4},{6,7},{7,6},{8,9},{9,8},{10,11... | collective-permute-start | bytes 491528 | tf_op jit(solution)/shard_map/ppermute | solution.py:316
  96.8 11.9 %collective-permute-start.7 = (bf16[640,128]{1,0:T(8,128)(2,1)S(1)}, bf16[640,128]{1,0:T(8,128)(2,1)S(1)}, u32[]{:S(2)}, u32[]{:S(2)}) collective-permute-start(bf16[640,128]{1,0:T(8,128)(2,1)S(1)} %get-tuple-element.17), channel_id=1, source_target_pairs={{0,2},{1,3},{2,0},{3,1},{4,6},{5,7},{6,4},{7,5},{8,10},{9,11},{10,... | collective-permute-start | bytes 491528 | tf_op jit(solution)/shard_map/ppermute | solution.py:316
  99.5 12.5 %collective-permute-start.8 = (bf16[640,128]{1,0:T(8,128)(2,1)S(1)}, bf16[640,128]{1,0:T(8,128)(2,1)S(1)}, u32[]{:S(2)}, u32[]{:S(2)}) collective-permute-start(bf16[640,128]{1,0:T(8,128)(2,1)S(1)} %get-tuple-element.18), channel_id=1, source_target_pairs={{0,3},{1,2},{2,1},{3,0},{4,7},{5,6},{6,5},{7,4},{8,11},{9,10},{10,... | collective-permute-start | bytes 491528 | tf_op jit(solution)/shard_map/ppermute | solution.py:316
  128.9 9.5 %copy-start.13 = (f32[512]{0:T(512)S(1)}, f32[512]{0:T(512)}, u32[]{:S(2)}) copy-start(f32[512]{0:T(512)} %param.20) | copy-start | bytes 6148
  128.9 9.5 %copy-start.14 = (s32[512]{0:T(512)S(1)}, s32[512]{0:T(512)}, u32[]{:S(2)}) copy-start(s32[512]{0:T(512)} %param.21) | copy-start | bytes 6148
  128.9 9.9 %copy-start.15 = (f32[24]{0:T(128)S(1)}, f32[24]{0:T(128)}, u32[]{:S(2)}) copy-start(f32[24]{0:T(128)} %param.19) | copy-start | bytes 292
  131.5 45.7 %all-to-all-start.2 = ((bf16[640,4,128]{2,1,0:T(4,128)(2,1)}), bf16[640,4,128]{2,1,0:T(4,128)(2,1)S(1)}, u32[]{:S(2)}, u32[]{:S(2)}) async-start(bf16[640,4,128]{2,1,0:T(4,128)(2,1)} %bitcast.8), calls=%async_computation.2 | async-start | bytes 1310720 | tf_op jit(solution)/shard_map/all_to_all | solution.py:312
  139.2 1.1 copy-start.3
  (4 other events, 4.0 us)

commit v6 on v5

--- a/solution.py
+++ b/solution.py
@@ -213,21 +213,14 @@
         out_ref[col ^ k] = (l_ref[col ^ k].astype(F32) + part[...].astype(F32)).astype(BF16)
 
 
-def combine_kernel(
-    y_ref, s_hbm, partner_col, out_hbm, wide, ycat, both, packed, sems_in, sems_out
-):
+def combine_kernel(y_ref, both, partner_col, out_hbm, wide, ycat, packed, sems):
     ncol, slots, nb = both.shape
-    fetches = pieces(s_hbm, both, sems_in, ncol)
-    for copy in fetches:
-        copy.start()
-    stores = pieces(packed, out_hbm, sems_out, sems_out.shape[0])
+    stores = pieces(packed, out_hbm, sems, sems.shape[0])
     wide[...] = y_ref[...].astype(F32)
     for d in range(ncol):
         ycat[:, d * nb : (d + 1) * nb] = wide[pl.ds(d, slots, stride=ncol), :].astype(BF16)
     pick = partner_col[...] == lax.broadcasted_iota(jnp.int32, (slots, slots), 1)
     total = dot(pick.astype(BF16), ycat[...])
-    for copy in fetches:
-        copy.wait()
     part = slots // len(stores)
     for i, store in enumerate(stores):
         at = slice(i * part, (i + 1) * part)
@@ -386,14 +379,12 @@
         [
             pltpu.VMEM((slots * ncol, nb), F32),
             pltpu.VMEM((slots, nvirt), BF16),
-            pltpu.VMEM((ncol, slots, nb), BF16),
             pltpu.VMEM((nb * count, nb), BF16),
-            dma((ncol,)),
             dma((2,)),
         ],
-        [VMEM, HBM, VMEM],
+        [VMEM, VMEM, VMEM],
         HBM,
-    )(y, stay(both_terms), partner_col)
+    )(y, both_terms, partner_col)
     z = exchange(back)
     own_pairs = lax.dynamic_slice_in_dim(slot_pair, pair * slot_dev, slot_dev)
     occ_iota = jnp.arange(nocc, dtype=jnp.int32)

time: 180 us -> 179 us (level)
    unnamed x32 -> x30, local copies, waits for them, and re-layouts: 7.47 us -> 6.62 us
where the time goes in v6:
time: 179 us; the launch traced here: 178 us
  waiting for transfers between devices  83.9 us (47%)
  starting transfers between devices  66.9 us (37%)
  Pallas kernels  19.3 us (11%)
  local copies, waits for them, and re-layouts  6.98 us (4%)
    all_to_all x3, waiting for transfers between devices, exchange(): got = lax.all_to_all(sent, 'pair', split_axis=0, concat_axis=0, tiled=True)  47.6 us
    all_to_all x3, starting transfers between devices, exchange(): got = lax.all_to_all(sent, 'pair', split_axis=0, concat_axis=0, tiled=True)  44.6 us
    ppermute x9, waiting for transfers between devices, swap(): return lax.ppermute(value, 'col', [(i, i ^ k) for i in range(ncol)])  36.3 us
    ppermute x9, starting transfers between devices, swap(): return lax.ppermute(value, 'col', [(i, i ^ k) for i in range(ncol)])  22.3 us
    unnamed x30, local copies, waits for them, and re-layouts  6.62 us
    pallas_call x1, Pallas kernels, update_of(): call(rows_kernel, shape((nb * count, nb), BF16), [pltpu.VMEM((nb, 2 * nvi...  5.32 us
    pallas_call x1, Pallas kernels, update_of(): call(cols_kernel, shape(amplitudes.shape, BF16), [pltpu.VMEM((nvirt, 2 *...  3.71 us
  transfers between devices with their start and end apart: 12, of which 7 were waited for; matrix products, arithmetic and copies ran while one was open for 1% of the time, Pallas kernels for 7%

profile of v6, /device:TPU:16, one launch (start us, length us, event | category | flops | bytes accessed | tf_op | source)
XLA Modules:
  0.0 178.4 jit_solution(16193924556720618485)
XLA Ops:
  0.0 2.4 %shard_map.110 = bf16[2560,128]{1,0:T(8,128)(2,1)} custom-call(bf16[5,512,128]{2,1,0:T(8,128)(2,1)} %g0.3), custom_call_target="tpu_custom_call" | custom-call | tf_op jit(solution)/shard_map/pallas_call | solution.py:313
  2.4 20.5 %all-to-all-start.1 = ((bf16[640,4,128]{2,1,0:T(4,128)(2,1)}), bf16[640,4,128]{2,1,0:T(4,128)(2,1)S(1)}, u32[]{:S(2)}, u32[]{:S(2)}) async-start(bf16[640,4,128]{2,1,0:T(4,128)(2,1)} %bitcast.6), calls=%async_computation.1 | async-start | bytes 1310720 | tf_op jit(solution)/shard_map/all_to_all | solution.py:305
  23.0 2.5 %collective-permute-start.1 = (bf16[5,512,128]{2,1,0:T(8,128)(2,1)S(1)}, bf16[5,512,128]{2,1,0:T(8,128)(2,1)S(1)}, u32[]{:S(2)}, u32[]{:S(2)}) collective-permute-start(bf16[5,512,128]{2,1,0:T(8,128)(2,1)S(1)} %copy-done), channel_id=1, source_target_pairs={{0,2},{1,3},{2,0},{3,1},{4,6},{5,7},{6,4},{7,5},{8,10},{9,11},{10,... | collective-permute-start | bytes 1966088 | tf_op jit(solution)/shard_map/ppermute | solution.py:309
  25.5 1.9 %collective-permute-start = (bf16[5,512,128]{2,1,0:T(8,128)(2,1)S(1)}, bf16[5,512,128]{2,1,0:T(8,128)(2,1)S(1)}, u32[]{:S(2)}, u32[]{:S(2)}) collective-permute-start(bf16[5,512,128]{2,1,0:T(8,128)(2,1)S(1)} %copy-done), channel_id=1, source_target_pairs={{0,1},{1,0},{2,3},{3,2},{4,5},{5,4},{6,7},{7,6},{8,9},{9,8},{10,11... | collective-permute-start | bytes 1966088 | tf_op jit(solution)/shard_map/ppermute | solution.py:309
  27.4 19.3 %collective-permute-done.1.g2 = bf16[5,512,128]{2,1,0:T(8,128)(2,1)S(1)} collective-permute-done((bf16[5,512,128]{2,1,0:T(8,128)(2,1)S(1)}, bf16[5,512,128]{2,1,0:T(8,128)(2,1)S(1)}, u32[]{:S(2)}, u32[]{:S(2)}) %collective-permute-start.1) | collective-permute-done | bytes 655392 | tf_op jit(solution)/shard_map/ppermute | solution.py:309
  46.7 1.9 %collective-permute-start.2 = (bf16[5,512,128]{2,1,0:T(8,128)(2,1)S(1)}, bf16[5,512,128]{2,1,0:T(8,128)(2,1)}, u32[]{:S(2)}, u32[]{:S(2)}) collective-permute-start(bf16[5,512,128]{2,1,0:T(8,128)(2,1)S(1)} %collective-permute-done.1.g2), channel_id=1, source_target_pairs={{0,1},{1,0},{2,3},{3,2},{4,5},{5,4},{6,7},{7,6},{8,9},{9,8},{10,11... | collective-permute-start | bytes 1966088 | tf_op jit(solution)/shard_map/ppermute | solution.py:309
  48.7 2.6 %collective-permute-start.4 = (bf16[2,512,128]{2,1,0:T(8,128)(2,1)S(1)}, bf16[2,512,128]{2,1,0:T(8,128)(2,1)S(1)}, u32[]{:S(2)}, u32[]{:S(2)}) collective-permute-start(bf16[2,512,128]{2,1,0:T(8,128)(2,1)S(1)} %pad_maximum_fusion.w0), channel_id=1, source_target_pairs={{0,2},{1,3},{2,0},{3,1},{4,6},{5,7},{6,4},{7,5},{8,10},{9,11},{10,... | collective-permute-start | bytes 786440 | tf_op jit(solution)/shard_map/ppermute | solution.py:309
  51.3 2.1 %collective-permute-start.3 = (bf16[2,512,128]{2,1,0:T(8,128)(2,1)S(1)}, bf16[2,512,128]{2,1,0:T(8,128)(2,1)S(1)}, u32[]{:S(2)}, u32[]{:S(2)}) collective-permute-start(bf16[2,512,128]{2,1,0:T(8,128)(2,1)S(1)} %pad_maximum_fusion.w0), channel_id=1, source_target_pairs={{0,1},{1,0},{2,3},{3,2},{4,5},{5,4},{6,7},{7,6},{8,9},{9,8},{10,11... | collective-permute-start | bytes 786440 | tf_op jit(solution)/shard_map/ppermute | solution.py:309
  53.4 7.5 %collective-permute-done.4.w2 = bf16[2,512,128]{2,1,0:T(8,128)(2,1)S(1)} collective-permute-done((bf16[2,512,128]{2,1,0:T(8,128)(2,1)S(1)}, bf16[2,512,128]{2,1,0:T(8,128)(2,1)S(1)}, u32[]{:S(2)}, u32[]{:S(2)}) %collective-permute-start.4) | collective-permute-done | bytes 262176 | tf_op jit(solution)/shard_map/ppermute | solution.py:309
  61.0 1.9 %collective-permute-start.5 = (bf16[2,512,128]{2,1,0:T(8,128)(2,1)S(1)}, bf16[2,512,128]{2,1,0:T(8,128)(2,1)}, u32[]{:S(2)}, u32[]{:S(2)}) collective-permute-start(bf16[2,512,128]{2,1,0:T(8,128)(2,1)S(1)} %collective-permute-done.4.w2), channel_id=1, source_target_pairs={{0,1},{1,0},{2,3},{3,2},{4,5},{5,4},{6,7},{7,6},{8,9},{9,8},{10,11... | collective-permute-start | bytes 786440 | tf_op jit(solution)/shard_map/ppermute | solution.py:309
  66.8 5.3 %shard_map.109 = bf16[2560,128]{1,0:T(8,128)(2,1)} custom-call(s32[1]{0:T(128)} %bitcast.c_ref, bf16[5,512,128]{2,1,0:T(8,128)(2,1)S(1)} %copy-done, bf16[5,512,128]{2,1,0:T(8,128)(2,1)S(1)} %collective-permute-done.g1, bf16[5,512,128]{2,1,0:T(8,128)(2,1)S(1)} %collective-permute-done.1.g2, bf16[5,512,128]{2,1,0:T(8,128)(2,1)} %collective-permute-done.2.g3, ...), custom_call_target="tpu_custom_call" | custom-call | tf_op jit(solution)/shard_map/pallas_call | solution.py:339
  72.2 17.2 %all-to-all-start = ((bf16[640,4,128]{2,1,0:T(4,128)(2,1)}), bf16[640,4,128]{2,1,0:T(4,128)(2,1)S(1)}, u32[]{:S(2)}, u32[]{:S(2)}) async-start(bf16[640,4,128]{2,1,0:T(4,128)(2,1)} %bitcast.3), calls=%async_computation | async-start | bytes 1310720 | tf_op jit(solution)/shard_map/all_to_all | solution.py:305
  90.8 2.4 %shard_map.111 = (bf16[640,640]{1,0:T(8,128)(2,1)S(1)}, bf16[640,640]{1,0:T(8,128)(2,1)S(1)}) custom-call(s32[640,1]{1,0:T(8,128)S(1)} %reshape.65.pair_col, s32[1,640]{1,0:T(1,128)S(1)} %reshape.61.pair_row, s32[640,1]{1,0:T(8,128)S(1)} %reshape.66.partner_col, bf16[576,576]{1,0:T(8,128)(2,1)S(1)} %copy-done.7), custom_call_target="tpu_custom_call" | custom-call | tf_op jit(solution)/shard_map/pallas_call | solution.py:330
  94.9 1.9 %collective-permute-start.6 = (bf16[640,128]{1,0:T(8,128)(2,1)S(1)}, bf16[640,128]{1,0:T(8,128)(2,1)S(1)}, u32[]{:S(2)}, u32[]{:S(2)}) collective-permute-start(bf16[640,128]{1,0:T(8,128)(2,1)S(1)} %get-tuple-element.16), channel_id=1, source_target_pairs={{0,1},{1,0},{2,3},{3,2},{4,5},{5,4},{6,7},{7,6},{8,9},{9,8},{10,11... | collective-permute-start | bytes 491528 | tf_op jit(solution)/shard_map/ppermute | solution.py:309
  96.8 2.7 %collective-permute-start.7 = (bf16[640,128]{1,0:T(8,128)(2,1)S(1)}, bf16[640,128]{1,0:T(8,128)(2,1)S(1)}, u32[]{:S(2)}, u32[]{:S(2)}) collective-permute-start(bf16[640,128]{1,0:T(8,128)(2,1)S(1)} %get-tuple-element.17), channel_id=1, source_target_pairs={{0,2},{1,3},{2,0},{3,1},{4,6},{5,7},{6,4},{7,5},{8,10},{9,11},{10,... | collective-permute-start | bytes 491528 | tf_op jit(solution)/shard_map/ppermute | solution.py:309
  99.5 4.6 %collective-permute-start.8 = (bf16[640,128]{1,0:T(8,128)(2,1)S(1)}, bf16[640,128]{1,0:T(8,128)(2,1)S(1)}, u32[]{:S(2)}, u32[]{:S(2)}) collective-permute-start(bf16[640,128]{1,0:T(8,128)(2,1)S(1)} %get-tuple-element.18), channel_id=1, source_target_pairs={{0,3},{1,2},{2,1},{3,0},{4,7},{5,6},{6,5},{7,4},{8,11},{9,10},{10,... | collective-permute-start | bytes 491528 | tf_op jit(solution)/shard_map/ppermute | solution.py:309
  104.2 4.5 %collective-permute-done.7.m2 = bf16[640,128]{1,0:T(8,128)(2,1)S(1)} collective-permute-done((bf16[640,128]{1,0:T(8,128)(2,1)S(1)}, bf16[640,128]{1,0:T(8,128)(2,1)S(1)}, u32[]{:S(2)}, u32[]{:S(2)}) %collective-permute-start.7) | collective-permute-done | bytes 163872 | tf_op jit(solution)/shard_map/ppermute | solution.py:309
  108.6 3.4 %collective-permute-done.8.m3 = bf16[640,128]{1,0:T(8,128)(2,1)S(1)} collective-permute-done((bf16[640,128]{1,0:T(8,128)(2,1)S(1)}, bf16[640,128]{1,0:T(8,128)(2,1)S(1)}, u32[]{:S(2)}, u32[]{:S(2)}) %collective-permute-start.8) | collective-permute-done | bytes 163872 | tf_op jit(solution)/shard_map/ppermute | solution.py:309
  112.2 16.6 %all-to-all-done = bf16[640,4,128]{2,1,0:T(4,128)(2,1)S(1)} async-done(((bf16[640,4,128]{2,1,0:T(4,128)(2,1)}), bf16[640,4,128]{2,1,0:T(4,128)(2,1)S(1)}, u32[]{:S(2)}, u32[]{:S(2)}) %all-to-all-start) | async-done | bytes 655392 | tf_op jit(solution)/shard_map/all_to_all | solution.py:305
  128.8 1.7 shard_map.114
  130.4 6.9 %all-to-all-start.2 = ((bf16[640,4,128]{2,1,0:T(4,128)(2,1)}), bf16[640,4,128]{2,1,0:T(4,128)(2,1)S(1)}, u32[]{:S(2)}, u32[]{:S(2)}) async-start(bf16[640,4,128]{2,1,0:T(4,128)(2,1)} %bitcast.8), calls=%async_computation.2 | async-start | bytes 1310720 | tf_op jit(solution)/shard_map/all_to_all | solution.py:305
  141.4 3.7 %shard_map.115.p_ref = bf16[5,512,128]{2,1,0:T(8,128)(2,1)S(1)} custom-call(s32[1]{0:T(128)} %bitcast.c_ref, bf16[5,512,128]{2,1,0:T(8,128)(2,1)S(1)} %copy-done, bf16[5,512,128]{2,1,0:T(8,128)(2,1)S(1)} %copy-done.2, bf16[5,512,128]{2,1,0:T(8,128)(2,1)S(1)} %collective-permute-done.1.g2, bf16[5,512,128]{2,1,0:T(8,128)(2,1)} %collective-permute-done.2.g3, ...), custom_call_target="tpu_custom_call" | custom-call | tf_op jit(solution)/shard_map/pallas_call | solution.py:356
  145.2 31.1 %all-to-all-done.2 = bf16[640,4,128]{2,1,0:T(4,128)(2,1)S(1)} async-done(((bf16[640,4,128]{2,1,0:T(4,128)(2,1)}), bf16[640,4,128]{2,1,0:T(4,128)(2,1)S(1)}, u32[]{:S(2)}, u32[]{:S(2)}) %all-to-all-start.2) | async-done | bytes 655392 | tf_op jit(solution)/shard_map/all_to_all | solution.py:305
  176.2 2.0 %shard_map.116 = f32[5,512,128]{2,1,0:T(8,128)} custom-call(f32[5]{0:T(128)S(1)} %compare_select_fusion.occ_ref, bf16[2560,128]{1,0:T(8,128)(2,1)S(1)} %bitcast.12, bf16[5,512,128]{2,1,0:T(8,128)(2,1)S(1)} %shard_map.115.p_ref, f32[512,128]{1,0:T(8,128)S(1)} %broadcast_add_fusion.base_ref), custom_call_target="tpu_custom_call" | custom-call | tf_op jit(solution)/shard_map/pallas_call | solution.py:403
  (48 shorter events, 11.1 us)
Async XLA Ops:
  0.0 23.0 %copy-start = (bf16[5,512,128]{2,1,0:T(8,128)(2,1)S(1)}, bf16[5,512,128]{2,1,0:T(8,128)(2,1)}, u32[]{:S(2)}) copy-start(bf16[5,512,128]{2,1,0:T(8,128)(2,1)} %g0.3) | copy-start | bytes 1966084
  0.0 48.6 %copy-start.9 = (bf16[512,128]{1,0:T(8,128)(2,1)S(1)}, bf16[512,128]{1,0:T(8,128)(2,1)}, u32[]{:S(2)}) copy-start(bf16[512,128]{1,0:T(8,128)(2,1)} %param.14) | copy-start | bytes 393220
  0.0 48.6 %copy-start.8 = (bf16[512,128]{1,0:T(8,128)(2,1)S(1)}, bf16[512,128]{1,0:T(8,128)(2,1)}, u32[]{:S(2)}) copy-start(bf16[512,128]{1,0:T(8,128)(2,1)} %param.15) | copy-start | bytes 393220
  2.4 69.7 %all-to-all-start.1 = ((bf16[640,4,128]{2,1,0:T(4,128)(2,1)}), bf16[640,4,128]{2,1,0:T(4,128)(2,1)S(1)}, u32[]{:S(2)}, u32[]{:S(2)}) async-start(bf16[640,4,128]{2,1,0:T(4,128)(2,1)} %bitcast.6), calls=%async_computation.1 | async-start | bytes 1310720 | tf_op jit(solution)/shard_map/all_to_all | solution.py:305
  23.0 23.7 %collective-permute-start.1 = (bf16[5,512,128]{2,1,0:T(8,128)(2,1)S(1)}, bf16[5,512,128]{2,1,0:T(8,128)(2,1)S(1)}, u32[]{:S(2)}, u32[]{:S(2)}) collective-permute-start(bf16[5,512,128]{2,1,0:T(8,128)(2,1)S(1)} %copy-done), channel_id=1, source_target_pairs={{0,2},{1,3},{2,0},{3,1},{4,6},{5,7},{6,4},{7,5},{8,10},{9,11},{10,... | collective-permute-start | bytes 1966088 | tf_op jit(solution)/shard_map/ppermute | solution.py:309
  25.5 39.0 %collective-permute-start = (bf16[5,512,128]{2,1,0:T(8,128)(2,1)S(1)}, bf16[5,512,128]{2,1,0:T(8,128)(2,1)S(1)}, u32[]{:S(2)}, u32[]{:S(2)}) collective-permute-start(bf16[5,512,128]{2,1,0:T(8,128)(2,1)S(1)} %copy-done), channel_id=1, source_target_pairs={{0,1},{1,0},{2,3},{3,2},{4,5},{5,4},{6,7},{7,6},{8,9},{9,8},{10,11... | collective-permute-start | bytes 1966088 | tf_op jit(solution)/shard_map/ppermute | solution.py:309
  46.7 17.8 %collective-permute-start.2 = (bf16[5,512,128]{2,1,0:T(8,128)(2,1)S(1)}, bf16[5,512,128]{2,1,0:T(8,128)(2,1)}, u32[]{:S(2)}, u32[]{:S(2)}) collective-permute-start(bf16[5,512,128]{2,1,0:T(8,128)(2,1)S(1)} %collective-permute-done.1.g2), channel_id=1, source_target_pairs={{0,1},{1,0},{2,3},{3,2},{4,5},{5,4},{6,7},{7,6},{8,9},{9,8},{10,11... | collective-permute-start | bytes 1966088 | tf_op jit(solution)/shard_map/ppermute | solution.py:309
  48.7 12.3 %collective-permute-start.4 = (bf16[2,512,128]{2,1,0:T(8,128)(2,1)S(1)}, bf16[2,512,128]{2,1,0:T(8,128)(2,1)S(1)}, u32[]{:S(2)}, u32[]{:S(2)}) collective-permute-start(bf16[2,512,128]{2,1,0:T(8,128)(2,1)S(1)} %pad_maximum_fusion.w0), channel_id=1, source_target_pairs={{0,2},{1,3},{2,0},{3,1},{4,6},{5,7},{6,4},{7,5},{8,10},{9,11},{10,... | collective-permute-start | bytes 786440 | tf_op jit(solution)/shard_map/ppermute | solution.py:309
  51.3 11.6 %collective-permute-start.3 = (bf16[2,512,128]{2,1,0:T(8,128)(2,1)S(1)}, bf16[2,512,128]{2,1,0:T(8,128)(2,1)S(1)}, u32[]{:S(2)}, u32[]{:S(2)}) collective-permute-start(bf16[2,512,128]{2,1,0:T(8,128)(2,1)S(1)} %pad_maximum_fusion.w0), channel_id=1, source_target_pairs={{0,1},{1,0},{2,3},{3,2},{4,5},{5,4},{6,7},{7,6},{8,9},{9,8},{10,11... | collective-permute-start | bytes 786440 | tf_op jit(solution)/shard_map/ppermute | solution.py:309
  61.0 3.6 %collective-permute-start.5 = (bf16[2,512,128]{2,1,0:T(8,128)(2,1)S(1)}, bf16[2,512,128]{2,1,0:T(8,128)(2,1)}, u32[]{:S(2)}, u32[]{:S(2)}) collective-permute-start(bf16[2,512,128]{2,1,0:T(8,128)(2,1)S(1)} %collective-permute-done.4.w2), channel_id=1, source_target_pairs={{0,1},{1,0},{2,3},{3,2},{4,5},{5,4},{6,7},{7,6},{8,9},{9,8},{10,11... | collective-permute-start | bytes 786440 | tf_op jit(solution)/shard_map/ppermute | solution.py:309
  64.5 7.7 %copy-start.1 = (bf16[5,512,128]{2,1,0:T(8,128)(2,1)}, bf16[5,512,128]{2,1,0:T(8,128)(2,1)S(1)}, u32[]{:S(2)}) copy-start(bf16[5,512,128]{2,1,0:T(8,128)(2,1)S(1)} %collective-permute-done.g1) | copy-start | bytes 1966084
  64.5 1.3 copy-start.3
  72.2 17.2 %copy-start.10 = (s32[640]{0:T(1024)S(1)}, s32[640]{0:T(1024)}, u32[]{:S(2)}) copy-start(s32[640]{0:T(1024)} %param.17) | copy-start | bytes 7684
  72.2 17.4 %copy-start.11 = (s32[640]{0:T(1024)S(1)}, s32[640]{0:T(1024)}, u32[]{:S(2)}) copy-start(s32[640]{0:T(1024)} %param.18) | copy-start | bytes 7684
  72.2 56.6 %all-to-all-start = ((bf16[640,4,128]{2,1,0:T(4,128)(2,1)}), bf16[640,4,128]{2,1,0:T(4,128)(2,1)S(1)}, u32[]{:S(2)}, u32[]{:S(2)}) async-start(bf16[640,4,128]{2,1,0:T(4,128)(2,1)} %bitcast.3), calls=%async_computation | async-start | bytes 1310720 | tf_op jit(solution)/shard_map/all_to_all | solution.py:305
  89.7 1.1 copy-start.7
  94.9 9.3 %collective-permute-start.6 = (bf16[640,128]{1,0:T(8,128)(2,1)S(1)}, bf16[640,128]{1,0:T(8,128)(2,1)S(1)}, u32[]{:S(2)}, u32[]{:S(2)}) collective-permute-start(bf16[640,128]{1,0:T(8,128)(2,1)S(1)} %get-tuple-element.16), channel_id=1, source_target_pairs={{0,1},{1,0},{2,3},{3,2},{4,5},{5,4},{6,7},{7,6},{8,9},{9,8},{10,11... | collective-permute-start | bytes 491528 | tf_op jit(solution)/shard_map/ppermute | solution.py:309
  96.8 11.9 %collective-permute-start.7 = (bf16[640,128]{1,0:T(8,128)(2,1)S(1)}, bf16[640,128]{1,0:T(8,128)(2,1)S(1)}, u32[]{:S(2)}, u32[]{:S(2)}) collective-permute-start(bf16[640,128]{1,0:T(8,128)(2,1)S(1)} %get-tuple-element.17), channel_id=1, source_target_pairs={{0,2},{1,3},{2,0},{3,1},{4,6},{5,7},{6,4},{7,5},{8,10},{9,11},{10,... | collective-permute-start | bytes 491528 | tf_op jit(solution)/shard_map/ppermute | solution.py:309
  99.5 12.5 %collective-permute-start.8 = (bf16[640,128]{1,0:T(8,128)(2,1)S(1)}, bf16[640,128]{1,0:T(8,128)(2,1)S(1)}, u32[]{:S(2)}, u32[]{:S(2)}) collective-permute-start(bf16[640,128]{1,0:T(8,128)(2,1)S(1)} %get-tuple-element.18), channel_id=1, source_target_pairs={{0,3},{1,2},{2,1},{3,0},{4,7},{5,6},{6,5},{7,4},{8,11},{9,10},{10,... | collective-permute-start | bytes 491528 | tf_op jit(solution)/shard_map/ppermute | solution.py:309
  128.8 8.6 %copy-start.12 = (f32[512]{0:T(512)S(1)}, f32[512]{0:T(512)}, u32[]{:S(2)}) copy-start(f32[512]{0:T(512)} %param.20) | copy-start | bytes 6148
  128.8 8.6 %copy-start.13 = (s32[512]{0:T(512)S(1)}, s32[512]{0:T(512)}, u32[]{:S(2)}) copy-start(s32[512]{0:T(512)} %param.21) | copy-start | bytes 6148
  128.8 9.0 %copy-start.14 = (f32[24]{0:T(128)S(1)}, f32[24]{0:T(128)}, u32[]{:S(2)}) copy-start(f32[24]{0:T(128)} %param.19) | copy-start | bytes 292
  130.4 45.8 %all-to-all-start.2 = ((bf16[640,4,128]{2,1,0:T(4,128)(2,1)}), bf16[640,4,128]{2,1,0:T(4,128)(2,1)S(1)}, u32[]{:S(2)}, u32[]{:S(2)}) async-start(bf16[640,4,128]{2,1,0:T(4,128)(2,1)} %bitcast.8), calls=%async_computation.2 | async-start | bytes 1310720 | tf_op jit(solution)/shard_map/all_to_all | solution.py:305
  138.3 1.1 copy-start.2
  (3 other events, 3.1 us)

commit v7 on v6

--- a/solution.py
+++ b/solution.py
@@ -239,7 +239,12 @@
     nslot, nvirt, nb = p_ref.shape
     ncol = nvirt // nb
     flat[: z_ref.shape[0], :] = z_ref[...].astype(F32)
-    copies = [pltpu.make_async_copy(stage.at[s], out_hbm.at[s], sems.at[s]) for s in range(nslot)]
+    copies = []
+    for block in range(nslot * ncol):
+        s, rows = block // ncol, pl.ds(block % ncol * nb, nb)
+        copies.append(
+            pltpu.make_async_copy(stage.at[s, rows], out_hbm.at[s, rows], sems.at[block])
+        )
 
     def done(start, size):
         for s in range(start // ncol, (start + size) // ncol):
@@ -248,7 +253,7 @@
                 rows = slice(d * nb, (d + 1) * nb)
                 total = p_ref[s, rows, :].astype(F32) + target[at : at + nb, :]
                 stage[s, rows, :] = total / (base_ref[rows, :] - occ_ref[s])
-            copies[s].start()
+                copies[s * ncol + d].start()
 
     unskew(flat, middle, target, nb, nslot * ncol, done)
     for copy in copies:
@@ -403,7 +408,7 @@
     return call(
         finish_kernel,
         shape(amplitudes.shape, F32),
-        [pltpu.VMEM(amplitudes.shape, F32), dma((slot_dev,))] + skew_scratch(count, nb),
+        [pltpu.VMEM(amplitudes.shape, F32), dma((count,))] + skew_scratch(count, nb),
         [SMEM] + [VMEM] * 3,
         HBM,
     )(occ_sum, z, particle, base)

time: 179 us -> 179 us (level)
  no operation moved by 1% of the time
where the time goes in v7:
time: 179 us; the launch traced here: 178 us
  waiting for transfers between devices  83.9 us (47%)
  starting transfers between devices  66.9 us (37%)
  Pallas kernels  19.4 us (11%)
  local copies, waits for them, and re-layouts  6.98 us (4%)
    all_to_all x3, waiting for transfers between devices, exchange(): got = lax.all_to_all(sent, 'pair', split_axis=0, concat_axis=0, tiled=True)  47.6 us
    all_to_all x3, starting transfers between devices, exchange(): got = lax.all_to_all(sent, 'pair', split_axis=0, concat_axis=0, tiled=True)  44.6 us
    ppermute x9, waiting for transfers between devices, swap(): return lax.ppermute(value, 'col', [(i, i ^ k) for i in range(ncol)])  36.3 us
    ppermute x9, starting transfers between devices, swap(): return lax.ppermute(value, 'col', [(i, i ^ k) for i in range(ncol)])  22.3 us
    unnamed x30, local copies, waits for them, and re-layouts  6.62 us
    pallas_call x1, Pallas kernels, update_of(): call(rows_kernel, shape((nb * count, nb), BF16), [pltpu.VMEM((nb, 2 * nvi...  5.32 us
    pallas_call x1, Pallas kernels, update_of(): call(cols_kernel, shape(amplitudes.shape, BF16), [pltpu.VMEM((nvirt, 2 *...  3.71 us
  transfers between devices with their start and end apart: 12, of which 7 were waited for; matrix products, arithmetic and copies ran while one was open for 1% of the time, Pallas kernels for 7%

profile of v7, /device:TPU:16, one launch (start us, length us, event | category | flops | bytes accessed | tf_op | source)
XLA Modules:
  0.0 178.5 jit_solution(4848375886189923264)
XLA Ops:
  0.0 2.4 %shard_map.110 = bf16[2560,128]{1,0:T(8,128)(2,1)} custom-call(bf16[5,512,128]{2,1,0:T(8,128)(2,1)} %g0.3), custom_call_target="tpu_custom_call" | custom-call | tf_op jit(solution)/shard_map/pallas_call | solution.py:318
  2.4 20.5 %all-to-all-start.1 = ((bf16[640,4,128]{2,1,0:T(4,128)(2,1)}), bf16[640,4,128]{2,1,0:T(4,128)(2,1)S(1)}, u32[]{:S(2)}, u32[]{:S(2)}) async-start(bf16[640,4,128]{2,1,0:T(4,128)(2,1)} %bitcast.6), calls=%async_computation.1 | async-start | bytes 1310720 | tf_op jit(solution)/shard_map/all_to_all | solution.py:310
  23.0 2.5 %collective-permute-start.1 = (bf16[5,512,128]{2,1,0:T(8,128)(2,1)S(1)}, bf16[5,512,128]{2,1,0:T(8,128)(2,1)S(1)}, u32[]{:S(2)}, u32[]{:S(2)}) collective-permute-start(bf16[5,512,128]{2,1,0:T(8,128)(2,1)S(1)} %copy-done), channel_id=1, source_target_pairs={{0,2},{1,3},{2,0},{3,1},{4,6},{5,7},{6,4},{7,5},{8,10},{9,11},{10,... | collective-permute-start | bytes 1966088 | tf_op jit(solution)/shard_map/ppermute | solution.py:314
  25.5 1.9 %collective-permute-start = (bf16[5,512,128]{2,1,0:T(8,128)(2,1)S(1)}, bf16[5,512,128]{2,1,0:T(8,128)(2,1)S(1)}, u32[]{:S(2)}, u32[]{:S(2)}) collective-permute-start(bf16[5,512,128]{2,1,0:T(8,128)(2,1)S(1)} %copy-done), channel_id=1, source_target_pairs={{0,1},{1,0},{2,3},{3,2},{4,5},{5,4},{6,7},{7,6},{8,9},{9,8},{10,11... | collective-permute-start | bytes 1966088 | tf_op jit(solution)/shard_map/ppermute | solution.py:314
  27.4 19.3 %collective-permute-done.1.g2 = bf16[5,512,128]{2,1,0:T(8,128)(2,1)S(1)} collective-permute-done((bf16[5,512,128]{2,1,0:T(8,128)(2,1)S(1)}, bf16[5,512,128]{2,1,0:T(8,128)(2,1)S(1)}, u32[]{:S(2)}, u32[]{:S(2)}) %collective-permute-start.1) | collective-permute-done | bytes 655392 | tf_op jit(solution)/shard_map/ppermute | solution.py:314
  46.7 1.9 %collective-permute-start.2 = (bf16[5,512,128]{2,1,0:T(8,128)(2,1)S(1)}, bf16[5,512,128]{2,1,0:T(8,128)(2,1)}, u32[]{:S(2)}, u32[]{:S(2)}) collective-permute-start(bf16[5,512,128]{2,1,0:T(8,128)(2,1)S(1)} %collective-permute-done.1.g2), channel_id=1, source_target_pairs={{0,1},{1,0},{2,3},{3,2},{4,5},{5,4},{6,7},{7,6},{8,9},{9,8},{10,11... | collective-permute-start | bytes 1966088 | tf_op jit(solution)/shard_map/ppermute | solution.py:314
  48.7 2.6 %collective-permute-start.4 = (bf16[2,512,128]{2,1,0:T(8,128)(2,1)S(1)}, bf16[2,512,128]{2,1,0:T(8,128)(2,1)S(1)}, u32[]{:S(2)}, u32[]{:S(2)}) collective-permute-start(bf16[2,512,128]{2,1,0:T(8,128)(2,1)S(1)} %pad_maximum_fusion.w0), channel_id=1, source_target_pairs={{0,2},{1,3},{2,0},{3,1},{4,6},{5,7},{6,4},{7,5},{8,10},{9,11},{10,... | collective-permute-start | bytes 786440 | tf_op jit(solution)/shard_map/ppermute | solution.py:314
  51.3 2.1 %collective-permute-start.3 = (bf16[2,512,128]{2,1,0:T(8,128)(2,1)S(1)}, bf16[2,512,128]{2,1,0:T(8,128)(2,1)S(1)}, u32[]{:S(2)}, u32[]{:S(2)}) collective-permute-start(bf16[2,512,128]{2,1,0:T(8,128)(2,1)S(1)} %pad_maximum_fusion.w0), channel_id=1, source_target_pairs={{0,1},{1,0},{2,3},{3,2},{4,5},{5,4},{6,7},{7,6},{8,9},{9,8},{10,11... | collective-permute-start | bytes 786440 | tf_op jit(solution)/shard_map/ppermute | solution.py:314
  53.4 7.5 %collective-permute-done.4.w2 = bf16[2,512,128]{2,1,0:T(8,128)(2,1)S(1)} collective-permute-done((bf16[2,512,128]{2,1,0:T(8,128)(2,1)S(1)}, bf16[2,512,128]{2,1,0:T(8,128)(2,1)S(1)}, u32[]{:S(2)}, u32[]{:S(2)}) %collective-permute-start.4) | collective-permute-done | bytes 262176 | tf_op jit(solution)/shard_map/ppermute | solution.py:314
  61.0 1.9 %collective-permute-start.5 = (bf16[2,512,128]{2,1,0:T(8,128)(2,1)S(1)}, bf16[2,512,128]{2,1,0:T(8,128)(2,1)}, u32[]{:S(2)}, u32[]{:S(2)}) collective-permute-start(bf16[2,512,128]{2,1,0:T(8,128)(2,1)S(1)} %collective-permute-done.4.w2), channel_id=1, source_target_pairs={{0,1},{1,0},{2,3},{3,2},{4,5},{5,4},{6,7},{7,6},{8,9},{9,8},{10,11... | collective-permute-start | bytes 786440 | tf_op jit(solution)/shard_map/ppermute | solution.py:314
  66.8 5.3 %shard_map.109 = bf16[2560,128]{1,0:T(8,128)(2,1)} custom-call(s32[1]{0:T(128)} %bitcast.c_ref, bf16[5,512,128]{2,1,0:T(8,128)(2,1)S(1)} %copy-done, bf16[5,512,128]{2,1,0:T(8,128)(2,1)S(1)} %collective-permute-done.g1, bf16[5,512,128]{2,1,0:T(8,128)(2,1)S(1)} %collective-permute-done.1.g2, bf16[5,512,128]{2,1,0:T(8,128)(2,1)} %collective-permute-done.2.g3, ...), custom_call_target="tpu_custom_call" | custom-call | tf_op jit(solution)/shard_map/pallas_call | solution.py:344
  72.2 17.2 %all-to-all-start = ((bf16[640,4,128]{2,1,0:T(4,128)(2,1)}), bf16[640,4,128]{2,1,0:T(4,128)(2,1)S(1)}, u32[]{:S(2)}, u32[]{:S(2)}) async-start(bf16[640,4,128]{2,1,0:T(4,128)(2,1)} %bitcast.3), calls=%async_computation | async-start | bytes 1310720 | tf_op jit(solution)/shard_map/all_to_all | solution.py:310
  90.8 2.4 %shard_map.111 = (bf16[640,640]{1,0:T(8,128)(2,1)S(1)}, bf16[640,640]{1,0:T(8,128)(2,1)S(1)}) custom-call(s32[640,1]{1,0:T(8,128)S(1)} %reshape.65.pair_col, s32[1,640]{1,0:T(1,128)S(1)} %reshape.61.pair_row, s32[640,1]{1,0:T(8,128)S(1)} %reshape.66.partner_col, bf16[576,576]{1,0:T(8,128)(2,1)S(1)} %copy-done.7), custom_call_target="tpu_custom_call" | custom-call | tf_op jit(solution)/shard_map/pallas_call | solution.py:335
  94.9 1.9 %collective-permute-start.6 = (bf16[640,128]{1,0:T(8,128)(2,1)S(1)}, bf16[640,128]{1,0:T(8,128)(2,1)S(1)}, u32[]{:S(2)}, u32[]{:S(2)}) collective-permute-start(bf16[640,128]{1,0:T(8,128)(2,1)S(1)} %get-tuple-element.16), channel_id=1, source_target_pairs={{0,1},{1,0},{2,3},{3,2},{4,5},{5,4},{6,7},{7,6},{8,9},{9,8},{10,11... | collective-permute-start | bytes 491528 | tf_op jit(solution)/shard_map/ppermute | solution.py:314
  96.8 2.7 %collective-permute-start.7 = (bf16[640,128]{1,0:T(8,128)(2,1)S(1)}, bf16[640,128]{1,0:T(8,128)(2,1)S(1)}, u32[]{:S(2)}, u32[]{:S(2)}) collective-permute-start(bf16[640,128]{1,0:T(8,128)(2,1)S(1)} %get-tuple-element.17), channel_id=1, source_target_pairs={{0,2},{1,3},{2,0},{3,1},{4,6},{5,7},{6,4},{7,5},{8,10},{9,11},{10,... | collective-permute-start | bytes 491528 | tf_op jit(solution)/shard_map/ppermute | solution.py:314
  99.5 4.6 %collective-permute-start.8 = (bf16[640,128]{1,0:T(8,128)(2,1)S(1)}, bf16[640,128]{1,0:T(8,128)(2,1)S(1)}, u32[]{:S(2)}, u32[]{:S(2)}) collective-permute-start(bf16[640,128]{1,0:T(8,128)(2,1)S(1)} %get-tuple-element.18), channel_id=1, source_target_pairs={{0,3},{1,2},{2,1},{3,0},{4,7},{5,6},{6,5},{7,4},{8,11},{9,10},{10,... | collective-permute-start | bytes 491528 | tf_op jit(solution)/shard_map/ppermute | solution.py:314
  104.2 4.5 %collective-permute-done.7.m2 = bf16[640,128]{1,0:T(8,128)(2,1)S(1)} collective-permute-done((bf16[640,128]{1,0:T(8,128)(2,1)S(1)}, bf16[640,128]{1,0:T(8,128)(2,1)S(1)}, u32[]{:S(2)}, u32[]{:S(2)}) %collective-permute-start.7) | collective-permute-done | bytes 163872 | tf_op jit(solution)/shard_map/ppermute | solution.py:314
  108.6 3.4 %collective-permute-done.8.m3 = bf16[640,128]{1,0:T(8,128)(2,1)S(1)} collective-permute-done((bf16[640,128]{1,0:T(8,128)(2,1)S(1)}, bf16[640,128]{1,0:T(8,128)(2,1)S(1)}, u32[]{:S(2)}, u32[]{:S(2)}) %collective-permute-start.8) | collective-permute-done | bytes 163872 | tf_op jit(solution)/shard_map/ppermute | solution.py:314
  112.2 16.6 %all-to-all-done = bf16[640,4,128]{2,1,0:T(4,128)(2,1)S(1)} async-done(((bf16[640,4,128]{2,1,0:T(4,128)(2,1)}), bf16[640,4,128]{2,1,0:T(4,128)(2,1)S(1)}, u32[]{:S(2)}, u32[]{:S(2)}) %all-to-all-start) | async-done | bytes 655392 | tf_op jit(solution)/shard_map/all_to_all | solution.py:310
  128.8 1.7 shard_map.114
  130.4 6.9 %all-to-all-start.2 = ((bf16[640,4,128]{2,1,0:T(4,128)(2,1)}), bf16[640,4,128]{2,1,0:T(4,128)(2,1)S(1)}, u32[]{:S(2)}, u32[]{:S(2)}) async-start(bf16[640,4,128]{2,1,0:T(4,128)(2,1)} %bitcast.8), calls=%async_computation.2 | async-start | bytes 1310720 | tf_op jit(solution)/shard_map/all_to_all | solution.py:310
  141.4 3.7 %shard_map.115.p_ref = bf16[5,512,128]{2,1,0:T(8,128)(2,1)S(1)} custom-call(s32[1]{0:T(128)} %bitcast.c_ref, bf16[5,512,128]{2,1,0:T(8,128)(2,1)S(1)} %copy-done, bf16[5,512,128]{2,1,0:T(8,128)(2,1)S(1)} %copy-done.2, bf16[5,512,128]{2,1,0:T(8,128)(2,1)S(1)} %collective-permute-done.1.g2, bf16[5,512,128]{2,1,0:T(8,128)(2,1)} %collective-permute-done.2.g3, ...), custom_call_target="tpu_custom_call" | custom-call | tf_op jit(solution)/shard_map/pallas_call | solution.py:361
  145.2 31.1 %all-to-all-done.2 = bf16[640,4,128]{2,1,0:T(4,128)(2,1)S(1)} async-done(((bf16[640,4,128]{2,1,0:T(4,128)(2,1)}), bf16[640,4,128]{2,1,0:T(4,128)(2,1)S(1)}, u32[]{:S(2)}, u32[]{:S(2)}) %all-to-all-start.2) | async-done | bytes 655392 | tf_op jit(solution)/shard_map/all_to_all | solution.py:310
  176.2 2.1 %shard_map.116 = f32[5,512,128]{2,1,0:T(8,128)} custom-call(f32[5]{0:T(128)S(1)} %compare_select_fusion.occ_ref, bf16[2560,128]{1,0:T(8,128)(2,1)S(1)} %bitcast.12, bf16[5,512,128]{2,1,0:T(8,128)(2,1)S(1)} %shard_map.115.p_ref, f32[512,128]{1,0:T(8,128)S(1)} %broadcast_add_fusion.base_ref), custom_call_target="tpu_custom_call" | custom-call | tf_op jit(solution)/shard_map/pallas_call | solution.py:408
  (48 shorter events, 11.1 us)
Async XLA Ops:
  0.0 23.0 %copy-start = (bf16[5,512,128]{2,1,0:T(8,128)(2,1)S(1)}, bf16[5,512,128]{2,1,0:T(8,128)(2,1)}, u32[]{:S(2)}) copy-start(bf16[5,512,128]{2,1,0:T(8,128)(2,1)} %g0.3) | copy-start | bytes 1966084
  0.0 48.6 %copy-start.9 = (bf16[512,128]{1,0:T(8,128)(2,1)S(1)}, bf16[512,128]{1,0:T(8,128)(2,1)}, u32[]{:S(2)}) copy-start(bf16[512,128]{1,0:T(8,128)(2,1)} %param.14) | copy-start | bytes 393220
  0.0 48.6 %copy-start.8 = (bf16[512,128]{1,0:T(8,128)(2,1)S(1)}, bf16[512,128]{1,0:T(8,128)(2,1)}, u32[]{:S(2)}) copy-start(bf16[512,128]{1,0:T(8,128)(2,1)} %param.15) | copy-start | bytes 393220
  2.4 69.7 %all-to-all-start.1 = ((bf16[640,4,128]{2,1,0:T(4,128)(2,1)}), bf16[640,4,128]{2,1,0:T(4,128)(2,1)S(1)}, u32[]{:S(2)}, u32[]{:S(2)}) async-start(bf16[640,4,128]{2,1,0:T(4,128)(2,1)} %bitcast.6), calls=%async_computation.1 | async-start | bytes 1310720 | tf_op jit(solution)/shard_map/all_to_all | solution.py:310
  23.0 23.7 %collective-permute-start.1 = (bf16[5,512,128]{2,1,0:T(8,128)(2,1)S(1)}, bf16[5,512,128]{2,1,0:T(8,128)(2,1)S(1)}, u32[]{:S(2)}, u32[]{:S(2)}) collective-permute-start(bf16[5,512,128]{2,1,0:T(8,128)(2,1)S(1)} %copy-done), channel_id=1, source_target_pairs={{0,2},{1,3},{2,0},{3,1},{4,6},{5,7},{6,4},{7,5},{8,10},{9,11},{10,... | collective-permute-start | bytes 1966088 | tf_op jit(solution)/shard_map/ppermute | solution.py:314
  25.5 39.0 %collective-permute-start = (bf16[5,512,128]{2,1,0:T(8,128)(2,1)S(1)}, bf16[5,512,128]{2,1,0:T(8,128)(2,1)S(1)}, u32[]{:S(2)}, u32[]{:S(2)}) collective-permute-start(bf16[5,512,128]{2,1,0:T(8,128)(2,1)S(1)} %copy-done), channel_id=1, source_target_pairs={{0,1},{1,0},{2,3},{3,2},{4,5},{5,4},{6,7},{7,6},{8,9},{9,8},{10,11... | collective-permute-start | bytes 1966088 | tf_op jit(solution)/shard_map/ppermute | solution.py:314
  46.7 17.8 %collective-permute-start.2 = (bf16[5,512,128]{2,1,0:T(8,128)(2,1)S(1)}, bf16[5,512,128]{2,1,0:T(8,128)(2,1)}, u32[]{:S(2)}, u32[]{:S(2)}) collective-permute-start(bf16[5,512,128]{2,1,0:T(8,128)(2,1)S(1)} %collective-permute-done.1.g2), channel_id=1, source_target_pairs={{0,1},{1,0},{2,3},{3,2},{4,5},{5,4},{6,7},{7,6},{8,9},{9,8},{10,11... | collective-permute-start | bytes 1966088 | tf_op jit(solution)/shard_map/ppermute | solution.py:314
  48.7 12.3 %collective-permute-start.4 = (bf16[2,512,128]{2,1,0:T(8,128)(2,1)S(1)}, bf16[2,512,128]{2,1,0:T(8,128)(2,1)S(1)}, u32[]{:S(2)}, u32[]{:S(2)}) collective-permute-start(bf16[2,512,128]{2,1,0:T(8,128)(2,1)S(1)} %pad_maximum_fusion.w0), channel_id=1, source_target_pairs={{0,2},{1,3},{2,0},{3,1},{4,6},{5,7},{6,4},{7,5},{8,10},{9,11},{10,... | collective-permute-start | bytes 786440 | tf_op jit(solution)/shard_map/ppermute | solution.py:314
  51.3 11.6 %collective-permute-start.3 = (bf16[2,512,128]{2,1,0:T(8,128)(2,1)S(1)}, bf16[2,512,128]{2,1,0:T(8,128)(2,1)S(1)}, u32[]{:S(2)}, u32[]{:S(2)}) collective-permute-start(bf16[2,512,128]{2,1,0:T(8,128)(2,1)S(1)} %pad_maximum_fusion.w0), channel_id=1, source_target_pairs={{0,1},{1,0},{2,3},{3,2},{4,5},{5,4},{6,7},{7,6},{8,9},{9,8},{10,11... | collective-permute-start | bytes 786440 | tf_op jit(solution)/shard_map/ppermute | solution.py:314
  61.0 3.6 %collective-permute-start.5 = (bf16[2,512,128]{2,1,0:T(8,128)(2,1)S(1)}, bf16[2,512,128]{2,1,0:T(8,128)(2,1)}, u32[]{:S(2)}, u32[]{:S(2)}) collective-permute-start(bf16[2,512,128]{2,1,0:T(8,128)(2,1)S(1)} %collective-permute-done.4.w2), channel_id=1, source_target_pairs={{0,1},{1,0},{2,3},{3,2},{4,5},{5,4},{6,7},{7,6},{8,9},{9,8},{10,11... | collective-permute-start | bytes 786440 | tf_op jit(solution)/shard_map/ppermute | solution.py:314
  64.5 7.7 %copy-start.1 = (bf16[5,512,128]{2,1,0:T(8,128)(2,1)}, bf16[5,512,128]{2,1,0:T(8,128)(2,1)S(1)}, u32[]{:S(2)}) copy-start(bf16[5,512,128]{2,1,0:T(8,128)(2,1)S(1)} %collective-permute-done.g1) | copy-start | bytes 1966084
  64.5 1.3 copy-start.3
  72.2 17.2 %copy-start.10 = (s32[640]{0:T(1024)S(1)}, s32[640]{0:T(1024)}, u32[]{:S(2)}) copy-start(s32[640]{0:T(1024)} %param.17) | copy-start | bytes 7684
  72.2 17.4 %copy-start.11 = (s32[640]{0:T(1024)S(1)}, s32[640]{0:T(1024)}, u32[]{:S(2)}) copy-start(s32[640]{0:T(1024)} %param.18) | copy-start | bytes 7684
  72.2 56.6 %all-to-all-start = ((bf16[640,4,128]{2,1,0:T(4,128)(2,1)}), bf16[640,4,128]{2,1,0:T(4,128)(2,1)S(1)}, u32[]{:S(2)}, u32[]{:S(2)}) async-start(bf16[640,4,128]{2,1,0:T(4,128)(2,1)} %bitcast.3), calls=%async_computation | async-start | bytes 1310720 | tf_op jit(solution)/shard_map/all_to_all | solution.py:310
  89.7 1.1 copy-start.7
  94.9 9.3 %collective-permute-start.6 = (bf16[640,128]{1,0:T(8,128)(2,1)S(1)}, bf16[640,128]{1,0:T(8,128)(2,1)S(1)}, u32[]{:S(2)}, u32[]{:S(2)}) collective-permute-start(bf16[640,128]{1,0:T(8,128)(2,1)S(1)} %get-tuple-element.16), channel_id=1, source_target_pairs={{0,1},{1,0},{2,3},{3,2},{4,5},{5,4},{6,7},{7,6},{8,9},{9,8},{10,11... | collective-permute-start | bytes 491528 | tf_op jit(solution)/shard_map/ppermute | solution.py:314
  96.8 11.9 %collective-permute-start.7 = (bf16[640,128]{1,0:T(8,128)(2,1)S(1)}, bf16[640,128]{1,0:T(8,128)(2,1)S(1)}, u32[]{:S(2)}, u32[]{:S(2)}) collective-permute-start(bf16[640,128]{1,0:T(8,128)(2,1)S(1)} %get-tuple-element.17), channel_id=1, source_target_pairs={{0,2},{1,3},{2,0},{3,1},{4,6},{5,7},{6,4},{7,5},{8,10},{9,11},{10,... | collective-permute-start | bytes 491528 | tf_op jit(solution)/shard_map/ppermute | solution.py:314
  99.5 12.5 %collective-permute-start.8 = (bf16[640,128]{1,0:T(8,128)(2,1)S(1)}, bf16[640,128]{1,0:T(8,128)(2,1)S(1)}, u32[]{:S(2)}, u32[]{:S(2)}) collective-permute-start(bf16[640,128]{1,0:T(8,128)(2,1)S(1)} %get-tuple-element.18), channel_id=1, source_target_pairs={{0,3},{1,2},{2,1},{3,0},{4,7},{5,6},{6,5},{7,4},{8,11},{9,10},{10,... | collective-permute-start | bytes 491528 | tf_op jit(solution)/shard_map/ppermute | solution.py:314
  128.8 8.6 %copy-start.12 = (f32[512]{0:T(512)S(1)}, f32[512]{0:T(512)}, u32[]{:S(2)}) copy-start(f32[512]{0:T(512)} %param.20) | copy-start | bytes 6148
  128.8 8.6 %copy-start.13 = (s32[512]{0:T(512)S(1)}, s32[512]{0:T(512)}, u32[]{:S(2)}) copy-start(s32[512]{0:T(512)} %param.21) | copy-start | bytes 6148
  128.8 9.0 %copy-start.14 = (f32[24]{0:T(128)S(1)}, f32[24]{0:T(128)}, u32[]{:S(2)}) copy-start(f32[24]{0:T(128)} %param.19) | copy-start | bytes 292
  130.4 45.8 %all-to-all-start.2 = ((bf16[640,4,128]{2,1,0:T(4,128)(2,1)}), bf16[640,4,128]{2,1,0:T(4,128)(2,1)S(1)}, u32[]{:S(2)}, u32[]{:S(2)}) async-start(bf16[640,4,128]{2,1,0:T(4,128)(2,1)} %bitcast.8), calls=%async_computation.2 | async-start | bytes 1310720 | tf_op jit(solution)/shard_map/all_to_all | solution.py:310
  138.3 1.1 copy-start.2
  (3 other events, 3.1 us)
